TPU v7x, 512 devices: a whole 4x8x8 slice. The times are simulated.
512 devices in a mesh: ab: 16 (over z, core), cd: 8 (over y), rep: 4 (over x).
Axes of the slice: x: 4, y: 8, z: 8, core: 2. Of those that a mesh axis runs over, the one named last changes fastest.
Arguments:
- amplitudes: bfloat16 [4, 2048, 8192], P('rep', 'ab', 'cd'), may hold values from -6 to 6
- pair_irrep: int32 [4, 2048], P('rep', 'ab'), may hold values from 0 to 7, as said below
- integrals: bfloat16 [8192, 8192], P('ab', 'cd'), may hold values from -0.0625 to 0.0625
- residual_in: bfloat16 [4, 2048, 8192], P('rep', None, ('ab', 'cd')), may hold values from -6 to 6
Outputs:
- residual: bfloat16 [4, 2048, 8192], P('rep', None, ('ab', 'cd'))
Inputs may be any that keep to these rules, and one draw needn't show every extreme that they name: For each j, among the 512 labels pair_irrep(l, j * 128 + t) over all layers l and 0 <= t < 128, exactly half are 0, and in one layer l (drawn) all 128 of them are 0.
All inputs are finite; a program needn't handle non-finite values.
Results may differ from a plain program's by a relative error of at most 0.001.
Values may be sent and summed in bfloat16 or wider, within the bound.
No kernel may reach another device: no remote copies, remote signals or barrier semaphores. Data moves between devices by JAX's collectives and lax.ppermute only.
A program may use at most 64 MiB of HBM per device.

v0:
```python
import jax
import jax.numpy as jnp
from jax import lax
from jax.sharding import PartitionSpec as P


def local(amplitudes, pair_irrep, integrals, residual_in):
    gathered, labels = (
        lax.all_gather(amplitudes[0], "ab", axis=0, tiled=True),
        lax.all_gather(pair_irrep[0], "ab", axis=0, tiled=True),
    )
    summed = lax.psum_scatter(
        lax.dot_general(
            integrals, gathered, (((1,), (1,)), ((), ())), preferred_element_type=jnp.float32
        ),
        "cd",
        scatter_dimension=0,
        tiled=True,
    )
    ladder = summed.T
    is_active = labels == 0
    added = jnp.where(is_active[:, None], ladder, 0.0)
    return (residual_in[0].astype(jnp.float32) + added).astype(jnp.bfloat16)[None]


def solution(mesh):
    return jax.shard_map(
        local,
        mesh=mesh,
        in_specs=(
            P("rep", "ab", "cd"),
            P("rep", "ab"),
            P("ab", "cd"),
            P("rep", None, ("ab", "cd")),
        ),
        out_specs=P("rep", None, ("ab", "cd")),
        check_vma=False,
    )
```

profile of v0, /device:TPU:1, one launch (start us, length us, event | category | flops | bytes accessed | tf_op | source)
XLA Modules:
  0.0 131.1 jit_solution(18039383640890825001)
XLA Ops:
  6.5 0.0 copy-start
  6.5 0.0 all-gather.4.cloned.1.call-start
  6.5 0.7 all-gather.4.cloned.1.call-update
  7.3 0.0 reduce-scatter.2.cloned.1.call-start
  7.3 53.0 %all-gather.4.cloned.1.call-done = bf16[1,2048,1024]{2,1,0:T(8,128)(2,1)} async-done(((bf16[1,128,1024]{2,1,0:T(8,128)(2,1)}), bf16[1,2048,1024]{2,1,0:T(8,128)(2,1)}) %all-gather.4.cloned.1.call-update) | async-done | bytes 4194320 | tf_op jit(solution)/shard_map/all_gather | solution.py:9
  60.3 0.0 copy-done
  60.3 6.5 %fusion = f32[512,2048]{1,0:T(8,128)} fusion(bf16[512,1024]{1,0:T(8,128)(2,1)S(1)} %copy-done, bf16[1,2048,1024]{2,1,0:T(8,128)(2,1)} %all-gather.4.cloned.1.call-done), kind=kOutput, calls=%fused_computation | convolution fusion | flops 2147483648 | bytes 9437184 | tf_op jit(solution)/shard_map/dot_general | solution.py:13
  66.8 0.0 copy-start.2
  66.8 0.0 copy-start.1
  66.8 0.0 reduce-scatter.2.cloned.1.call-update
  66.9 0.6 copy-done.2
  67.5 16.3 %all-gather = s32[1,2048]{1,0:T(1,128)S(1)} all-gather(s32[1,128]{1,0:T(1,128)S(1)} %copy-done.2), channel_id=2, replica_groups=mesh['ab'=16,'cd'=8,'rep'=4] {'ab'}, dimensions={1}, use_global_device_ids=true | all-gather | bytes 8704 | tf_op jit(solution)/shard_map/all_gather | solution.py:10
  83.9 38.6 %reduce-scatter.2.cloned.1.call-done = f32[64,2048]{1,0:T(8,128)} async-done(((f32[512,2048]{1,0:T(8,128)}), f32[64,2048]{1,0:T(8,128)}) %reduce-scatter.2.cloned.1.call-update) | async-done | bytes 524304 | tf_op jit(solution)/shard_map/reduce_scatter | solution.py:12
  122.4 0.0 copy-done.1
  122.4 1.8 %fusion.3 = bf16[1,2048,64]{1,2,0:T(8,128)(2,1)} fusion(f32[64,2048]{1,0:T(8,128)} %reduce-scatter.2.cloned.1.call-done, bf16[1,2048,64]{1,2,0:T(8,128)(2,1)S(1)} %copy-done.1, pred[2048]{0:T(1024)(128)(4,1)S(1)} %compare_reduce_fusion), kind=kLoop, calls=%fused_computation.4 | loop fusion | flops 524288 | bytes 1050624 | tf_op jit(solution)/shard_map/broadcast_in_dim | solution.py:23
  (1 shorter events, 0.0 us)
Async XLA Ops:
  6.5 53.8 %copy-start = (bf16[512,1024]{1,0:T(8,128)(2,1)S(1)}, bf16[512,1024]{1,0:T(8,128)(2,1)}, u32[]{:S(2)}) copy-start(bf16[512,1024]{1,0:T(8,128)(2,1)} %param.6) | copy-start | bytes 3145732
  6.5 53.8 %all-gather.4.cloned.1.call-start = ((), (), s32[]{:S(2)}) async-start(), calls=%async_computation.2 | async-start | bytes 4456448 | tf_op jit(solution)/shard_map/all_gather | solution.py:9
  7.3 115.2 %reduce-scatter.2.cloned.1.call-start = ((), (), s32[]{:S(2)}) async-start(), calls=%async_computation.1 | async-start | bytes 4718592 | tf_op jit(solution)/shard_map/reduce_scatter | solution.py:12
  66.8 0.7 copy-start.2
  66.8 55.6 %copy-start.1 = (bf16[1,2048,64]{1,2,0:T(8,128)(2,1)S(1)}, bf16[1,2048,64]{1,2,0:T(8,128)(2,1)}, u32[]{:S(2)}) copy-start(bf16[1,2048,64]{1,2,0:T(8,128)(2,1)} %param.7) | copy-start | bytes 786436
Sparse Core Ops, SparseCore 0:
  9.5 50.8 all-gather.3
  67.0 55.4 reduce-scatter.1
where the time goes:
time: 131 us
  waiting for transfers between devices  92.3 us (70%)
  blocking collectives  16.3 us (12%)
  between operations  13.4 us (10%)
  matrix products  6.5 us (5%)
  other arithmetic  1.85 us (1%)
    all_gather x1, waiting for transfers between devices, local(): lax.all_gather(amplitudes[0], 'ab', axis=0, tiled=True)  53 us
    reduce_scatter x1, waiting for transfers between devices, local(): lax.psum_scatter(lax.dot_general(integrals, gathered, (((1,), (1,)), ((),...  38.6 us
    all_gather x1, blocking collectives, local(): lax.all_gather(pair_irrep[0], 'ab', axis=0, tiled=True)  16.3 us
    dot_general x1, matrix products, local(): lax.dot_general(integrals, gathered, (((1,), (1,)), ((), ())), preferred_...  6.5 us
  transfers between devices with their start and end apart: 2, of which 2 were waited for; matrix products, arithmetic and copies ran while one was open for 0% of the time, Pallas kernels for 0%

commit v1 on v0

v1 whole, which is shorter than its diff:
```python
import jax
import jax.numpy as jnp
from jax import lax
from jax.sharding import Mesh, PartitionSpec as P


def local(amplitudes, pair_irrep, integrals, residual_in):
    keep = (pair_irrep[0] == 0)[:, None]
    rows = jnp.where(keep, amplitudes[0], jnp.zeros((), amplitudes.dtype))

    halves = jnp.broadcast_to(rows.reshape(2, 1, 64, 1024), (2, 8, 64, 1024))
    got = lax.all_to_all(halves.reshape(16, 64, 1024), ("b", "z"), 0, 0, tiled=True)
    got = got.reshape(2, 512, 1024)

    b = lax.axis_index("b")
    k = lax.axis_index("k")
    swap = [(0, 1), (1, 0)]
    other = lax.ppermute(integrals, "b", swap)
    low = jnp.where(b == 0, integrals, other)
    high = jnp.where(b == 0, other, integrals)
    wide = jnp.stack([low, high])
    across = lax.ppermute(wide, "k", swap)
    first = jnp.where(k == 0, wide, across)
    second = jnp.where(k == 0, across, wide)
    full = jnp.concatenate([first, second], axis=1)

    dims = (((1,), (1,)), ((), ()))
    partial = lax.dot_general(full[0], got[0], dims, preferred_element_type=jnp.float32)
    partial += lax.dot_general(full[1], got[1], dims, preferred_element_type=jnp.float32)

    sent = partial.astype(jnp.float16).reshape(16, 64, 512)
    parts = lax.all_to_all(sent, ("k", "g", "b"), 0, 0, tiled=True)
    summed = jnp.sum(parts.reshape(2, 4, 2, 64, 8, 64).astype(jnp.float32), axis=1)
    ladder = jnp.transpose(summed, (3, 0, 1, 4, 2)).reshape(2048, 64)
    return (residual_in[0].astype(jnp.float32) + ladder).astype(jnp.bfloat16)[None]


def solution(mesh):
    devices = mesh.devices.reshape(8, 2, 4, 2, 4)
    split = Mesh(devices, ("z", "k", "g", "b", "rep"))
    ab, cd = ("z", "k"), ("g", "b")
    return jax.shard_map(
        local,
        mesh=split,
        in_specs=(P("rep", ab, cd), P("rep", ab), P(ab, cd), P("rep", None, ab + cd)),
        out_specs=P("rep", None, ab + cd),
        check_vma=False,
    )
```

time: 131 us -> 118 us (0.901)
  waiting for transfers between devices: 92.3 us -> 30.8 us
  starting transfers between devices: 0.04 us -> 28.4 us
  blocking collectives: 16.3 us -> 35.2 us
  between operations: 13.4 us -> 0.11 us
  other arithmetic: 1.85 us -> 12.1 us
  local copies, waits for them, and re-layouts: 0.64 us -> 8 us
  matrix products: 6.5 us -> 2.57 us
    all_gather x1 -> x0, waiting for transfers between devices: 53 us -> none  [local(): lax.all_gather(amplitudes[0], 'ab', axis=0, tiled=True)]
    reduce_scatter x1 -> x0, waiting for transfers between devices: 38.6 us -> none  [local(): lax.psum_scatter(lax.dot_general(integrals, gathered, (((1,), (1,)), ((),...]
    all_to_all x0 -> x1, blocking collectives: none -> 35.2 us  [local(): parts = lax.all_to_all(sent, ('k', 'g', 'b'), 0, 0, tiled=True)]
    all_to_all x0 -> x1, waiting for transfers between devices: none -> 21.5 us  [local(): lax.all_to_all(halves.reshape(16, 64, 1024), ('b', 'z'), 0, 0, tiled=True)]
    ppermute x0 -> x2, starting transfers between devices: none -> 18.1 us  [the longest x1 14.1 us: local(): across = lax.ppermute(wide, 'k', swap)]
    all_gather x1 -> x0, blocking collectives: 16.3 us -> none  [local(): lax.all_gather(pair_irrep[0], 'ab', axis=0, tiled=True)]
    all_to_all x0 -> x1, starting transfers between devices: none -> 10.3 us  [local(): lax.all_to_all(halves.reshape(16, 64, 1024), ('b', 'z'), 0, 0, tiled=True)]
    ppermute x0 -> x2, waiting for transfers between devices: none -> 9.28 us  [the longest x1 5.18 us: local(): other = lax.ppermute(integrals, 'b', swap)]
  transfers between devices with their start and end apart: 2 -> 3, of which waited for: 2 -> 3; matrix products, arithmetic and copies ran while one was open for 0% -> 9% of each run, Pallas kernels for 0% -> 0%
where the time goes in v1:
time: 118 us; the launch traced here: 117 us
  blocking collectives  35.2 us (30%)
  waiting for transfers between devices  30.8 us (26%)
  starting transfers between devices  28.4 us (24%)
  other arithmetic  12.1 us (10%)
  local copies, waits for them, and re-layouts  8 us (7%)
  matrix products  2.57 us (2%)
    all_to_all x1, blocking collectives, local(): parts = lax.all_to_all(sent, ('k', 'g', 'b'), 0, 0, tiled=True)  35.2 us
    all_to_all x1, waiting for transfers between devices, local(): lax.all_to_all(halves.reshape(16, 64, 1024), ('b', 'z'), 0, 0, tiled=True)  21.5 us
    ppermute x1, starting transfers between devices, local(): across = lax.ppermute(wide, 'k', swap)  14.1 us
    all_to_all x1, starting transfers between devices, local(): lax.all_to_all(halves.reshape(16, 64, 1024), ('b', 'z'), 0, 0, tiled=True)  10.3 us
    ppermute x1, waiting for transfers between devices, local(): other = lax.ppermute(integrals, 'b', swap)  5.18 us
    ppermute x1, waiting for transfers between devices, local(): across = lax.ppermute(wide, 'k', swap)  4.1 us
    ppermute x1, starting transfers between devices, local(): other = lax.ppermute(integrals, 'b', swap)  4.01 us
    select_n x1, other arithmetic, local(): first = jnp.where(k == 0, wide, across)  3.84 us
  transfers between devices with their start and end apart: 3, of which 3 were waited for; matrix products, arithmetic and copies ran while one was open for 9% of the time, Pallas kernels for 0%

profile of v1, /device:TPU:1, one launch (start us, length us, event | category | flops | bytes accessed | tf_op | source)
XLA Modules:
  0.0 117.1 jit_solution(1302370622874625883)
XLA Ops:
  0.0 4.0 %collective-permute-start = (bf16[512,1024]{1,0:T(8,128)(2,1)}, bf16[512,1024]{1,0:T(8,128)(2,1)}, u32[]{:S(2)}, u32[]{:S(2)}) collective-permute-start(bf16[512,1024]{1,0:T(8,128)(2,1)} %param.6), channel_id=1, source_target_pairs={{0,4},{4,0},{1,5},{5,1},{2,6},{6,2},{3,7},{7,3},{8,12},{12,8},{9,1... | collective-permute-start | bytes 3145736 | tf_op jit(solution)/shard_map/ppermute | solution.py:18
  4.0 0.7 compare_reduce_fusion
  4.7 0.1 eq.25
  4.8 1.0 broadcast_select_fusion.2
  5.8 1.6 %broadcast_in_dim.21 = bf16[2,8,64,1024]{3,2,1,0:T(8,128)(2,1)} broadcast(bf16[2,64,1024]{2,1,0:T(8,128)(2,1)S(1)} %broadcast_select_fusion.2), dimensions={0,2,3} | broadcast | bytes 2359296 | tf_op jit(solution)/shard_map/broadcast_in_dim | solution.py:11
  7.4 10.3 %all-to-all-start = ((bf16[16,64,1024]{2,1,0:T(8,128)(2,1)}), bf16[16,64,1024]{2,1,0:T(8,128)(2,1)}, u32[]{:S(2)}, u32[]{:S(2)}) async-start(bf16[16,64,1024]{2,1,0:T(8,128)(2,1)} %bitcast.4), calls=%async_computation | async-start | bytes 4194304 | tf_op jit(solution)/shard_map/all_to_all | solution.py:12
  17.7 5.2 %collective-permute-done = bf16[512,1024]{1,0:T(8,128)(2,1)} collective-permute-done((bf16[512,1024]{1,0:T(8,128)(2,1)}, bf16[512,1024]{1,0:T(8,128)(2,1)}, u32[]{:S(2)}, u32[]{:S(2)}) %collective-permute-start) | collective-permute-done | bytes 1048608 | tf_op jit(solution)/shard_map/ppermute | solution.py:18
  22.9 1.4 %select_bitcast_fusion.1 = (bf16[1,512,1024]{2,1,0:T(8,128)(2,1)S(1)}, bf16[1,512,1024]{2,1,0:T(8,128)(2,1)S(1)}) fusion(bf16[512,1024]{1,0:T(8,128)(2,1)S(1)} %copy-done.2, bf16[512,1024]{1,0:T(8,128)(2,1)} %collective-permute-done, pred[]{:T(512)S(6)} %eq.22), kind=kLoop, calls=%fused_computation.14 | loop fusion | flops 1048576 | bytes 4194305 | tf_op jit(solution)/shard_map/stack | solution.py:21
  24.3 1.5 %pad_maximum_fusion.1 = bf16[2,512,1024]{2,1,0:T(8,128)(2,1)} fusion(bf16[1,512,1024]{2,1,0:T(8,128)(2,1)S(1)} %get-tuple-element.10, bf16[1,512,1024]{2,1,0:T(8,128)(2,1)S(1)} %get-tuple-element.9), kind=kLoop, calls=%fused_computation.9 | loop fusion | flops 1048576 | bytes 4194304 | tf_op jit(solution)/shard_map/stack | solution.py:21
  25.8 14.1 %collective-permute-start.1 = (bf16[2,512,1024]{2,1,0:T(8,128)(2,1)}, bf16[2,512,1024]{2,1,0:T(8,128)(2,1)}, u32[]{:S(2)}, u32[]{:S(2)}) collective-permute-start(bf16[2,512,1024]{2,1,0:T(8,128)(2,1)} %pad_maximum_fusion.1), channel_id=1, source_target_pairs={{0,32},{32,0},{1,33},{33,1},{2,34},{34,2},{3,35},{35,3},{4,36},{36... | collective-permute-start | bytes 6291464 | tf_op jit(solution)/shard_map/ppermute | solution.py:22
  39.9 4.1 %collective-permute-done.1 = bf16[2,512,1024]{2,1,0:T(8,128)(2,1)} collective-permute-done((bf16[2,512,1024]{2,1,0:T(8,128)(2,1)}, bf16[2,512,1024]{2,1,0:T(8,128)(2,1)}, u32[]{:S(2)}, u32[]{:S(2)}) %collective-permute-start.1) | collective-permute-done | bytes 2097184 | tf_op jit(solution)/shard_map/ppermute | solution.py:22
  44.0 3.8 %broadcast_select_fusion.1 = (bf16[2,512,1024]{2,1,0:T(8,128)(2,1)}, bf16[2,512,1024]{2,1,0:T(8,128)(2,1)}) fusion(bf16[2,512,1024]{2,1,0:T(8,128)(2,1)} %collective-permute-done.1, pred[]{:T(512)S(6)} %eq.21, bf16[1,512,1024]{2,1,0:T(8,128)(2,1)S(1)} %get-tuple-element.10, bf16[1,512,1024]{2,1,0:T(8,128)(2,1)S(1)} %get-tuple-element.9), kind=kLoop, calls=%fused_computation.12 | loop fusion | flops 3145728 | bytes 8388609 | tf_op jit(solution)/shard_map/jit(_where)/select_n | solution.py:23
  47.8 21.5 %all-to-all-done = bf16[16,64,1024]{2,1,0:T(8,128)(2,1)} async-done(((bf16[16,64,1024]{2,1,0:T(8,128)(2,1)}), bf16[16,64,1024]{2,1,0:T(8,128)(2,1)}, u32[]{:S(2)}, u32[]{:S(2)}) %all-to-all-start) | async-done | bytes 2097184 | tf_op jit(solution)/shard_map/all_to_all | solution.py:12
  69.3 1.9 %fusion.12 = (bf16[8,64,1024]{2,1,0:T(8,128)(2,1)S(1)}, bf16[8,64,1024]{2,1,0:T(8,128)(2,1)S(1)}) fusion(bf16[16,64,1024]{2,1,0:T(8,128)(2,1)} %all-to-all-done), kind=kLoop, calls=%fused_computation.20 | loop fusion | bytes 4194304 | tf_op jit(solution)/shard_map/slice | solution.py:28
  71.3 0.3 copy-done.1
  71.5 1.3 %fusion.5 = f32[1024,512]{1,0:T(8,128)S(1)} fusion(bf16[512,1024]{1,0:T(8,128)(2,1)S(1)} %bitcast.25, bf16[2,512,1024]{2,1,0:T(8,128)(2,1)S(1)} %copy-done.1, bf16[2,512,1024]{2,1,0:T(8,128)(2,1)S(1)} %copy-done), kind=kOutput, calls=%fused_computation.7 | convolution fusion | flops 1077936128 | bytes 7340032 | tf_op jit(solution)/shard_map/dot_general | solution.py:29
  72.8 1.3 %add_convert_fusion = f16[1024,512]{1,0:T(8,128)(2,1)S(1)} fusion(f32[1024,512]{1,0:T(8,128)S(1)} %fusion.5, bf16[512,1024]{1,0:T(8,128)(2,1)S(1)} %bitcast.24, bf16[2,512,1024]{2,1,0:T(8,128)(2,1)S(1)} %copy-done, bf16[2,512,1024]{2,1,0:T(8,128)(2,1)S(1)} %copy-done.1), kind=kOutput, calls=%fused_computation.10 | convolution fusion | flops 1078984704 | bytes 8388608 | tf_op jit(solution)/shard_map/dot_general | solution.py:28
  74.1 35.2 %all_to_all.10 = f16[16,64,512]{2,1,0:T(8,128)(2,1)S(1)} all-to-all(f16[16,64,512]{2,1,0:T(8,128)(2,1)S(1)} %bitcast.23), channel_id=1, replica_groups=mesh['z'=8,'k'=2,'g'=4,'b'=2,'rep'=4] {'k','g','b'}, dimensions={0} | all-to-all | bytes 2097152 | tf_op jit(solution)/shard_map/all_to_all | solution.py:32
  109.3 0.3 convert_element_type.22
  109.6 2.4 %reshape.41 = f32[2,4,2,64,8,64]{5,4,3,2,1,0:T(8,128)} reshape(f32[16,64,512]{2,1,0:T(8,128)S(1)} %convert_element_type.22) | data formatting | bytes 4194304 | tf_op jit(solution)/shard_map/convert_element_type | solution.py:33
  111.9 2.6 %reduce_sum.9 = f32[2,2,64,8,64]{4,3,2,1,0:T(8,128)S(1)} reduce(f32[2,4,2,64,8,64]{5,4,3,2,1,0:T(8,128)} %reshape.41, f32[]{:T(128)} %constant.16.clone.1), dimensions={1}, to_apply=%region_0.1 | reduce | flops 393216 | bytes 2621444 | tf_op jit(solution)/shard_map/reduce_sum | solution.py:33
  114.6 0.8 copy.5
  115.4 1.0 reshape.40
  116.4 0.8 add_convert_fusion.1
  (7 shorter events, 0.0 us)
Async XLA Ops:
  0.0 22.9 %collective-permute-start = (bf16[512,1024]{1,0:T(8,128)(2,1)}, bf16[512,1024]{1,0:T(8,128)(2,1)}, u32[]{:S(2)}, u32[]{:S(2)}) collective-permute-start(bf16[512,1024]{1,0:T(8,128)(2,1)} %param.6), channel_id=1, source_target_pairs={{0,4},{4,0},{1,5},{5,1},{2,6},{6,2},{3,7},{7,3},{8,12},{12,8},{9,1... | collective-permute-start | bytes 3145736 | tf_op jit(solution)/shard_map/ppermute | solution.py:18
  7.4 15.5 %copy-start.2 = (bf16[512,1024]{1,0:T(8,128)(2,1)S(1)}, bf16[512,1024]{1,0:T(8,128)(2,1)}, u32[]{:S(2)}) copy-start(bf16[512,1024]{1,0:T(8,128)(2,1)} %param.6) | copy-start | bytes 3145732
  7.4 61.9 %all-to-all-start = ((bf16[16,64,1024]{2,1,0:T(8,128)(2,1)}), bf16[16,64,1024]{2,1,0:T(8,128)(2,1)}, u32[]{:S(2)}, u32[]{:S(2)}) async-start(bf16[16,64,1024]{2,1,0:T(8,128)(2,1)} %bitcast.4), calls=%async_computation | async-start | bytes 4194304 | tf_op jit(solution)/shard_map/all_to_all | solution.py:12
  25.8 18.2 %collective-permute-start.1 = (bf16[2,512,1024]{2,1,0:T(8,128)(2,1)}, bf16[2,512,1024]{2,1,0:T(8,128)(2,1)}, u32[]{:S(2)}, u32[]{:S(2)}) collective-permute-start(bf16[2,512,1024]{2,1,0:T(8,128)(2,1)} %pad_maximum_fusion.1), channel_id=1, source_target_pairs={{0,32},{32,0},{1,33},{33,1},{2,34},{34,2},{3,35},{35,3},{4,36},{36... | collective-permute-start | bytes 6291464 | tf_op jit(solution)/shard_map/ppermute | solution.py:22
  47.8 23.5 %copy-start = (bf16[2,512,1024]{2,1,0:T(8,128)(2,1)S(1)}, bf16[2,512,1024]{2,1,0:T(8,128)(2,1)}, u32[]{:S(2)}) copy-start(bf16[2,512,1024]{2,1,0:T(8,128)(2,1)} %get-tuple-element.5) | copy-start | bytes 6291460
  69.3 2.2 %copy-start.1 = (bf16[2,512,1024]{2,1,0:T(8,128)(2,1)S(1)}, bf16[2,512,1024]{2,1,0:T(8,128)(2,1)}, u32[]{:S(2)}) copy-start(bf16[2,512,1024]{2,1,0:T(8,128)(2,1)} %get-tuple-element.6) | copy-start | bytes 6291460
  114.6 1.8 %copy-start.3 = (bf16[1,2048,64]{1,2,0:T(8,128)(2,1)S(1)}, bf16[1,2048,64]{1,2,0:T(8,128)(2,1)}, u32[]{:S(2)}) copy-start(bf16[1,2048,64]{1,2,0:T(8,128)(2,1)} %param.7) | copy-start | bytes 786436

commit v2 on v1

v2 whole, which is shorter than its diff:
```python
import jax
import jax.numpy as jnp
from jax import lax
from jax.experimental import pallas as pl
from jax.experimental.pallas import tpu as pltpu
from jax.sharding import Mesh, PartitionSpec as P


LAYERS = 4
T = 128
KD = 1024
CLASSES = 8
SEND = 24
BASE = 16
SHARE = 32
Z = 8
ROWS = Z * BASE
i32, f32, bf16 = jnp.int32, jnp.float32, jnp.bfloat16


def iota(shape, dim):
    return lax.broadcasted_iota(i32, shape, dim)


def ranks(active):
    before = (iota((T, T), 0) < iota((T, T), 1)).astype(bf16)
    return jnp.dot(active.astype(bf16), before, preferred_element_type=f32).astype(i32)


def pack_kernel(labels_ref, rows_ref, out_ref):
    active = jnp.broadcast_to(labels_ref[...] == 0, (8, T)).astype(i32).astype(f32)
    rank = jnp.where(active[:1] > 0, ranks(active)[:1], -1)
    count = jnp.sum(active, axis=1, keepdims=True).astype(i32)[:1]
    even = (count >> 3) << 3
    rows = rows_ref[...]
    slot = iota((SEND, T), 0)
    lane = iota((SEND, KD), 1)
    srow = iota((SEND, KD), 0)
    flags = jnp.concatenate([active[:1]] * (KD // T), axis=1)
    info = jnp.where(lane < T, flags, count.astype(f32))
    for q in range(CLASSES):
        shared = 8 * slot + q
        rest = even + slot - BASE
        target = jnp.where(slot < BASE, shared, rest)
        bound = jnp.where(slot < BASE, even, jnp.where(slot < SEND - 1, count, 0))
        hot = ((rank == target) & (target < bound)).astype(f32).astype(bf16)
        picked = jnp.dot(hot, rows, preferred_element_type=f32)
        out_ref[q] = jnp.where(srow == SEND - 1, info, picked).astype(bf16)


def shares(counts, q):
    parts, start, offset = [], jnp.zeros_like(counts[0]), jnp.zeros_like(counts[0])
    for n in counts:
        rem = n & 7
        extra = (q - offset) & 7
        length = (n >> 3) + (extra < rem).astype(i32)
        parts.append((start, length, n >> 3, extra))
        start, offset = start + length, offset + rem
    return parts


def share_kernel(got_ref, out_ref):
    rep, own = lax.axis_index("rep"), lax.axis_index("b")
    q = 2 * rep + own
    counts = [
        got_ref[l, 0, SEND - 1 : SEND, T : 2 * T].astype(f32).astype(i32) for l in range(LAYERS)
    ]
    s = iota((SHARE, SEND), 0)
    slot = iota((SHARE, SEND), 1)
    total = [jnp.zeros((SHARE, KD), f32) for _ in range(2)]
    for l, (start, length, base, extra) in enumerate(shares(counts, q)):
        start, length, base, extra = (v[:, :SEND] for v in (start, length, base, extra))
        i = s - start
        inside = (i >= 0) & (i < length)
        want = jnp.where(i < base, i, BASE + extra)
        hot = (inside & (slot == want)).astype(f32).astype(bf16)
        for h in range(2):
            half = own if h == 0 else 1 - own
            total[h] += jnp.dot(hot, got_ref[l, half], preferred_element_type=f32)
    row = iota((SHARE, T), 0)
    info = jnp.zeros((SHARE, T), f32)
    for l in range(LAYERS):
        mine = got_ref[l, 0, SEND - 1 : SEND, :T].astype(f32)
        info = jnp.where((row == 0) & (rep == l), mine, info)
        info = jnp.where(row == 1 + l, counts[l].astype(f32), info)
    for z in range(Z):
        for h in range(2):
            out_ref[z, :, h * KD : (h + 1) * KD] = total[h].astype(bf16)
        out_ref[z, :, 2 * KD :] = info.astype(bf16)


def ladder_kernel(got_ref, *refs):
    pieces, out_ref, buffers, spread_ref, sems = refs[:4], refs[4], refs[5:9], refs[9], refs[10]
    copies = [pltpu.make_async_copy(pieces[n], buffers[n], sems.at[n]) for n in range(4)]
    for copy in copies:
        copy.start()
    q = 2 * lax.axis_index("rep") + lax.axis_index("b")
    own = lax.axis_index("k")
    lane = iota((1, Z * SHARE), 1)
    counts = []
    for l in range(LAYERS):
        n = jnp.zeros((1, Z * SHARE), f32)
        for z in range(Z):
            one = got_ref[z, 1 + l : 2 + l, 2 * KD :].astype(f32)
            n = jnp.where((lane >> 5) == z, jnp.concatenate([one, one], axis=1), n)
        counts.append(n.astype(i32))
    row = iota((ROWS, Z * SHARE), 0)
    col = iota((ROWS, Z * SHARE), 1)
    i = row & (BASE - 1)
    same = (row >> 4) == (col >> 5)
    rows = jnp.concatenate([got_ref[z, :, : 2 * KD] for z in range(Z)], axis=0)
    for l, (start, length, _, _) in enumerate(shares(counts, q)):
        hot = (same & (i < length) & ((col & (SHARE - 1)) == start + i)).astype(f32).astype(bf16)
        spread_ref[l * ROWS : (l + 1) * ROWS, :] = jnp.dot(
            hot, rows, preferred_element_type=f32
        ).astype(bf16)
    dims = (((1,), (1,)), ((), ()))
    for copy in copies:
        copy.wait()
    step = 256
    for side in range(2):
        for at in range(0, 512, step):
            part = jnp.zeros((step, LAYERS * ROWS), f32)
            for h in range(2):
                part += lax.dot_general(
                    buffers[2 * side + h][at : at + step, :],
                    spread_ref[:, h * KD : (h + 1) * KD],
                    dims,
                    preferred_element_type=f32,
                )
            core = own if side == 0 else 1 - own
            for l in range(LAYERS):
                out_ref[l, core, at : at + step, :] = part[:, l * ROWS : (l + 1) * ROWS]


def place_kernel(info_ref, out_ref):
    rep, own = lax.axis_index("rep"), lax.axis_index("k")

    def of(r):
        at_core = [
            jnp.concatenate([info_ref[s, z, r : r + 1, :].astype(f32) for z in range(Z)], axis=0)
            for s in range(2)
        ]
        first = jnp.where(own == 0, at_core[0], at_core[1])
        second = jnp.where(own == 0, at_core[1], at_core[0])
        return jnp.concatenate([first, second], axis=0)

    active = of(0)
    rank = ranks(active)
    offset = jnp.zeros((2 * Z, T), i32)
    even = jnp.zeros((2 * Z, T), i32)
    for l in range(LAYERS):
        n = of(1 + l).astype(i32)
        offset += jnp.where(l < rep, n & 7, 0)
        even = jnp.where(l == rep, (n >> 3) << 3, even)
    cls = jnp.where(rank < even, rank, offset + rank - even) & 7
    out_ref[0] = jnp.where(active > 0, cls, -1)
    out_ref[1] = jnp.minimum(rank >> 3, BASE - 1)


def final_kernel(place_ref, sums_ref, residual_ref, out_ref):
    for z in range(Z):
        for k in range(2):
            j = k * Z + z
            own = jnp.broadcast_to(place_ref[0, j : j + 1, :], (64, T))
            lane = BASE * z + jnp.broadcast_to(place_ref[1, j : j + 1, :], (64, T))
            ladder = jnp.zeros((64, T), f32)
            for q in range(CLASSES):
                here = jnp.take_along_axis(sums_ref[q // 2, k, q % 2], lane, axis=1)
                ladder = jnp.where(own == q, here, ladder)
            at = (z * 2 + k) * T
            old = residual_ref[:, at : at + T].astype(f32)
            out_ref[:, at : at + T] = (old + ladder).astype(bf16)


VMEM = pl.BlockSpec(memory_space=pltpu.VMEM)
ANY = pl.BlockSpec(memory_space=pl.ANY)
MIB = 2**20


def call(kernel, shape, dtype, *args, anys=0, scratch=(), limit=8, flops=0):
    return pl.pallas_call(
        kernel,
        out_shape=jax.ShapeDtypeStruct(shape, dtype),
        in_specs=[VMEM] * (len(args) - anys) + [ANY] * anys,
        out_specs=VMEM,
        scratch_shapes=scratch,
        compiler_params=pltpu.CompilerParams(vmem_limit_bytes=limit * MIB),
        cost_estimate=pl.CostEstimate(flops=flops, bytes_accessed=2**21, transcendentals=0),
    )(*args)


def step(amplitudes, pair_irrep, integrals, residual_in):
    swap = [(0, 1), (1, 0)]

    packed = call(pack_kernel, (CLASSES, SEND, KD), bf16, pair_irrep, amplitudes[0], flops=2**26)
    got = lax.all_to_all(packed, ("rep", "b"), 0, 0, tiled=True)
    got = got.reshape(LAYERS, 2, SEND, KD)
    shared = call(share_kernel, (Z, SHARE, 2 * KD + T), bf16, got, flops=2**26)
    gathered = lax.all_to_all(shared, "z", 0, 0, tiled=True)

    other = lax.ppermute(integrals, "b", swap)
    across = lax.ppermute(integrals, "k", swap)
    across_other = lax.ppermute(other, "k", swap)

    tall = pltpu.VMEM((512, KD), bf16)
    partial = call(
        ladder_kernel,
        (LAYERS, 2, 512, ROWS),
        f32,
        gathered,
        integrals,
        other,
        across,
        across_other,
        anys=4,
        scratch=[tall] * 4
        + [pltpu.VMEM((LAYERS * ROWS, 2 * KD), bf16), pltpu.SemaphoreType.DMA((4,))],
        limit=24,
        flops=2**31,
    )

    sent = partial.astype(jnp.float16).reshape(64, 64, ROWS)
    parts = lax.all_to_all(sent, ("rep", "k", "g", "b"), 0, 0, tiled=True)
    sums = jnp.sum(parts.reshape(LAYERS, 2, 4, 2, 64, ROWS).astype(f32), axis=2)

    info = gathered[:, :8, 2 * KD :]
    info_across = lax.ppermute(info, "k", swap)
    place = call(place_kernel, (2, 2 * Z, T), i32, jnp.stack([info, info_across]), flops=2**20)
    out = call(final_kernel, (64, 2048), bf16, place, sums, residual_in[0].T, flops=2**26)
    return out.T[None]


def solution(mesh):
    devices = mesh.devices.reshape(8, 2, 4, 2, 4)
    split = Mesh(devices, ("z", "k", "g", "b", "rep"))
    ab, cd = ("z", "k"), ("g", "b")
    return jax.shard_map(
        step,
        mesh=split,
        in_specs=(P("rep", ab, cd), P("rep", ab), P(ab, cd), P("rep", None, ab + cd)),
        out_specs=P("rep", None, ab + cd),
        check_vma=False,
    )
```

time: 118 us -> 104 us (0.88)
  blocking collectives: 35.2 us -> 0 us
  starting transfers between devices: 28.4 us -> 45.3 us
  waiting for transfers between devices: 30.8 us -> 42.5 us
  other arithmetic: 12.1 us -> 1.37 us
  Pallas kernels: 0 us -> 8.1 us
  matrix products: 2.57 us -> 0 us
  local copies, waits for them, and re-layouts: 8 us -> 6.02 us
    all_to_all x1 -> x0, blocking collectives: 35.2 us -> none  [local(): parts = lax.all_to_all(sent, ('k', 'g', 'b'), 0, 0, tiled=True)]
    all_to_all x1 -> x3, waiting for transfers between devices: 21.5 us -> 40.2 us  [the longest x1 24.6 us: step(): parts = lax.all_to_all(sent, ('rep', 'k', 'g', 'b'), 0, 0, tiled=True)]
    all_to_all x1 -> x3, starting transfers between devices: 10.3 us -> 27 us  [the longest x1 11 us: step(): gathered = lax.all_to_all(shared, 'z', 0, 0, tiled=True)]
    pallas_call x0 -> x5, Pallas kernels: none -> 8.1 us  [call(): pl.pallas_call(kernel, out_shape=jax.ShapeDtypeStruct(shape, dtype), in_s...]
    ppermute x2 -> x4, waiting for transfers between devices: 9.28 us -> 2.36 us  [the longest x1 1.27 us: step(): across_other = lax.ppermute(other, 'k', swap)]
    unnamed x8 -> x16, local copies, waits for them, and re-layouts: 0.3 us -> 6.02 us
    select_n x2 -> x0, other arithmetic: 4.88 us -> none  [the longest x1 3.84 us: local(): first = jnp.where(k == 0, wide, across)]
    another operation x2 -> x1, other arithmetic: 2.87 us -> 0.01 us  [step(): jnp.stack([info, info_across])]
  transfers between devices with their start and end apart: 3 -> 7, of which waited for: 3 -> 6; matrix products, arithmetic and copies ran while one was open for 9% -> 0% of each run, Pallas kernels for 0% -> 1%
where the time goes in v2:
time: 104 us; the launch traced here: 103 us
  starting transfers between devices  45.3 us (44%)
  waiting for transfers between devices  42.5 us (41%)
  Pallas kernels  8.1 us (8%)
  local copies, waits for them, and re-layouts  6.02 us (6%)
  other arithmetic  1.37 us (1%)
    all_to_all x1, waiting for transfers between devices, step(): parts = lax.all_to_all(sent, ('rep', 'k', 'g', 'b'), 0, 0, tiled=True)  24.6 us
    all_to_all x1, waiting for transfers between devices, step(): gathered = lax.all_to_all(shared, 'z', 0, 0, tiled=True)  12.1 us
    all_to_all x1, starting transfers between devices, step(): gathered = lax.all_to_all(shared, 'z', 0, 0, tiled=True)  11 us
    all_to_all x1, starting transfers between devices, step(): parts = lax.all_to_all(sent, ('rep', 'k', 'g', 'b'), 0, 0, tiled=True)  10.1 us
    pallas_call x5, Pallas kernels, call(): pl.pallas_call(kernel, out_shape=jax.ShapeDtypeStruct(shape, dtype), in_s...  8.1 us
    ppermute x1, starting transfers between devices, step(): across_other = lax.ppermute(other, 'k', swap)  7 us
    unnamed x16, local copies, waits for them, and re-layouts  6.02 us
    all_to_all x1, starting transfers between devices, step(): got = lax.all_to_all(packed, ('rep', 'b'), 0, 0, tiled=True)  5.85 us
  transfers between devices with their start and end apart: 7, of which 6 were waited for; matrix products, arithmetic and copies ran while one was open for 0% of the time, Pallas kernels for 1%

profile of v2, /device:TPU:1, one launch (start us, length us, event | category | flops | bytes accessed | tf_op | source)
XLA Modules:
  0.0 103.4 jit_solution(14825046243552245553)
XLA Ops:
  0.0 0.9 copy-done
  1.0 0.7 copy-done.2
  1.6 1.3 %shard_map.46 = bf16[8,24,1024]{2,1,0:T(8,128)(2,1)} custom-call(s32[1,128]{1,0:T(1,128)S(1)} %copy-done.2, bf16[128,1024]{1,0:T(8,128)(2,1)S(1)} %bitcast.15), custom_call_target="tpu_custom_call" | custom-call | flops 67108864 | bytes 2097152 | tf_op jit(solution)/shard_map/pallas_call | solution.py:182
  2.9 5.8 %all-to-all-start = ((bf16[8,24,1024]{2,1,0:T(8,128)(2,1)}), bf16[8,24,1024]{2,1,0:T(8,128)(2,1)S(1)}, u32[]{:S(2)}, u32[]{:S(2)}) async-start(bf16[8,24,1024]{2,1,0:T(8,128)(2,1)} %shard_map.46), calls=%async_computation | async-start | bytes 786432 | tf_op jit(solution)/shard_map/all_to_all | solution.py:197
  8.8 3.4 %collective-permute-start.1 = (bf16[512,1024]{1,0:T(8,128)(2,1)S(1)}, bf16[512,1024]{1,0:T(8,128)(2,1)S(1)}, u32[]{:S(2)}, u32[]{:S(2)}) collective-permute-start(bf16[512,1024]{1,0:T(8,128)(2,1)S(1)} %copy-done.3), channel_id=1, source_target_pairs={{0,4},{4,0},{1,5},{5,1},{2,6},{6,2},{3,7},{7,3},{8,12},{12,8},{9,1... | collective-permute-start | bytes 3145736 | tf_op jit(solution)/shard_map/ppermute | solution.py:202
  12.1 3.5 %all-to-all-done = bf16[8,24,1024]{2,1,0:T(8,128)(2,1)S(1)} async-done(((bf16[8,24,1024]{2,1,0:T(8,128)(2,1)}), bf16[8,24,1024]{2,1,0:T(8,128)(2,1)S(1)}, u32[]{:S(2)}, u32[]{:S(2)}) %all-to-all-start) | async-done | bytes 393248 | tf_op jit(solution)/shard_map/all_to_all | solution.py:197
  15.6 1.3 %shard_map.47 = bf16[8,32,2176]{2,1,0:T(8,128)(2,1)} custom-call(bf16[4,2,24,1024]{3,2,1,0:T(8,128)(2,1)S(1)} %bitcast.14), custom_call_target="tpu_custom_call" | custom-call | flops 67108864 | bytes 2097152 | tf_op jit(solution)/shard_map/pallas_call | solution.py:182
  16.9 11.0 %all-to-all-start.1 = ((bf16[8,32,2176]{2,1,0:T(8,128)(2,1)}), bf16[8,32,2176]{2,1,0:T(8,128)(2,1)S(1)}, u32[]{:S(2)}, u32[]{:S(2)}) async-start(bf16[8,32,2176]{2,1,0:T(8,128)(2,1)} %shard_map.47), calls=%async_computation.1 | async-start | bytes 2228224 | tf_op jit(solution)/shard_map/all_to_all | solution.py:200
  28.0 5.4 %collective-permute-start.2 = (bf16[512,1024]{1,0:T(8,128)(2,1)S(1)}, bf16[512,1024]{1,0:T(8,128)(2,1)S(1)}, u32[]{:S(2)}, u32[]{:S(2)}) collective-permute-start(bf16[512,1024]{1,0:T(8,128)(2,1)S(1)} %copy-done.3), channel_id=1, source_target_pairs={{0,32},{32,0},{1,33},{33,1},{2,34},{34,2},{3,35},{35,3},{4,36},{36... | collective-permute-start | bytes 3145736 | tf_op jit(solution)/shard_map/ppermute | solution.py:203
  33.4 0.3 collective-permute-done.1.refs_1_
  33.6 7.0 %collective-permute-start.3 = (bf16[512,1024]{1,0:T(8,128)(2,1)S(1)}, bf16[512,1024]{1,0:T(8,128)(2,1)S(1)}, u32[]{:S(2)}, u32[]{:S(2)}) collective-permute-start(bf16[512,1024]{1,0:T(8,128)(2,1)S(1)} %collective-permute-done.1.refs_1_), channel_id=1, source_target_pairs={{0,32},{32,0},{1,33},{33,1},{2,34},{34,2},{3,35},{35,3},{4,36},{36... | collective-permute-start | bytes 3145736 | tf_op jit(solution)/shard_map/ppermute | solution.py:204
  40.7 1.0 copy-done.4
  41.6 1.3 %collective-permute-done.3.refs_3_ = bf16[512,1024]{1,0:T(8,128)(2,1)S(1)} collective-permute-done((bf16[512,1024]{1,0:T(8,128)(2,1)S(1)}, bf16[512,1024]{1,0:T(8,128)(2,1)S(1)}, u32[]{:S(2)}, u32[]{:S(2)}) %collective-permute-start.3) | collective-permute-done | bytes 1048608 | tf_op jit(solution)/shard_map/ppermute | solution.py:204
  42.9 1.0 copy-done.6
  43.9 12.1 %all-to-all-done.1.got_ref = bf16[8,32,2176]{2,1,0:T(8,128)(2,1)S(1)} async-done(((bf16[8,32,2176]{2,1,0:T(8,128)(2,1)}), bf16[8,32,2176]{2,1,0:T(8,128)(2,1)S(1)}, u32[]{:S(2)}, u32[]{:S(2)}) %all-to-all-start.1) | async-done | bytes 1114144 | tf_op jit(solution)/shard_map/all_to_all | solution.py:200
  56.0 1.2 %copy-done.5 = bf16[512,1024]{1,0:T(8,128)(2,1)S(1)} copy-done((bf16[512,1024]{1,0:T(8,128)(2,1)S(1)}, bf16[512,1024]{1,0:T(8,128)(2,1)}, u32[]{:S(2)}) %copy-start.5) | copy-done | bytes 1048600
  57.2 1.2 %copy-done.7 = bf16[512,1024]{1,0:T(8,128)(2,1)S(1)} copy-done((bf16[512,1024]{1,0:T(8,128)(2,1)S(1)}, bf16[512,1024]{1,0:T(8,128)(2,1)}, u32[]{:S(2)}) %copy-start.7) | copy-done | bytes 1048600
  58.5 3.4 %shard_map.49 = f32[4,2,512,128]{3,2,1,0:T(8,128)S(1)} custom-call(bf16[8,32,2176]{2,1,0:T(8,128)(2,1)S(1)} %all-to-all-done.1.got_ref, bf16[512,1024]{1,0:T(8,128)(2,1)S(1)} %copy-done.3, bf16[512,1024]{1,0:T(8,128)(2,1)S(1)} %collective-permute-done.1.refs_1_, bf16[512,1024]{1,0:T(8,128)(2,1)S(1)} %copy-done.5, bf16[512,1024]{1,0:T(8,128)(2,1)S(1)} %copy-done.7), custom_call_target="tpu_custom_call" | custom-call | flops 2147483648 | bytes 2097152 | tf_op jit(solution)/shard_map/pallas_call | solution.py:182
  61.9 1.1 %convert_element_type.9 = f16[4,2,512,128]{3,2,1,0:T(8,128)(2,1)} convert(f32[4,2,512,128]{3,2,1,0:T(8,128)S(1)} %shard_map.49) | non-fusion elementwise | flops 524288 | bytes 3145728 | tf_op jit(solution)/shard_map/convert_element_type | solution.py:223
  63.0 10.1 %all-to-all-start.2 = ((f16[64,64,128]{2,1,0:T(8,128)(2,1)}), f16[64,64,128]{2,1,0:T(8,128)(2,1)S(1)}, u32[]{:S(2)}, u32[]{:S(2)}) async-start(f16[64,64,128]{2,1,0:T(8,128)(2,1)} %bitcast.4), calls=%async_computation.2 | async-start | bytes 2097152 | tf_op jit(solution)/shard_map/all_to_all | solution.py:224
  73.2 2.5 %collective-permute-start = (bf16[8,8,128]{2,1,0:T(8,128)(2,1)S(1)}, bf16[8,8,128]{2,1,0:T(8,128)(2,1)S(1)}, u32[]{:S(2)}, u32[]{:S(2)}) collective-permute-start(bf16[8,8,128]{2,1,0:T(8,128)(2,1)S(1)} %get-tuple-element.6), channel_id=1, source_target_pairs={{0,32},{32,0},{1,33},{33,1},{2,34},{34,2},{3,35},{35,3},{4,36},{36... | collective-permute-start | bytes 49160 | tf_op jit(solution)/shard_map/ppermute | solution.py:228
  75.7 0.8 collective-permute-done
  76.6 24.6 %all-to-all-done.2 = f16[64,64,128]{2,1,0:T(8,128)(2,1)S(1)} async-done(((f16[64,64,128]{2,1,0:T(8,128)(2,1)}), f16[64,64,128]{2,1,0:T(8,128)(2,1)S(1)}, u32[]{:S(2)}, u32[]{:S(2)}) %all-to-all-start.2) | async-done | bytes 1048608 | tf_op jit(solution)/shard_map/all_to_all | solution.py:224
  101.5 1.9 %shard_map.50 = bf16[64,2048]{1,0:T(8,128)(2,1)} custom-call(s32[2,16,128]{2,1,0:T(8,128)S(1)} %shard_map.48.place_ref, f32[4,2,2,64,128]{4,3,2,1,0:T(8,128)S(1)} %convert_reduce_fusion.sums_ref, bf16[64,2048]{1,0:T(8,128)(2,1)S(1)} %bitcast.16), custom_call_target="tpu_custom_call" | custom-call | flops 67108864 | bytes 2097152 | tf_op jit(solution)/shard_map/pallas_call | solution.py:182
  (15 shorter events, 0.4 us)
Async XLA Ops:
  0.0 0.9 copy-start
  1.0 0.7 copy-start.2
  1.6 7.2 %copy-start.3 = (bf16[512,1024]{1,0:T(8,128)(2,1)S(1)}, bf16[512,1024]{1,0:T(8,128)(2,1)}, u32[]{:S(2)}) copy-start(bf16[512,1024]{1,0:T(8,128)(2,1)} %refs_0_.1) | copy-start | bytes 3145732
  2.9 12.7 %all-to-all-start = ((bf16[8,24,1024]{2,1,0:T(8,128)(2,1)}), bf16[8,24,1024]{2,1,0:T(8,128)(2,1)S(1)}, u32[]{:S(2)}, u32[]{:S(2)}) async-start(bf16[8,24,1024]{2,1,0:T(8,128)(2,1)} %shard_map.46), calls=%async_computation | async-start | bytes 786432 | tf_op jit(solution)/shard_map/all_to_all | solution.py:197
  8.8 24.9 %collective-permute-start.1 = (bf16[512,1024]{1,0:T(8,128)(2,1)S(1)}, bf16[512,1024]{1,0:T(8,128)(2,1)S(1)}, u32[]{:S(2)}, u32[]{:S(2)}) collective-permute-start(bf16[512,1024]{1,0:T(8,128)(2,1)S(1)} %copy-done.3), channel_id=1, source_target_pairs={{0,4},{4,0},{1,5},{5,1},{2,6},{6,2},{3,7},{7,3},{8,12},{12,8},{9,1... | collective-permute-start | bytes 3145736 | tf_op jit(solution)/shard_map/ppermute | solution.py:202
  16.9 39.1 %all-to-all-start.1 = ((bf16[8,32,2176]{2,1,0:T(8,128)(2,1)}), bf16[8,32,2176]{2,1,0:T(8,128)(2,1)S(1)}, u32[]{:S(2)}, u32[]{:S(2)}) async-start(bf16[8,32,2176]{2,1,0:T(8,128)(2,1)} %shard_map.47), calls=%async_computation.1 | async-start | bytes 2228224 | tf_op jit(solution)/shard_map/all_to_all | solution.py:200
  28.0 12.7 %collective-permute-start.2 = (bf16[512,1024]{1,0:T(8,128)(2,1)S(1)}, bf16[512,1024]{1,0:T(8,128)(2,1)S(1)}, u32[]{:S(2)}, u32[]{:S(2)}) collective-permute-start(bf16[512,1024]{1,0:T(8,128)(2,1)S(1)} %copy-done.3), channel_id=1, source_target_pairs={{0,32},{32,0},{1,33},{33,1},{2,34},{34,2},{3,35},{35,3},{4,36},{36... | collective-permute-start | bytes 3145736 | tf_op jit(solution)/shard_map/ppermute | solution.py:203
  33.6 9.3 %collective-permute-start.3 = (bf16[512,1024]{1,0:T(8,128)(2,1)S(1)}, bf16[512,1024]{1,0:T(8,128)(2,1)S(1)}, u32[]{:S(2)}, u32[]{:S(2)}) collective-permute-start(bf16[512,1024]{1,0:T(8,128)(2,1)S(1)} %collective-permute-done.1.refs_1_), channel_id=1, source_target_pairs={{0,32},{32,0},{1,33},{33,1},{2,34},{34,2},{3,35},{35,3},{4,36},{36... | collective-permute-start | bytes 3145736 | tf_op jit(solution)/shard_map/ppermute | solution.py:204
  40.7 1.0 copy-start.4
  42.9 1.0 copy-start.6
  56.0 1.2 %copy-start.5 = (bf16[512,1024]{1,0:T(8,128)(2,1)S(1)}, bf16[512,1024]{1,0:T(8,128)(2,1)}, u32[]{:S(2)}) copy-start(bf16[512,1024]{1,0:T(8,128)(2,1)} %copy-done.4) | copy-start | bytes 3145732
  57.2 1.2 %copy-start.7 = (bf16[512,1024]{1,0:T(8,128)(2,1)S(1)}, bf16[512,1024]{1,0:T(8,128)(2,1)}, u32[]{:S(2)}) copy-start(bf16[512,1024]{1,0:T(8,128)(2,1)} %copy-done.6) | copy-start | bytes 3145732
  63.0 38.2 %all-to-all-start.2 = ((f16[64,64,128]{2,1,0:T(8,128)(2,1)}), f16[64,64,128]{2,1,0:T(8,128)(2,1)S(1)}, u32[]{:S(2)}, u32[]{:S(2)}) async-start(f16[64,64,128]{2,1,0:T(8,128)(2,1)} %bitcast.4), calls=%async_computation.2 | async-start | bytes 2097152 | tf_op jit(solution)/shard_map/all_to_all | solution.py:224
  73.2 28.3 %copy-start.1 = (bf16[1,2048,64]{1,2,0:T(8,128)(2,1)S(1)}, bf16[1,2048,64]{1,2,0:T(8,128)(2,1)}, u32[]{:S(2)}) copy-start(bf16[1,2048,64]{1,2,0:T(8,128)(2,1)} %param.7) | copy-start | bytes 786436
  73.2 3.3 %collective-permute-start = (bf16[8,8,128]{2,1,0:T(8,128)(2,1)S(1)}, bf16[8,8,128]{2,1,0:T(8,128)(2,1)S(1)}, u32[]{:S(2)}, u32[]{:S(2)}) collective-permute-start(bf16[8,8,128]{2,1,0:T(8,128)(2,1)S(1)} %get-tuple-element.6), channel_id=1, source_target_pairs={{0,32},{32,0},{1,33},{33,1},{2,34},{34,2},{3,35},{35,3},{4,36},{36... | collective-permute-start | bytes 49160 | tf_op jit(solution)/shard_map/ppermute | solution.py:228

commit v3 on v2

--- a/solution.py
+++ b/solution.py
@@ -10,8 +10,9 @@
 T = 128
 KD = 1024
 CLASSES = 8
-SEND = 24
 BASE = 16
+REST = 2 * BASE
+SEND = REST + 8
 SHARE = 32
 Z = 8
 ROWS = Z * BASE
@@ -27,25 +28,31 @@
     return jnp.dot(active.astype(bf16), before, preferred_element_type=f32).astype(i32)
 
 
-def pack_kernel(labels_ref, rows_ref, out_ref):
+def pack_kernel(labels_far, rows_far, out_ref, labels_ref, rows_ref, sems):
+    labels_in = pltpu.make_async_copy(labels_far, labels_ref, sems.at[0])
+    rows_in = pltpu.make_async_copy(rows_far, rows_ref, sems.at[1])
+    labels_in.start()
+    rows_in.start()
+    labels_in.wait()
     active = jnp.broadcast_to(labels_ref[...] == 0, (8, T)).astype(i32).astype(f32)
     rank = jnp.where(active[:1] > 0, ranks(active)[:1], -1)
     count = jnp.sum(active, axis=1, keepdims=True).astype(i32)[:1]
     even = (count >> 3) << 3
+    rows_in.wait()
     rows = rows_ref[...]
     slot = iota((SEND, T), 0)
     lane = iota((SEND, KD), 1)
     srow = iota((SEND, KD), 0)
     flags = jnp.concatenate([active[:1]] * (KD // T), axis=1)
     info = jnp.where(lane < T, flags, count.astype(f32))
-    for q in range(CLASSES):
-        shared = 8 * slot + q
-        rest = even + slot - BASE
-        target = jnp.where(slot < BASE, shared, rest)
-        bound = jnp.where(slot < BASE, even, jnp.where(slot < SEND - 1, count, 0))
+    for rep in range(LAYERS):
+        shared = 8 * (slot & (BASE - 1)) + 2 * rep + (slot >> 4)
+        rest = even + slot - REST
+        target = jnp.where(slot < REST, shared, rest)
+        bound = jnp.where(slot < REST, even, jnp.where(slot < SEND - 1, count, 0))
         hot = ((rank == target) & (target < bound)).astype(f32).astype(bf16)
         picked = jnp.dot(hot, rows, preferred_element_type=f32)
-        out_ref[q] = jnp.where(srow == SEND - 1, info, picked).astype(bf16)
+        out_ref[rep] = jnp.where(srow == SEND - 1, info, picked).astype(bf16)
 
 
 def shares(counts, q):
@@ -60,33 +67,28 @@
 
 
 def share_kernel(got_ref, out_ref):
-    rep, own = lax.axis_index("rep"), lax.axis_index("b")
-    q = 2 * rep + own
-    counts = [
-        got_ref[l, 0, SEND - 1 : SEND, T : 2 * T].astype(f32).astype(i32) for l in range(LAYERS)
-    ]
-    s = iota((SHARE, SEND), 0)
-    slot = iota((SHARE, SEND), 1)
-    total = [jnp.zeros((SHARE, KD), f32) for _ in range(2)]
-    for l, (start, length, base, extra) in enumerate(shares(counts, q)):
-        start, length, base, extra = (v[:, :SEND] for v in (start, length, base, extra))
-        i = s - start
-        inside = (i >= 0) & (i < length)
-        want = jnp.where(i < base, i, BASE + extra)
-        hot = (inside & (slot == want)).astype(f32).astype(bf16)
-        for h in range(2):
-            half = own if h == 0 else 1 - own
-            total[h] += jnp.dot(hot, got_ref[l, half], preferred_element_type=f32)
+    rep = lax.axis_index("rep")
+    counts = [got_ref[l, SEND - 1 : SEND, T : 2 * T].astype(f32).astype(i32) for l in range(LAYERS)]
     row = iota((SHARE, T), 0)
     info = jnp.zeros((SHARE, T), f32)
     for l in range(LAYERS):
-        mine = got_ref[l, 0, SEND - 1 : SEND, :T].astype(f32)
+        mine = got_ref[l, SEND - 1 : SEND, :T].astype(f32)
         info = jnp.where((row == 0) & (rep == l), mine, info)
         info = jnp.where(row == 1 + l, counts[l].astype(f32), info)
-    for z in range(Z):
-        for h in range(2):
-            out_ref[z, :, h * KD : (h + 1) * KD] = total[h].astype(bf16)
-        out_ref[z, :, 2 * KD :] = info.astype(bf16)
+    s = iota((SHARE, SEND), 0)
+    slot = iota((SHARE, SEND), 1)
+    for b in range(2):
+        total = jnp.zeros((SHARE, KD), f32)
+        for l, parts in enumerate(shares(counts, 2 * rep + b)):
+            start, length, base, extra = (v[:, :SEND] for v in parts)
+            i = s - start
+            inside = (i >= 0) & (i < length)
+            want = jnp.where(i < base, BASE * b + i, REST + extra)
+            hot = (inside & (slot == want)).astype(f32).astype(bf16)
+            total += jnp.dot(hot, got_ref[l], preferred_element_type=f32)
+        for z in range(Z):
+            out_ref[b, z, :, :KD] = total.astype(bf16)
+            out_ref[b, z, :, KD:] = info.astype(bf16)
 
 
 def ladder_kernel(got_ref, *refs):
@@ -101,14 +103,21 @@
     for l in range(LAYERS):
         n = jnp.zeros((1, Z * SHARE), f32)
         for z in range(Z):
-            one = got_ref[z, 1 + l : 2 + l, 2 * KD :].astype(f32)
+            one = got_ref[0, z, 1 + l : 2 + l, KD:].astype(f32)
             n = jnp.where((lane >> 5) == z, jnp.concatenate([one, one], axis=1), n)
         counts.append(n.astype(i32))
     row = iota((ROWS, Z * SHARE), 0)
     col = iota((ROWS, Z * SHARE), 1)
     i = row & (BASE - 1)
     same = (row >> 4) == (col >> 5)
-    rows = jnp.concatenate([got_ref[z, :, : 2 * KD] for z in range(Z)], axis=0)
+    pair = lax.axis_index("b")
+    rows = jnp.concatenate(
+        [
+            jnp.concatenate([got_ref[half, z, :, :KD] for z in range(Z)], axis=0)
+            for half in (pair, 1 - pair)
+        ],
+        axis=1,
+    )
     for l, (start, length, _, _) in enumerate(shares(counts, q)):
         hot = (same & (i < length) & ((col & (SHARE - 1)) == start + i)).astype(f32).astype(bf16)
         spread_ref[l * ROWS : (l + 1) * ROWS, :] = jnp.dot(
@@ -174,15 +183,15 @@
 
 
 VMEM = pl.BlockSpec(memory_space=pltpu.VMEM)
-ANY = pl.BlockSpec(memory_space=pl.ANY)
+HBM = pl.BlockSpec(memory_space=pltpu.HBM)
 MIB = 2**20
 
 
-def call(kernel, shape, dtype, *args, anys=0, scratch=(), limit=8, flops=0):
+def call(kernel, shape, dtype, *args, far=0, scratch=(), limit=8, flops=0):
     return pl.pallas_call(
         kernel,
         out_shape=jax.ShapeDtypeStruct(shape, dtype),
-        in_specs=[VMEM] * (len(args) - anys) + [ANY] * anys,
+        in_specs=[VMEM] * (len(args) - far) + [HBM] * far,
         out_specs=VMEM,
         scratch_shapes=scratch,
         compiler_params=pltpu.CompilerParams(vmem_limit_bytes=limit * MIB),
@@ -193,11 +202,21 @@
 def step(amplitudes, pair_irrep, integrals, residual_in):
     swap = [(0, 1), (1, 0)]
 
-    packed = call(pack_kernel, (CLASSES, SEND, KD), bf16, pair_irrep, amplitudes[0], flops=2**26)
-    got = lax.all_to_all(packed, ("rep", "b"), 0, 0, tiled=True)
-    got = got.reshape(LAYERS, 2, SEND, KD)
-    shared = call(share_kernel, (Z, SHARE, 2 * KD + T), bf16, got, flops=2**26)
-    gathered = lax.all_to_all(shared, "z", 0, 0, tiled=True)
+    packed = call(
+        pack_kernel,
+        (LAYERS, SEND, KD),
+        bf16,
+        pair_irrep,
+        amplitudes[0],
+        far=2,
+        scratch=[pltpu.VMEM((1, T), i32), pltpu.VMEM((T, KD), bf16), pltpu.SemaphoreType.DMA((2,))],
+        flops=2**26,
+    )
+    got = lax.all_to_all(packed, "rep", 0, 0, tiled=True)
+    shared = call(share_kernel, (2, Z, SHARE, KD + T), bf16, got, flops=2**26)
+    gathered = lax.all_to_all(
+        shared.reshape(2 * Z, SHARE, KD + T), ("b", "z"), 0, 0, tiled=True
+    ).reshape(2, Z, SHARE, KD + T)
 
     other = lax.ppermute(integrals, "b", swap)
     across = lax.ppermute(integrals, "k", swap)
@@ -213,10 +232,10 @@
         other,
         across,
         across_other,
-        anys=4,
+        far=4,
         scratch=[tall] * 4
         + [pltpu.VMEM((LAYERS * ROWS, 2 * KD), bf16), pltpu.SemaphoreType.DMA((4,))],
-        limit=24,
+        limit=54,
         flops=2**31,
     )
 
@@ -224,7 +243,7 @@
     parts = lax.all_to_all(sent, ("rep", "k", "g", "b"), 0, 0, tiled=True)
     sums = jnp.sum(parts.reshape(LAYERS, 2, 4, 2, 64, ROWS).astype(f32), axis=2)
 
-    info = gathered[:, :8, 2 * KD :]
+    info = gathered[0, :, :8, KD:]
     info_across = lax.ppermute(info, "k", swap)
     place = call(place_kernel, (2, 2 * Z, T), i32, jnp.stack([info, info_across]), flops=2**20)
     out = call(final_kernel, (64, 2048), bf16, place, sums, residual_in[0].T, flops=2**26)

time: 104 us -> 119 us (1.14)
  waiting for transfers between devices: 42.5 us -> 55 us
  starting transfers between devices: 45.3 us -> 34.7 us
  blocking collectives: 0 us -> 10.5 us
  Pallas kernels: 8.1 us -> 11 us
  local copies, waits for them, and re-layouts: 6.02 us -> 4.36 us
  other arithmetic: 1.37 us -> 2.98 us
    ppermute x1, waiting for transfers between devices: 0.27 us -> 28.8 us  [step(): other = lax.ppermute(integrals, 'b', swap)]
    all_to_all x2 -> x1, waiting for transfers between devices: 15.6 us -> 0.01 us  [step(): lax.all_to_all(shared.reshape(2 * Z, SHARE, KD + T), ('b', 'z'), 0, 0, ti...]
    all_to_all x0 -> x1, blocking collectives: none -> 10.5 us  [step(): got = lax.all_to_all(packed, 'rep', 0, 0, tiled=True)]
    all_to_all x2 -> x1, starting transfers between devices: 16.9 us -> 11.6 us  [step(): lax.all_to_all(shared.reshape(2 * Z, SHARE, KD + T), ('b', 'z'), 0, 0, ti...]
    pallas_call x5, Pallas kernels: 8.1 us -> 11 us  [call(): pl.pallas_call(kernel, out_shape=jax.ShapeDtypeStruct(shape, dtype), in_s...]
    unnamed x16 -> x14, local copies, waits for them, and re-layouts: 6.02 us -> 3.6 us
    all_to_all x1, starting transfers between devices: 10.1 us -> 7.74 us  [step(): parts = lax.all_to_all(sent, ('rep', 'k', 'g', 'b'), 0, 0, tiled=True)]
    ppermute x1, starting transfers between devices: 7 us -> 4.89 us  [step(): across_other = lax.ppermute(other, 'k', swap)]
  transfers between devices with their start and end apart: 7 -> 6, of which waited for: 6 -> 4; matrix products, arithmetic and copies ran while one was open for 0% -> 1% of each run, Pallas kernels for 1% -> 0%
where the time goes in v3:
time: 119 us
  waiting for transfers between devices  55 us (46%)
  starting transfers between devices  34.7 us (29%)
  Pallas kernels  11 us (9%)
  blocking collectives  10.5 us (9%)
  local copies, waits for them, and re-layouts  4.36 us (4%)
  other arithmetic  2.98 us (3%)
    ppermute x1, waiting for transfers between devices, step(): other = lax.ppermute(integrals, 'b', swap)  28.8 us
    all_to_all x1, waiting for transfers between devices, step(): parts = lax.all_to_all(sent, ('rep', 'k', 'g', 'b'), 0, 0, tiled=True)  24 us
    all_to_all x1, starting transfers between devices, step(): lax.all_to_all(shared.reshape(2 * Z, SHARE, KD + T), ('b', 'z'), 0, 0, ti...  11.6 us
    pallas_call x5, Pallas kernels, call(): pl.pallas_call(kernel, out_shape=jax.ShapeDtypeStruct(shape, dtype), in_s...  11 us
    all_to_all x1, blocking collectives, step(): got = lax.all_to_all(packed, 'rep', 0, 0, tiled=True)  10.5 us
    all_to_all x1, starting transfers between devices, step(): parts = lax.all_to_all(sent, ('rep', 'k', 'g', 'b'), 0, 0, tiled=True)  7.74 us
    ppermute x1, starting transfers between devices, step(): across_other = lax.ppermute(other, 'k', swap)  4.89 us
    ppermute x1, starting transfers between devices, step(): across = lax.ppermute(integrals, 'k', swap)  4.85 us
  transfers between devices with their start and end apart: 6, of which 4 were waited for; matrix products, arithmetic and copies ran while one was open for 1% of the time, Pallas kernels for 0%

profile of v3, /device:TPU:1, one launch (start us, length us, event | category | flops | bytes accessed | tf_op | source)
XLA Modules:
  0.0 118.8 jit_solution(9438885674757801483)
XLA Ops:
  0.0 0.9 copy-done
  1.0 0.7 copy-done.2
  1.6 0.5 shard_map.46
  2.1 10.5 %all_to_all.15.got_ref = bf16[4,40,1024]{2,1,0:T(8,128)(2,1)S(1)} all-to-all(bf16[4,40,1024]{2,1,0:T(8,128)(2,1)S(1)} %shard_map.46), channel_id=1, replica_groups=mesh['z'=8,'k'=2,'g'=4,'b'=2,'rep'=4] {'rep'}, dimensions={0} | all-to-all | bytes 655360 | tf_op jit(solution)/shard_map/all_to_all | solution.py:215
  12.6 1.3 %shard_map.47 = bf16[2,8,32,1152]{3,2,1,0:T(8,128)(2,1)} custom-call(bf16[4,40,1024]{2,1,0:T(8,128)(2,1)S(1)} %all_to_all.15.got_ref), custom_call_target="tpu_custom_call" | custom-call | flops 67108864 | bytes 2097152 | tf_op jit(solution)/shard_map/pallas_call | solution.py:191
  14.0 11.6 %all-to-all-start.1 = ((bf16[16,32,1152]{2,1,0:T(8,128)(2,1)}), bf16[16,32,1152]{2,1,0:T(8,128)(2,1)S(1)}, u32[]{:S(2)}, u32[]{:S(2)}) async-start(bf16[16,32,1152]{2,1,0:T(8,128)(2,1)} %bitcast.1), calls=%async_computation.1 | async-start | bytes 2359296 | tf_op jit(solution)/shard_map/all_to_all | solution.py:217
  25.6 3.3 %collective-permute-start.1 = (bf16[512,1024]{1,0:T(8,128)(2,1)S(1)}, bf16[512,1024]{1,0:T(8,128)(2,1)S(1)}, u32[]{:S(2)}, u32[]{:S(2)}) collective-permute-start(bf16[512,1024]{1,0:T(8,128)(2,1)S(1)} %copy-done.4), channel_id=1, source_target_pairs={{0,4},{4,0},{1,5},{5,1},{2,6},{6,2},{3,7},{7,3},{8,12},{12,8},{9,1... | collective-permute-start | bytes 3145736 | tf_op jit(solution)/shard_map/ppermute | solution.py:221
  28.9 4.9 %collective-permute-start.2 = (bf16[512,1024]{1,0:T(8,128)(2,1)S(1)}, bf16[512,1024]{1,0:T(8,128)(2,1)S(1)}, u32[]{:S(2)}, u32[]{:S(2)}) collective-permute-start(bf16[512,1024]{1,0:T(8,128)(2,1)S(1)} %copy-done.4), channel_id=1, source_target_pairs={{0,32},{32,0},{1,33},{33,1},{2,34},{34,2},{3,35},{35,3},{4,36},{36... | collective-permute-start | bytes 3145736 | tf_op jit(solution)/shard_map/ppermute | solution.py:222
  33.7 28.8 %collective-permute-done.1.refs_1_ = bf16[512,1024]{1,0:T(8,128)(2,1)S(1)} collective-permute-done((bf16[512,1024]{1,0:T(8,128)(2,1)S(1)}, bf16[512,1024]{1,0:T(8,128)(2,1)S(1)}, u32[]{:S(2)}, u32[]{:S(2)}) %collective-permute-start.1) | collective-permute-done | bytes 1048608 | tf_op jit(solution)/shard_map/ppermute | solution.py:221
  62.5 4.9 %collective-permute-start.3 = (bf16[512,1024]{1,0:T(8,128)(2,1)S(1)}, bf16[512,1024]{1,0:T(8,128)(2,1)}, u32[]{:S(2)}, u32[]{:S(2)}) collective-permute-start(bf16[512,1024]{1,0:T(8,128)(2,1)S(1)} %collective-permute-done.1.refs_1_), channel_id=1, source_target_pairs={{0,32},{32,0},{1,33},{33,1},{2,34},{34,2},{3,35},{35,3},{4,36},{36... | collective-permute-start | bytes 3145736 | tf_op jit(solution)/shard_map/ppermute | solution.py:223
  67.5 1.0 copy-done.6
  68.4 1.4 %collective-permute-done.3.refs_3_ = bf16[512,1024]{1,0:T(8,128)(2,1)} collective-permute-done((bf16[512,1024]{1,0:T(8,128)(2,1)S(1)}, bf16[512,1024]{1,0:T(8,128)(2,1)}, u32[]{:S(2)}, u32[]{:S(2)}) %collective-permute-start.3) | collective-permute-done | bytes 1048608 | tf_op jit(solution)/shard_map/ppermute | solution.py:223
  69.8 1.0 copy-done.3
  70.9 7.2 %shard_map.49 = f32[4,2,512,128]{3,2,1,0:T(8,128)} custom-call(bf16[2,8,32,1152]{3,2,1,0:T(8,128)(2,1)} %bitcast.18, bf16[512,1024]{1,0:T(8,128)(2,1)} %refs_0_.1, bf16[512,1024]{1,0:T(8,128)(2,1)} %copy-done.5, bf16[512,1024]{1,0:T(8,128)(2,1)} %copy-done.6, bf16[512,1024]{1,0:T(8,128)(2,1)} %collective-permute-done.3.refs_3_), custom_call_target="tpu_custom_call" | custom-call | flops 2147483648 | bytes 2097152 | tf_op jit(solution)/shard_map/pallas_call | solution.py:191
  78.0 2.7 %convert_element_type.9 = f16[4,2,512,128]{3,2,1,0:T(8,128)(2,1)} convert(f32[4,2,512,128]{3,2,1,0:T(8,128)} %shard_map.49) | non-fusion elementwise | flops 524288 | bytes 3145728 | tf_op jit(solution)/shard_map/convert_element_type | solution.py:242
  80.8 7.7 %all-to-all-start.2 = ((f16[64,64,128]{2,1,0:T(8,128)(2,1)}), f16[64,64,128]{2,1,0:T(8,128)(2,1)S(1)}, u32[]{:S(2)}, u32[]{:S(2)}) async-start(f16[64,64,128]{2,1,0:T(8,128)(2,1)} %bitcast.5), calls=%async_computation.2 | async-start | bytes 2097152 | tf_op jit(solution)/shard_map/all_to_all | solution.py:243
  88.5 0.0 copy-start.1
  88.5 0.8 fusion
  89.3 2.3 %collective-permute-start = (bf16[8,8,128]{2,1,0:T(8,128)(2,1)S(1)}, bf16[8,8,128]{2,1,0:T(8,128)(2,1)S(1)}, u32[]{:S(2)}, u32[]{:S(2)}) collective-permute-start(bf16[8,8,128]{2,1,0:T(8,128)(2,1)S(1)} %get-tuple-element.6), channel_id=1, source_target_pairs={{0,32},{32,0},{1,33},{33,1},{2,34},{34,2},{3,35},{35,3},{4,36},{36... | collective-permute-start | bytes 49160 | tf_op jit(solution)/shard_map/ppermute | solution.py:247
  91.7 0.8 collective-permute-done
  92.5 0.1 shard_map.48.place_ref
  92.6 24.0 %all-to-all-done.2 = f16[64,64,128]{2,1,0:T(8,128)(2,1)S(1)} async-done(((f16[64,64,128]{2,1,0:T(8,128)(2,1)}), f16[64,64,128]{2,1,0:T(8,128)(2,1)S(1)}, u32[]{:S(2)}, u32[]{:S(2)}) %all-to-all-start.2) | async-done | bytes 1048608 | tf_op jit(solution)/shard_map/all_to_all | solution.py:243
  116.6 0.2 convert_reduce_fusion.sums_ref
  116.9 1.9 %shard_map.50 = bf16[64,2048]{1,0:T(8,128)(2,1)} custom-call(s32[2,16,128]{2,1,0:T(8,128)S(1)} %shard_map.48.place_ref, f32[4,2,2,64,128]{4,3,2,1,0:T(8,128)S(1)} %convert_reduce_fusion.sums_ref, bf16[64,2048]{1,0:T(8,128)(2,1)S(1)} %bitcast.16), custom_call_target="tpu_custom_call" | custom-call | flops 67108864 | bytes 2097152 | tf_op jit(solution)/shard_map/pallas_call | solution.py:191
  (12 shorter events, 0.0 us)
Async XLA Ops:
  0.0 0.9 copy-start
  1.0 0.7 copy-start.2
  13.9 11.6 %copy-start.4 = (bf16[512,1024]{1,0:T(8,128)(2,1)S(1)}, bf16[512,1024]{1,0:T(8,128)(2,1)}, u32[]{:S(2)}) copy-start(bf16[512,1024]{1,0:T(8,128)(2,1)} %refs_0_.1) | copy-start | bytes 3145732
  14.0 55.9 %all-to-all-start.1 = ((bf16[16,32,1152]{2,1,0:T(8,128)(2,1)}), bf16[16,32,1152]{2,1,0:T(8,128)(2,1)S(1)}, u32[]{:S(2)}, u32[]{:S(2)}) async-start(bf16[16,32,1152]{2,1,0:T(8,128)(2,1)} %bitcast.1), calls=%async_computation.1 | async-start | bytes 2359296 | tf_op jit(solution)/shard_map/all_to_all | solution.py:217
  25.6 36.9 %collective-permute-start.1 = (bf16[512,1024]{1,0:T(8,128)(2,1)S(1)}, bf16[512,1024]{1,0:T(8,128)(2,1)S(1)}, u32[]{:S(2)}, u32[]{:S(2)}) collective-permute-start(bf16[512,1024]{1,0:T(8,128)(2,1)S(1)} %copy-done.4), channel_id=1, source_target_pairs={{0,4},{4,0},{1,5},{5,1},{2,6},{6,2},{3,7},{7,3},{8,12},{12,8},{9,1... | collective-permute-start | bytes 3145736 | tf_op jit(solution)/shard_map/ppermute | solution.py:221
  28.9 38.6 %collective-permute-start.2 = (bf16[512,1024]{1,0:T(8,128)(2,1)S(1)}, bf16[512,1024]{1,0:T(8,128)(2,1)S(1)}, u32[]{:S(2)}, u32[]{:S(2)}) collective-permute-start(bf16[512,1024]{1,0:T(8,128)(2,1)S(1)} %copy-done.4), channel_id=1, source_target_pairs={{0,32},{32,0},{1,33},{33,1},{2,34},{34,2},{3,35},{35,3},{4,36},{36... | collective-permute-start | bytes 3145736 | tf_op jit(solution)/shard_map/ppermute | solution.py:222
  62.5 7.3 %copy-start.5 = (bf16[512,1024]{1,0:T(8,128)(2,1)}, bf16[512,1024]{1,0:T(8,128)(2,1)S(1)}, u32[]{:S(2)}) copy-start(bf16[512,1024]{1,0:T(8,128)(2,1)S(1)} %collective-permute-done.1.refs_1_) | copy-start | bytes 3145732
  62.5 7.3 %collective-permute-start.3 = (bf16[512,1024]{1,0:T(8,128)(2,1)S(1)}, bf16[512,1024]{1,0:T(8,128)(2,1)}, u32[]{:S(2)}, u32[]{:S(2)}) collective-permute-start(bf16[512,1024]{1,0:T(8,128)(2,1)S(1)} %collective-permute-done.1.refs_1_), channel_id=1, source_target_pairs={{0,32},{32,0},{1,33},{33,1},{2,34},{34,2},{3,35},{35,3},{4,36},{36... | collective-permute-start | bytes 3145736 | tf_op jit(solution)/shard_map/ppermute | solution.py:223
  67.4 1.0 copy-start.6
  69.8 1.0 copy-start.3
  80.8 35.8 %all-to-all-start.2 = ((f16[64,64,128]{2,1,0:T(8,128)(2,1)}), f16[64,64,128]{2,1,0:T(8,128)(2,1)S(1)}, u32[]{:S(2)}, u32[]{:S(2)}) async-start(f16[64,64,128]{2,1,0:T(8,128)(2,1)} %bitcast.5), calls=%async_computation.2 | async-start | bytes 2097152 | tf_op jit(solution)/shard_map/all_to_all | solution.py:243
  88.5 28.3 %copy-start.1 = (bf16[1,2048,64]{1,2,0:T(8,128)(2,1)S(1)}, bf16[1,2048,64]{1,2,0:T(8,128)(2,1)}, u32[]{:S(2)}) copy-start(bf16[1,2048,64]{1,2,0:T(8,128)(2,1)} %param.7) | copy-start | bytes 786436
  89.3 3.2 %collective-permute-start = (bf16[8,8,128]{2,1,0:T(8,128)(2,1)S(1)}, bf16[8,8,128]{2,1,0:T(8,128)(2,1)S(1)}, u32[]{:S(2)}, u32[]{:S(2)}) collective-permute-start(bf16[8,8,128]{2,1,0:T(8,128)(2,1)S(1)} %get-tuple-element.6), channel_id=1, source_target_pairs={{0,32},{32,0},{1,33},{33,1},{2,34},{34,2},{3,35},{35,3},{4,36},{36... | collective-permute-start | bytes 49160 | tf_op jit(solution)/shard_map/ppermute | solution.py:247

commit v4 on v3

--- a/solution.py
+++ b/solution.py
@@ -15,7 +15,6 @@
 SEND = REST + 8
 SHARE = 32
 Z = 8
-ROWS = Z * BASE
 i32, f32, bf16 = jnp.int32, jnp.float32, jnp.bfloat16
 
 
@@ -28,17 +27,11 @@
     return jnp.dot(active.astype(bf16), before, preferred_element_type=f32).astype(i32)
 
 
-def pack_kernel(labels_far, rows_far, out_ref, labels_ref, rows_ref, sems):
-    labels_in = pltpu.make_async_copy(labels_far, labels_ref, sems.at[0])
-    rows_in = pltpu.make_async_copy(rows_far, rows_ref, sems.at[1])
-    labels_in.start()
-    rows_in.start()
-    labels_in.wait()
+def pack_kernel(labels_ref, rows_ref, out_ref):
     active = jnp.broadcast_to(labels_ref[...] == 0, (8, T)).astype(i32).astype(f32)
     rank = jnp.where(active[:1] > 0, ranks(active)[:1], -1)
     count = jnp.sum(active, axis=1, keepdims=True).astype(i32)[:1]
     even = (count >> 3) << 3
-    rows_in.wait()
     rows = rows_ref[...]
     slot = iota((SEND, T), 0)
     lane = iota((SEND, KD), 1)
@@ -92,57 +85,27 @@
 
 
 def ladder_kernel(got_ref, *refs):
-    pieces, out_ref, buffers, spread_ref, sems = refs[:4], refs[4], refs[5:9], refs[9], refs[10]
+    pieces, out_ref, buffers, sems = refs[:4], refs[4], refs[5:9], refs[9]
     copies = [pltpu.make_async_copy(pieces[n], buffers[n], sems.at[n]) for n in range(4)]
     for copy in copies:
         copy.start()
-    q = 2 * lax.axis_index("rep") + lax.axis_index("b")
-    own = lax.axis_index("k")
-    lane = iota((1, Z * SHARE), 1)
-    counts = []
-    for l in range(LAYERS):
-        n = jnp.zeros((1, Z * SHARE), f32)
-        for z in range(Z):
-            one = got_ref[0, z, 1 + l : 2 + l, KD:].astype(f32)
-            n = jnp.where((lane >> 5) == z, jnp.concatenate([one, one], axis=1), n)
-        counts.append(n.astype(i32))
-    row = iota((ROWS, Z * SHARE), 0)
-    col = iota((ROWS, Z * SHARE), 1)
-    i = row & (BASE - 1)
-    same = (row >> 4) == (col >> 5)
-    pair = lax.axis_index("b")
-    rows = jnp.concatenate(
-        [
-            jnp.concatenate([got_ref[half, z, :, :KD] for z in range(Z)], axis=0)
-            for half in (pair, 1 - pair)
-        ],
-        axis=1,
-    )
-    for l, (start, length, _, _) in enumerate(shares(counts, q)):
-        hot = (same & (i < length) & ((col & (SHARE - 1)) == start + i)).astype(f32).astype(bf16)
-        spread_ref[l * ROWS : (l + 1) * ROWS, :] = jnp.dot(
-            hot, rows, preferred_element_type=f32
-        ).astype(bf16)
+    own, pair = lax.axis_index("k"), lax.axis_index("b")
+    rows = [
+        jnp.concatenate([got_ref[half, z, :, :KD] for z in range(Z)], axis=0)
+        for half in (pair, 1 - pair)
+    ]
     dims = (((1,), (1,)), ((), ()))
-    for copy in copies:
-        copy.wait()
-    step = 256
     for side in range(2):
-        for at in range(0, 512, step):
-            part = jnp.zeros((step, LAYERS * ROWS), f32)
-            for h in range(2):
-                part += lax.dot_general(
-                    buffers[2 * side + h][at : at + step, :],
-                    spread_ref[:, h * KD : (h + 1) * KD],
-                    dims,
-                    preferred_element_type=f32,
-                )
-            core = own if side == 0 else 1 - own
-            for l in range(LAYERS):
-                out_ref[l, core, at : at + step, :] = part[:, l * ROWS : (l + 1) * ROWS]
-
-
-def place_kernel(info_ref, out_ref):
+        part = jnp.zeros((512, Z * SHARE), f32)
+        for h in range(2):
+            copies[2 * side + h].wait()
+            part += lax.dot_general(
+                buffers[2 * side + h][...], rows[h], dims, preferred_element_type=f32
+            )
+        out_ref[own if side == 0 else 1 - own] = part
+
+
+def plan_kernel(info_ref, place_ref, route_ref):
     rep, own = lax.axis_index("rep"), lax.axis_index("k")
 
     def of(r):
@@ -158,13 +121,38 @@
     rank = ranks(active)
     offset = jnp.zeros((2 * Z, T), i32)
     even = jnp.zeros((2 * Z, T), i32)
-    for l in range(LAYERS):
-        n = of(1 + l).astype(i32)
+    counts = [of(1 + l).astype(i32) for l in range(LAYERS)]
+    for l, n in enumerate(counts):
         offset += jnp.where(l < rep, n & 7, 0)
         even = jnp.where(l == rep, (n >> 3) << 3, even)
     cls = jnp.where(rank < even, rank, offset + rank - even) & 7
-    out_ref[0] = jnp.where(active > 0, cls, -1)
-    out_ref[1] = jnp.minimum(rank >> 3, BASE - 1)
+    place_ref[0] = jnp.where(active > 0, cls, -1)
+    place_ref[1] = jnp.minimum(rank >> 3, BASE - 1)
+
+    lane = iota((1, T), 1)
+    for k in range(2):
+        spread = []
+        for n in counts:
+            at = jnp.zeros((1, T), i32)
+            for z in range(Z):
+                at = jnp.where((lane >> 4) == z, n[k * Z + z : k * Z + z + 1], at)
+            spread.append(at)
+        for b in range(2):
+            for l, (start, _, _, _) in enumerate(shares(spread, 2 * rep + b)):
+                source = SHARE * ((lane >> 4) & 3) + start + (lane & (BASE - 1))
+                route_ref[(l * 2 + k) * 2 + b : (l * 2 + k) * 2 + b + 1, :] = source & (T - 1)
+
+
+def route_kernel(route_ref, sums_ref, out_ref):
+    low = iota((64, T), 1) < T // 2
+    for k in range(2):
+        for b in range(2):
+            halves = [sums_ref[k, b, :, h * T : (h + 1) * T] for h in range(2)]
+            for l in range(LAYERS):
+                row = (l * 2 + k) * 2 + b
+                source = jnp.broadcast_to(route_ref[row : row + 1, :], (64, T))
+                first, second = (jnp.take_along_axis(x, source, axis=1) for x in halves)
+                out_ref[l, k, b] = jnp.where(low, first, second)
 
 
 def final_kernel(place_ref, sums_ref, residual_ref, out_ref):
@@ -190,9 +178,11 @@
 def call(kernel, shape, dtype, *args, far=0, scratch=(), limit=8, flops=0):
     return pl.pallas_call(
         kernel,
-        out_shape=jax.ShapeDtypeStruct(shape, dtype),
+        out_shape=[jax.ShapeDtypeStruct(one, dtype) for one in shape]
+        if isinstance(shape, list)
+        else jax.ShapeDtypeStruct(shape, dtype),
         in_specs=[VMEM] * (len(args) - far) + [HBM] * far,
-        out_specs=VMEM,
+        out_specs=[VMEM] * len(shape) if isinstance(shape, list) else VMEM,
         scratch_shapes=scratch,
         compiler_params=pltpu.CompilerParams(vmem_limit_bytes=limit * MIB),
         cost_estimate=pl.CostEstimate(flops=flops, bytes_accessed=2**21, transcendentals=0),
@@ -202,16 +192,7 @@
 def step(amplitudes, pair_irrep, integrals, residual_in):
     swap = [(0, 1), (1, 0)]
 
-    packed = call(
-        pack_kernel,
-        (LAYERS, SEND, KD),
-        bf16,
-        pair_irrep,
-        amplitudes[0],
-        far=2,
-        scratch=[pltpu.VMEM((1, T), i32), pltpu.VMEM((T, KD), bf16), pltpu.SemaphoreType.DMA((2,))],
-        flops=2**26,
-    )
+    packed = call(pack_kernel, (LAYERS, SEND, KD), bf16, pair_irrep, amplitudes[0], flops=2**26)
     got = lax.all_to_all(packed, "rep", 0, 0, tiled=True)
     shared = call(share_kernel, (2, Z, SHARE, KD + T), bf16, got, flops=2**26)
     gathered = lax.all_to_all(
@@ -222,10 +203,9 @@
     across = lax.ppermute(integrals, "k", swap)
     across_other = lax.ppermute(other, "k", swap)
 
-    tall = pltpu.VMEM((512, KD), bf16)
     partial = call(
         ladder_kernel,
-        (LAYERS, 2, 512, ROWS),
+        (2, 512, Z * SHARE),
         f32,
         gathered,
         integrals,
@@ -233,20 +213,23 @@
         across,
         across_other,
         far=4,
-        scratch=[tall] * 4
-        + [pltpu.VMEM((LAYERS * ROWS, 2 * KD), bf16), pltpu.SemaphoreType.DMA((4,))],
-        limit=54,
-        flops=2**31,
+        scratch=[pltpu.VMEM((512, KD), bf16)] * 4 + [pltpu.SemaphoreType.DMA((4,))],
+        limit=48,
+        flops=2**30,
     )
 
-    sent = partial.astype(jnp.float16).reshape(64, 64, ROWS)
-    parts = lax.all_to_all(sent, ("rep", "k", "g", "b"), 0, 0, tiled=True)
-    sums = jnp.sum(parts.reshape(LAYERS, 2, 4, 2, 64, ROWS).astype(f32), axis=2)
+    sent = partial.astype(jnp.float16).reshape(16, 64, Z * SHARE)
+    parts = lax.all_to_all(sent, ("k", "g", "b"), 0, 0, tiled=True)
+    sums = jnp.sum(parts.reshape(2, 4, 2, 64, Z * SHARE).astype(f32), axis=1)
 
     info = gathered[0, :, :8, KD:]
     info_across = lax.ppermute(info, "k", swap)
-    place = call(place_kernel, (2, 2 * Z, T), i32, jnp.stack([info, info_across]), flops=2**20)
-    out = call(final_kernel, (64, 2048), bf16, place, sums, residual_in[0].T, flops=2**26)
+    place, route = call(
+        plan_kernel, [(2, 2 * Z, T), (16, T)], i32, jnp.stack([info, info_across]), flops=2**20
+    )
+    routed = call(route_kernel, (LAYERS, 2, 2, 64, T), f32, route, sums, flops=2**24)
+    owned = lax.all_to_all(routed, "rep", 0, 0, tiled=True)
+    out = call(final_kernel, (64, 2048), bf16, place, owned, residual_in[0].T, flops=2**26)
     return out.T[None]
 
 

time: 119 us -> 113 us (0.950)
  waiting for transfers between devices: 55 us -> 43 us
  blocking collectives: 10.5 us -> 21.5 us
  Pallas kernels: 11 us -> 8.55 us
  other arithmetic: 2.98 us -> 0.96 us
  starting transfers between devices: 34.7 us -> 33.3 us
    all_to_all x1, waiting for transfers between devices: 24 us -> 10.8 us  [step(): parts = lax.all_to_all(sent, ('k', 'g', 'b'), 0, 0, tiled=True)]
    all_to_all x0 -> x1, blocking collectives: none -> 11 us  [step(): owned = lax.all_to_all(routed, 'rep', 0, 0, tiled=True)]
    pallas_call x5 -> x6, Pallas kernels: 11 us -> 8.55 us  [call(): pl.pallas_call(kernel, out_shape=[jax.ShapeDtypeStruct(one, dtype) for on...]
    convert_element_type x1, other arithmetic: 2.74 us -> 0.88 us  [step(): sent = partial.astype(jnp.float16).reshape(16, 64, Z * SHARE)]
    unnamed x14 -> x12, local copies, waits for them, and re-layouts: 3.6 us -> 3.82 us
where the time goes in v4:
time: 113 us; the launch traced here: 112 us
  waiting for transfers between devices  43 us (38%)
  starting transfers between devices  33.3 us (29%)
  blocking collectives  21.5 us (19%)
  Pallas kernels  8.55 us (8%)
  local copies, waits for them, and re-layouts  4.54 us (4%)
    ppermute x1, waiting for transfers between devices, step(): other = lax.ppermute(integrals, 'b', swap)  28.8 us
    all_to_all x1, starting transfers between devices, step(): lax.all_to_all(shared.reshape(2 * Z, SHARE, KD + T), ('b', 'z'), 0, 0, ti...  11.7 us
    all_to_all x1, blocking collectives, step(): owned = lax.all_to_all(routed, 'rep', 0, 0, tiled=True)  11 us
    all_to_all x1, waiting for transfers between devices, step(): parts = lax.all_to_all(sent, ('k', 'g', 'b'), 0, 0, tiled=True)  10.8 us
    all_to_all x1, blocking collectives, step(): got = lax.all_to_all(packed, 'rep', 0, 0, tiled=True)  10.5 us
    pallas_call x6, Pallas kernels, call(): pl.pallas_call(kernel, out_shape=[jax.ShapeDtypeStruct(one, dtype) for on...  8.55 us
    all_to_all x1, starting transfers between devices, step(): parts = lax.all_to_all(sent, ('k', 'g', 'b'), 0, 0, tiled=True)  6.64 us
    ppermute x1, starting transfers between devices, step(): across_other = lax.ppermute(other, 'k', swap)  4.89 us
  transfers between devices with their start and end apart: 6, of which 4 were waited for; matrix products, arithmetic and copies ran while one was open for 1% of the time, Pallas kernels for 0%

profile of v4, /device:TPU:1, one launch (start us, length us, event | category | flops | bytes accessed | tf_op | source)
XLA Modules:
  0.0 111.8 jit_solution(2571017429646949532)
XLA Ops:
  0.0 0.9 copy-done.3
  1.0 0.7 copy-done.5
  1.6 0.4 shard_map.46
  2.0 10.5 %all_to_all.20.got_ref = bf16[4,40,1024]{2,1,0:T(8,128)(2,1)S(1)} all-to-all(bf16[4,40,1024]{2,1,0:T(8,128)(2,1)S(1)} %shard_map.46), channel_id=1, replica_groups=mesh['z'=8,'k'=2,'g'=4,'b'=2,'rep'=4] {'rep'}, dimensions={0} | all-to-all | bytes 655360 | tf_op jit(solution)/shard_map/all_to_all | solution.py:196
  12.5 1.3 %shard_map.47 = bf16[2,8,32,1152]{3,2,1,0:T(8,128)(2,1)} custom-call(bf16[4,40,1024]{2,1,0:T(8,128)(2,1)S(1)} %all_to_all.20.got_ref), custom_call_target="tpu_custom_call" | custom-call | flops 67108864 | bytes 2097152 | tf_op jit(solution)/shard_map/pallas_call | solution.py:179
  13.9 11.7 %all-to-all-start.1 = ((bf16[16,32,1152]{2,1,0:T(8,128)(2,1)}), bf16[16,32,1152]{2,1,0:T(8,128)(2,1)}, u32[]{:S(2)}, u32[]{:S(2)}) async-start(bf16[16,32,1152]{2,1,0:T(8,128)(2,1)} %bitcast.1), calls=%async_computation.1 | async-start | bytes 2359296 | tf_op jit(solution)/shard_map/all_to_all | solution.py:198
  25.6 3.2 %collective-permute-start.1 = (bf16[512,1024]{1,0:T(8,128)(2,1)S(1)}, bf16[512,1024]{1,0:T(8,128)(2,1)S(1)}, u32[]{:S(2)}, u32[]{:S(2)}) collective-permute-start(bf16[512,1024]{1,0:T(8,128)(2,1)S(1)} %copy-done), channel_id=1, source_target_pairs={{0,4},{4,0},{1,5},{5,1},{2,6},{6,2},{3,7},{7,3},{8,12},{12,8},{9,1... | collective-permute-start | bytes 3145736 | tf_op jit(solution)/shard_map/ppermute | solution.py:202
  28.8 4.9 %collective-permute-start.2 = (bf16[512,1024]{1,0:T(8,128)(2,1)S(1)}, bf16[512,1024]{1,0:T(8,128)(2,1)S(1)}, u32[]{:S(2)}, u32[]{:S(2)}) collective-permute-start(bf16[512,1024]{1,0:T(8,128)(2,1)S(1)} %copy-done), channel_id=1, source_target_pairs={{0,32},{32,0},{1,33},{33,1},{2,34},{34,2},{3,35},{35,3},{4,36},{36... | collective-permute-start | bytes 3145736 | tf_op jit(solution)/shard_map/ppermute | solution.py:203
  33.7 28.8 %collective-permute-done.1.refs_1_ = bf16[512,1024]{1,0:T(8,128)(2,1)S(1)} collective-permute-done((bf16[512,1024]{1,0:T(8,128)(2,1)S(1)}, bf16[512,1024]{1,0:T(8,128)(2,1)S(1)}, u32[]{:S(2)}, u32[]{:S(2)}) %collective-permute-start.1) | collective-permute-done | bytes 1048608 | tf_op jit(solution)/shard_map/ppermute | solution.py:202
  62.5 4.9 %collective-permute-start.3 = (bf16[512,1024]{1,0:T(8,128)(2,1)S(1)}, bf16[512,1024]{1,0:T(8,128)(2,1)S(1)}, u32[]{:S(2)}, u32[]{:S(2)}) collective-permute-start(bf16[512,1024]{1,0:T(8,128)(2,1)S(1)} %collective-permute-done.1.refs_1_), channel_id=1, source_target_pairs={{0,32},{32,0},{1,33},{33,1},{2,34},{34,2},{3,35},{35,3},{4,36},{36... | collective-permute-start | bytes 3145736 | tf_op jit(solution)/shard_map/ppermute | solution.py:204
  67.4 2.3 %collective-permute-done.3.refs_3_ = bf16[512,1024]{1,0:T(8,128)(2,1)S(1)} collective-permute-done((bf16[512,1024]{1,0:T(8,128)(2,1)S(1)}, bf16[512,1024]{1,0:T(8,128)(2,1)S(1)}, u32[]{:S(2)}, u32[]{:S(2)}) %collective-permute-start.3) | collective-permute-done | bytes 1048608 | tf_op jit(solution)/shard_map/ppermute | solution.py:204
  69.6 1.0 copy-done.1
  70.6 1.2 %copy-done.2 = bf16[512,1024]{1,0:T(8,128)(2,1)S(1)} copy-done((bf16[512,1024]{1,0:T(8,128)(2,1)S(1)}, bf16[512,1024]{1,0:T(8,128)(2,1)}, u32[]{:S(2)}) %copy-start.2) | copy-done | bytes 1048600
  71.8 4.4 %shard_map.49 = f32[2,512,256]{2,1,0:T(8,128)S(1)} custom-call(bf16[2,8,32,1152]{3,2,1,0:T(8,128)(2,1)} %bitcast.2.got_ref, bf16[512,1024]{1,0:T(8,128)(2,1)S(1)} %copy-done, bf16[512,1024]{1,0:T(8,128)(2,1)S(1)} %collective-permute-done.1.refs_1_, bf16[512,1024]{1,0:T(8,128)(2,1)S(1)} %collective-permute-done.2.refs_2_, bf16[512,1024]{1,0:T(8,128)(2,1)S(1)} %copy-done.2), custom_call_target="tpu_custom_call" | custom-call | flops 1073741824 | bytes 2097152 | tf_op jit(solution)/shard_map/pallas_call | solution.py:179
  76.2 0.9 convert_element_type.9
  77.1 6.6 %all-to-all-start.2 = ((f16[16,64,256]{2,1,0:T(8,128)(2,1)}), f16[16,64,256]{2,1,0:T(8,128)(2,1)S(1)}, u32[]{:S(2)}, u32[]{:S(2)}) async-start(f16[16,64,256]{2,1,0:T(8,128)(2,1)} %bitcast.5), calls=%async_computation.2 | async-start | bytes 1048576 | tf_op jit(solution)/shard_map/all_to_all | solution.py:222
  83.7 0.7 fusion
  84.5 2.0 %collective-permute-start = (bf16[8,8,128]{2,1,0:T(8,128)(2,1)S(1)}, bf16[8,8,128]{2,1,0:T(8,128)(2,1)S(1)}, u32[]{:S(2)}, u32[]{:S(2)}) collective-permute-start(bf16[8,8,128]{2,1,0:T(8,128)(2,1)S(1)} %get-tuple-element.10), channel_id=1, source_target_pairs={{0,32},{32,0},{1,33},{33,1},{2,34},{34,2},{3,35},{35,3},{4,36},{36... | collective-permute-start | bytes 49160 | tf_op jit(solution)/shard_map/ppermute | solution.py:226
  86.5 1.1 collective-permute-done
  87.5 0.1 shard_map.48
  87.7 10.8 %all-to-all-done.2 = f16[16,64,256]{2,1,0:T(8,128)(2,1)S(1)} async-done(((f16[16,64,256]{2,1,0:T(8,128)(2,1)}), f16[16,64,256]{2,1,0:T(8,128)(2,1)S(1)}, u32[]{:S(2)}, u32[]{:S(2)}) %all-to-all-start.2) | async-done | bytes 524320 | tf_op jit(solution)/shard_map/all_to_all | solution.py:222
  98.6 0.4 shard_map.50
  99.0 11.0 %all_to_all.21.sums_ref = f32[4,2,2,64,128]{4,3,2,1,0:T(8,128)S(1)} all-to-all(f32[4,2,2,64,128]{4,3,2,1,0:T(8,128)S(1)} %shard_map.50), channel_id=1, replica_groups=mesh['z'=8,'k'=2,'g'=4,'b'=2,'rep'=4] {'rep'}, dimensions={0} | all-to-all | bytes 1048576 | tf_op jit(solution)/shard_map/all_to_all | solution.py:231
  109.9 1.9 %shard_map.51 = bf16[64,2048]{1,0:T(8,128)(2,1)} custom-call(s32[2,16,128]{2,1,0:T(8,128)S(1)} %get-tuple-element.7.place_ref, f32[4,2,2,64,128]{4,3,2,1,0:T(8,128)S(1)} %all_to_all.21.sums_ref, bf16[64,2048]{1,0:T(8,128)(2,1)S(1)} %bitcast.16), custom_call_target="tpu_custom_call" | custom-call | flops 67108864 | bytes 2097152 | tf_op jit(solution)/shard_map/pallas_call | solution.py:179
  (12 shorter events, 0.1 us)
Async XLA Ops:
  0.0 0.9 copy-start.3
  1.0 0.7 copy-start.5
  13.9 11.7 %copy-start = (bf16[512,1024]{1,0:T(8,128)(2,1)S(1)}, bf16[512,1024]{1,0:T(8,128)(2,1)}, u32[]{:S(2)}) copy-start(bf16[512,1024]{1,0:T(8,128)(2,1)} %refs_0_.1) | copy-start | bytes 3145732
  13.9 56.7 %all-to-all-start.1 = ((bf16[16,32,1152]{2,1,0:T(8,128)(2,1)}), bf16[16,32,1152]{2,1,0:T(8,128)(2,1)}, u32[]{:S(2)}, u32[]{:S(2)}) async-start(bf16[16,32,1152]{2,1,0:T(8,128)(2,1)} %bitcast.1), calls=%async_computation.1 | async-start | bytes 2359296 | tf_op jit(solution)/shard_map/all_to_all | solution.py:198
  25.6 36.9 %collective-permute-start.1 = (bf16[512,1024]{1,0:T(8,128)(2,1)S(1)}, bf16[512,1024]{1,0:T(8,128)(2,1)S(1)}, u32[]{:S(2)}, u32[]{:S(2)}) collective-permute-start(bf16[512,1024]{1,0:T(8,128)(2,1)S(1)} %copy-done), channel_id=1, source_target_pairs={{0,4},{4,0},{1,5},{5,1},{2,6},{6,2},{3,7},{7,3},{8,12},{12,8},{9,1... | collective-permute-start | bytes 3145736 | tf_op jit(solution)/shard_map/ppermute | solution.py:202
  28.8 38.6 %collective-permute-start.2 = (bf16[512,1024]{1,0:T(8,128)(2,1)S(1)}, bf16[512,1024]{1,0:T(8,128)(2,1)S(1)}, u32[]{:S(2)}, u32[]{:S(2)}) collective-permute-start(bf16[512,1024]{1,0:T(8,128)(2,1)S(1)} %copy-done), channel_id=1, source_target_pairs={{0,32},{32,0},{1,33},{33,1},{2,34},{34,2},{3,35},{35,3},{4,36},{36... | collective-permute-start | bytes 3145736 | tf_op jit(solution)/shard_map/ppermute | solution.py:203
  62.5 7.2 %collective-permute-start.3 = (bf16[512,1024]{1,0:T(8,128)(2,1)S(1)}, bf16[512,1024]{1,0:T(8,128)(2,1)S(1)}, u32[]{:S(2)}, u32[]{:S(2)}) collective-permute-start(bf16[512,1024]{1,0:T(8,128)(2,1)S(1)} %collective-permute-done.1.refs_1_), channel_id=1, source_target_pairs={{0,32},{32,0},{1,33},{33,1},{2,34},{34,2},{3,35},{35,3},{4,36},{36... | collective-permute-start | bytes 3145736 | tf_op jit(solution)/shard_map/ppermute | solution.py:204
  69.6 1.0 copy-start.1
  70.6 1.2 %copy-start.2 = (bf16[512,1024]{1,0:T(8,128)(2,1)S(1)}, bf16[512,1024]{1,0:T(8,128)(2,1)}, u32[]{:S(2)}) copy-start(bf16[512,1024]{1,0:T(8,128)(2,1)} %copy-done.1) | copy-start | bytes 3145732
  77.1 21.4 %all-to-all-start.2 = ((f16[16,64,256]{2,1,0:T(8,128)(2,1)}), f16[16,64,256]{2,1,0:T(8,128)(2,1)S(1)}, u32[]{:S(2)}, u32[]{:S(2)}) async-start(f16[16,64,256]{2,1,0:T(8,128)(2,1)} %bitcast.5), calls=%async_computation.2 | async-start | bytes 1048576 | tf_op jit(solution)/shard_map/all_to_all | solution.py:222
  84.5 3.1 %collective-permute-start = (bf16[8,8,128]{2,1,0:T(8,128)(2,1)S(1)}, bf16[8,8,128]{2,1,0:T(8,128)(2,1)S(1)}, u32[]{:S(2)}, u32[]{:S(2)}) collective-permute-start(bf16[8,8,128]{2,1,0:T(8,128)(2,1)S(1)} %get-tuple-element.10), channel_id=1, source_target_pairs={{0,32},{32,0},{1,33},{33,1},{2,34},{34,2},{3,35},{35,3},{4,36},{36... | collective-permute-start | bytes 49160 | tf_op jit(solution)/shard_map/ppermute | solution.py:226
  98.5 11.4 %copy-start.4 = (bf16[1,2048,64]{1,2,0:T(8,128)(2,1)S(1)}, bf16[1,2048,64]{1,2,0:T(8,128)(2,1)}, u32[]{:S(2)}) copy-start(bf16[1,2048,64]{1,2,0:T(8,128)(2,1)} %param.7) | copy-start | bytes 786436

commit v5 on v4

--- a/solution.py
+++ b/solution.py
@@ -84,25 +84,27 @@
             out_ref[b, z, :, KD:] = info.astype(bf16)
 
 
-def ladder_kernel(got_ref, *refs):
-    pieces, out_ref, buffers, sems = refs[:4], refs[4], refs[5:9], refs[9]
-    copies = [pltpu.make_async_copy(pieces[n], buffers[n], sems.at[n]) for n in range(4)]
+def ladder_kernel(own_ref, pair_ref, got_far, across_far, across_pair_far, out_ref, *scratch):
+    got_ref, across_ref, across_pair_ref, sems = scratch
+    far = ((got_far, got_ref), (across_far, across_ref), (across_pair_far, across_pair_ref))
+    copies = [pltpu.make_async_copy(*two, sems.at[n]) for n, two in enumerate(far)]
     for copy in copies:
         copy.start()
     own, pair = lax.axis_index("k"), lax.axis_index("b")
+    dims = (((1,), (1,)), ((), ()))
+    copies[0].wait()
     rows = [
         jnp.concatenate([got_ref[half, z, :, :KD] for z in range(Z)], axis=0)
         for half in (pair, 1 - pair)
     ]
-    dims = (((1,), (1,)), ((), ()))
-    for side in range(2):
-        part = jnp.zeros((512, Z * SHARE), f32)
-        for h in range(2):
-            copies[2 * side + h].wait()
-            part += lax.dot_general(
-                buffers[2 * side + h][...], rows[h], dims, preferred_element_type=f32
-            )
-        out_ref[own if side == 0 else 1 - own] = part
+
+    def part(piece, half):
+        return lax.dot_general(piece[...], half, dims, preferred_element_type=f32)
+
+    out_ref[own] = part(own_ref, rows[0]) + part(pair_ref, rows[1])
+    copies[1].wait()
+    copies[2].wait()
+    out_ref[1 - own] = part(across_ref, rows[0]) + part(across_pair_ref, rows[1])
 
 
 def plan_kernel(info_ref, place_ref, route_ref):
@@ -184,7 +186,7 @@
         in_specs=[VMEM] * (len(args) - far) + [HBM] * far,
         out_specs=[VMEM] * len(shape) if isinstance(shape, list) else VMEM,
         scratch_shapes=scratch,
-        compiler_params=pltpu.CompilerParams(vmem_limit_bytes=limit * MIB),
+        compiler_params=pltpu.CompilerParams(vmem_limit_bytes=limit and limit * MIB),
         cost_estimate=pl.CostEstimate(flops=flops, bytes_accessed=2**21, transcendentals=0),
     )(*args)
 
@@ -192,7 +194,7 @@
 def step(amplitudes, pair_irrep, integrals, residual_in):
     swap = [(0, 1), (1, 0)]
 
-    packed = call(pack_kernel, (LAYERS, SEND, KD), bf16, pair_irrep, amplitudes[0], flops=2**26)
+    packed = call(pack_kernel, (LAYERS, SEND, KD), bf16, pair_irrep, amplitudes[0], limit=None, flops=2**26)
     got = lax.all_to_all(packed, "rep", 0, 0, tiled=True)
     shared = call(share_kernel, (2, Z, SHARE, KD + T), bf16, got, flops=2**26)
     gathered = lax.all_to_all(
@@ -207,14 +209,19 @@
         ladder_kernel,
         (2, 512, Z * SHARE),
         f32,
-        gathered,
         integrals,
         other,
+        gathered,
         across,
         across_other,
-        far=4,
-        scratch=[pltpu.VMEM((512, KD), bf16)] * 4 + [pltpu.SemaphoreType.DMA((4,))],
-        limit=48,
+        far=3,
+        scratch=[
+            pltpu.VMEM((2, Z, SHARE, KD + T), bf16),
+            pltpu.VMEM((512, KD), bf16),
+            pltpu.VMEM((512, KD), bf16),
+            pltpu.SemaphoreType.DMA((3,)),
+        ],
+        limit=49,
         flops=2**30,
     )
 

time: 113 us -> 111 us (0.982)
  local copies, waits for them, and re-layouts: 4.54 us -> 0.73 us
  Pallas kernels: 8.55 us -> 9.7 us
    unnamed x12 -> x4, local copies, waits for them, and re-layouts: 3.82 us -> 0.01 us
    pallas_call x6, Pallas kernels: 8.55 us -> 9.7 us  [call(): pl.pallas_call(kernel, out_shape=[jax.ShapeDtypeStruct(one, dtype) for on...]
where the time goes in v5:
time: 111 us; the launch traced here: 110 us
  waiting for transfers between devices  43.1 us (39%)
  starting transfers between devices  33.3 us (30%)
  blocking collectives  21.7 us (20%)
  Pallas kernels  9.7 us (9%)
    ppermute x1, waiting for transfers between devices, step(): other = lax.ppermute(integrals, 'b', swap)  28.8 us
    all_to_all x1, starting transfers between devices, step(): lax.all_to_all(shared.reshape(2 * Z, SHARE, KD + T), ('b', 'z'), 0, 0, ti...  11.7 us
    all_to_all x1, blocking collectives, step(): owned = lax.all_to_all(routed, 'rep', 0, 0, tiled=True)  11 us
    all_to_all x1, waiting for transfers between devices, step(): parts = lax.all_to_all(sent, ('k', 'g', 'b'), 0, 0, tiled=True)  10.8 us
    all_to_all x1, blocking collectives, step(): got = lax.all_to_all(packed, 'rep', 0, 0, tiled=True)  10.7 us
    pallas_call x6, Pallas kernels, call(): pl.pallas_call(kernel, out_shape=[jax.ShapeDtypeStruct(one, dtype) for on...  9.7 us
    all_to_all x1, starting transfers between devices, step(): parts = lax.all_to_all(sent, ('k', 'g', 'b'), 0, 0, tiled=True)  6.66 us
    ppermute x1, starting transfers between devices, step(): across_other = lax.ppermute(other, 'k', swap)  4.9 us
  transfers between devices with their start and end apart: 6, of which 4 were waited for; matrix products, arithmetic and copies ran while one was open for 1% of the time, Pallas kernels for 0%

profile of v5, /device:TPU:1, one launch (start us, length us, event | category | flops | bytes accessed | tf_op | source)
XLA Modules:
  0.0 109.5 jit_solution(6082062331739383129)
XLA Ops:
  0.0 2.1 %shard_map.46 = bf16[4,40,1024]{2,1,0:T(8,128)(2,1)} custom-call(s32[1,128]{1,0:T(1,128)} %labels_ref.1, bf16[128,1024]{1,0:T(8,128)(2,1)} %bitcast.17), custom_call_target="tpu_custom_call" | custom-call | flops 67108864 | bytes 2097152 | tf_op jit(solution)/shard_map/pallas_call | solution.py:181
  2.1 10.7 %all_to_all.20.got_ref = bf16[4,40,1024]{2,1,0:T(8,128)(2,1)S(1)} all-to-all(bf16[4,40,1024]{2,1,0:T(8,128)(2,1)} %shard_map.46), channel_id=1, replica_groups=mesh['z'=8,'k'=2,'g'=4,'b'=2,'rep'=4] {'rep'}, dimensions={0} | all-to-all | bytes 655360 | tf_op jit(solution)/shard_map/all_to_all | solution.py:198
  12.8 1.4 %shard_map.47 = bf16[2,8,32,1152]{3,2,1,0:T(8,128)(2,1)} custom-call(bf16[4,40,1024]{2,1,0:T(8,128)(2,1)S(1)} %all_to_all.20.got_ref), custom_call_target="tpu_custom_call" | custom-call | flops 67108864 | bytes 2097152 | tf_op jit(solution)/shard_map/pallas_call | solution.py:181
  14.2 11.7 %all-to-all-start.1 = ((bf16[16,32,1152]{2,1,0:T(8,128)(2,1)}), bf16[16,32,1152]{2,1,0:T(8,128)(2,1)}, u32[]{:S(2)}, u32[]{:S(2)}) async-start(bf16[16,32,1152]{2,1,0:T(8,128)(2,1)} %bitcast.1), calls=%async_computation.1 | async-start | bytes 2359296 | tf_op jit(solution)/shard_map/all_to_all | solution.py:200
  25.8 0.0 copy-done
  25.8 3.2 %collective-permute-start.1 = (bf16[512,1024]{1,0:T(8,128)(2,1)S(1)}, bf16[512,1024]{1,0:T(8,128)(2,1)S(1)}, u32[]{:S(2)}, u32[]{:S(2)}) collective-permute-start(bf16[512,1024]{1,0:T(8,128)(2,1)S(1)} %copy-done), channel_id=1, source_target_pairs={{0,4},{4,0},{1,5},{5,1},{2,6},{6,2},{3,7},{7,3},{8,12},{12,8},{9,1... | collective-permute-start | bytes 3145736 | tf_op jit(solution)/shard_map/ppermute | solution.py:204
  29.1 4.9 %collective-permute-start.2 = (bf16[512,1024]{1,0:T(8,128)(2,1)S(1)}, bf16[512,1024]{1,0:T(8,128)(2,1)S(1)}, u32[]{:S(2)}, u32[]{:S(2)}) collective-permute-start(bf16[512,1024]{1,0:T(8,128)(2,1)S(1)} %copy-done), channel_id=1, source_target_pairs={{0,32},{32,0},{1,33},{33,1},{2,34},{34,2},{3,35},{35,3},{4,36},{36... | collective-permute-start | bytes 3145736 | tf_op jit(solution)/shard_map/ppermute | solution.py:205
  34.0 28.8 %collective-permute-done.1.pair_ref = bf16[512,1024]{1,0:T(8,128)(2,1)S(1)} collective-permute-done((bf16[512,1024]{1,0:T(8,128)(2,1)S(1)}, bf16[512,1024]{1,0:T(8,128)(2,1)S(1)}, u32[]{:S(2)}, u32[]{:S(2)}) %collective-permute-start.1) | collective-permute-done | bytes 1048608 | tf_op jit(solution)/shard_map/ppermute | solution.py:204
  62.7 4.9 %collective-permute-start.3 = (bf16[512,1024]{1,0:T(8,128)(2,1)S(1)}, bf16[512,1024]{1,0:T(8,128)(2,1)}, u32[]{:S(2)}, u32[]{:S(2)}) collective-permute-start(bf16[512,1024]{1,0:T(8,128)(2,1)S(1)} %collective-permute-done.1.pair_ref), channel_id=1, source_target_pairs={{0,32},{32,0},{1,33},{33,1},{2,34},{34,2},{3,35},{35,3},{4,36},{36... | collective-permute-start | bytes 3145736 | tf_op jit(solution)/shard_map/ppermute | solution.py:206
  67.6 0.0 collective-permute-done.2.across_far
  67.7 2.4 %collective-permute-done.3.across_pair_far = bf16[512,1024]{1,0:T(8,128)(2,1)} collective-permute-done((bf16[512,1024]{1,0:T(8,128)(2,1)S(1)}, bf16[512,1024]{1,0:T(8,128)(2,1)}, u32[]{:S(2)}, u32[]{:S(2)}) %collective-permute-start.3) | collective-permute-done | bytes 1048608 | tf_op jit(solution)/shard_map/ppermute | solution.py:206
  70.0 0.0 all-to-all-done.1
  70.0 3.8 %shard_map.49 = f32[2,512,256]{2,1,0:T(8,128)S(1)} custom-call(bf16[512,1024]{1,0:T(8,128)(2,1)S(1)} %copy-done, bf16[512,1024]{1,0:T(8,128)(2,1)S(1)} %collective-permute-done.1.pair_ref, bf16[2,8,32,1152]{3,2,1,0:T(8,128)(2,1)} %bitcast.2.got_far, bf16[512,1024]{1,0:T(8,128)(2,1)S(1)} %collective-permute-done.2.across_far, ...), custom_call_target="tpu_custom_call" | custom-call | flops 1073741824 | bytes 2097152 | tf_op jit(solution)/shard_map/pallas_call | solution.py:181
  73.9 0.9 convert_element_type.9
  74.8 6.7 %all-to-all-start.2 = ((f16[16,64,256]{2,1,0:T(8,128)(2,1)}), f16[16,64,256]{2,1,0:T(8,128)(2,1)S(1)}, u32[]{:S(2)}, u32[]{:S(2)}) async-start(f16[16,64,256]{2,1,0:T(8,128)(2,1)} %bitcast.5), calls=%async_computation.2 | async-start | bytes 1048576 | tf_op jit(solution)/shard_map/all_to_all | solution.py:229
  81.4 0.7 fusion
  82.2 2.0 %collective-permute-start = (bf16[8,8,128]{2,1,0:T(8,128)(2,1)S(1)}, bf16[8,8,128]{2,1,0:T(8,128)(2,1)S(1)}, u32[]{:S(2)}, u32[]{:S(2)}) collective-permute-start(bf16[8,8,128]{2,1,0:T(8,128)(2,1)S(1)} %get-tuple-element.10), channel_id=1, source_target_pairs={{0,32},{32,0},{1,33},{33,1},{2,34},{34,2},{3,35},{35,3},{4,36},{36... | collective-permute-start | bytes 49160 | tf_op jit(solution)/shard_map/ppermute | solution.py:233
  84.2 1.1 collective-permute-done
  85.2 0.1 shard_map.48
  85.4 10.8 %all-to-all-done.2 = f16[16,64,256]{2,1,0:T(8,128)(2,1)S(1)} async-done(((f16[16,64,256]{2,1,0:T(8,128)(2,1)}), f16[16,64,256]{2,1,0:T(8,128)(2,1)S(1)}, u32[]{:S(2)}, u32[]{:S(2)}) %all-to-all-start.2) | async-done | bytes 524320 | tf_op jit(solution)/shard_map/all_to_all | solution.py:229
  96.2 0.1 convert_reduce_fusion.sums_ref
  96.3 0.4 shard_map.50
  96.7 11.0 %all_to_all.21.sums_ref = f32[4,2,2,64,128]{4,3,2,1,0:T(8,128)S(1)} all-to-all(f32[4,2,2,64,128]{4,3,2,1,0:T(8,128)S(1)} %shard_map.50), channel_id=1, replica_groups=mesh['z'=8,'k'=2,'g'=4,'b'=2,'rep'=4] {'rep'}, dimensions={0} | all-to-all | bytes 1048576 | tf_op jit(solution)/shard_map/all_to_all | solution.py:238
  107.6 1.9 %shard_map.51 = bf16[64,2048]{1,0:T(8,128)(2,1)} custom-call(s32[2,16,128]{2,1,0:T(8,128)S(1)} %get-tuple-element.7.place_ref, f32[4,2,2,64,128]{4,3,2,1,0:T(8,128)S(1)} %all_to_all.21.sums_ref, bf16[64,2048]{1,0:T(8,128)(2,1)S(1)} %bitcast.15), custom_call_target="tpu_custom_call" | custom-call | flops 67108864 | bytes 2097152 | tf_op jit(solution)/shard_map/pallas_call | solution.py:181
  (4 shorter events, 0.0 us)
Async XLA Ops:
  14.2 11.7 %copy-start = (bf16[512,1024]{1,0:T(8,128)(2,1)S(1)}, bf16[512,1024]{1,0:T(8,128)(2,1)}, u32[]{:S(2)}) copy-start(bf16[512,1024]{1,0:T(8,128)(2,1)} %own_ref.1) | copy-start | bytes 3145732
  14.2 55.9 %all-to-all-start.1 = ((bf16[16,32,1152]{2,1,0:T(8,128)(2,1)}), bf16[16,32,1152]{2,1,0:T(8,128)(2,1)}, u32[]{:S(2)}, u32[]{:S(2)}) async-start(bf16[16,32,1152]{2,1,0:T(8,128)(2,1)} %bitcast.1), calls=%async_computation.1 | async-start | bytes 2359296 | tf_op jit(solution)/shard_map/all_to_all | solution.py:200
  25.8 36.9 %collective-permute-start.1 = (bf16[512,1024]{1,0:T(8,128)(2,1)S(1)}, bf16[512,1024]{1,0:T(8,128)(2,1)S(1)}, u32[]{:S(2)}, u32[]{:S(2)}) collective-permute-start(bf16[512,1024]{1,0:T(8,128)(2,1)S(1)} %copy-done), channel_id=1, source_target_pairs={{0,4},{4,0},{1,5},{5,1},{2,6},{6,2},{3,7},{7,3},{8,12},{12,8},{9,1... | collective-permute-start | bytes 3145736 | tf_op jit(solution)/shard_map/ppermute | solution.py:204
  29.1 38.6 %collective-permute-start.2 = (bf16[512,1024]{1,0:T(8,128)(2,1)S(1)}, bf16[512,1024]{1,0:T(8,128)(2,1)S(1)}, u32[]{:S(2)}, u32[]{:S(2)}) collective-permute-start(bf16[512,1024]{1,0:T(8,128)(2,1)S(1)} %copy-done), channel_id=1, source_target_pairs={{0,32},{32,0},{1,33},{33,1},{2,34},{34,2},{3,35},{35,3},{4,36},{36... | collective-permute-start | bytes 3145736 | tf_op jit(solution)/shard_map/ppermute | solution.py:205
  62.7 7.3 %collective-permute-start.3 = (bf16[512,1024]{1,0:T(8,128)(2,1)S(1)}, bf16[512,1024]{1,0:T(8,128)(2,1)}, u32[]{:S(2)}, u32[]{:S(2)}) collective-permute-start(bf16[512,1024]{1,0:T(8,128)(2,1)S(1)} %collective-permute-done.1.pair_ref), channel_id=1, source_target_pairs={{0,32},{32,0},{1,33},{33,1},{2,34},{34,2},{3,35},{35,3},{4,36},{36... | collective-permute-start | bytes 3145736 | tf_op jit(solution)/shard_map/ppermute | solution.py:206
  74.8 21.4 %all-to-all-start.2 = ((f16[16,64,256]{2,1,0:T(8,128)(2,1)}), f16[16,64,256]{2,1,0:T(8,128)(2,1)S(1)}, u32[]{:S(2)}, u32[]{:S(2)}) async-start(f16[16,64,256]{2,1,0:T(8,128)(2,1)} %bitcast.5), calls=%async_computation.2 | async-start | bytes 1048576 | tf_op jit(solution)/shard_map/all_to_all | solution.py:229
  82.2 3.1 %collective-permute-start = (bf16[8,8,128]{2,1,0:T(8,128)(2,1)S(1)}, bf16[8,8,128]{2,1,0:T(8,128)(2,1)S(1)}, u32[]{:S(2)}, u32[]{:S(2)}) collective-permute-start(bf16[8,8,128]{2,1,0:T(8,128)(2,1)S(1)} %get-tuple-element.10), channel_id=1, source_target_pairs={{0,32},{32,0},{1,33},{33,1},{2,34},{34,2},{3,35},{35,3},{4,36},{36... | collective-permute-start | bytes 49160 | tf_op jit(solution)/shard_map/ppermute | solution.py:233
  96.2 11.4 %copy-start.1 = (bf16[1,2048,64]{1,2,0:T(8,128)(2,1)S(1)}, bf16[1,2048,64]{1,2,0:T(8,128)(2,1)}, u32[]{:S(2)}) copy-start(bf16[1,2048,64]{1,2,0:T(8,128)(2,1)} %param.7) | copy-start | bytes 786436

commit v6 on v5

--- a/solution.py
+++ b/solution.py
@@ -59,15 +59,16 @@
     return parts
 
 
-def share_kernel(got_ref, out_ref):
+def share_kernel(got_ref, out_ref, info_ref):
     rep = lax.axis_index("rep")
     counts = [got_ref[l, SEND - 1 : SEND, T : 2 * T].astype(f32).astype(i32) for l in range(LAYERS)]
-    row = iota((SHARE, T), 0)
-    info = jnp.zeros((SHARE, T), f32)
+    row = iota((8, T), 0)
+    info = jnp.zeros((8, T), f32)
     for l in range(LAYERS):
         mine = got_ref[l, SEND - 1 : SEND, :T].astype(f32)
         info = jnp.where((row == 0) & (rep == l), mine, info)
         info = jnp.where(row == 1 + l, counts[l].astype(f32), info)
+    info_ref[0] = info.astype(bf16)
     s = iota((SHARE, SEND), 0)
     slot = iota((SHARE, SEND), 1)
     for b in range(2):
@@ -80,39 +81,35 @@
             hot = (inside & (slot == want)).astype(f32).astype(bf16)
             total += jnp.dot(hot, got_ref[l], preferred_element_type=f32)
         for z in range(Z):
-            out_ref[b, z, :, :KD] = total.astype(bf16)
-            out_ref[b, z, :, KD:] = info.astype(bf16)
-
-
-def ladder_kernel(own_ref, pair_ref, got_far, across_far, across_pair_far, out_ref, *scratch):
-    got_ref, across_ref, across_pair_ref, sems = scratch
-    far = ((got_far, got_ref), (across_far, across_ref), (across_pair_far, across_pair_ref))
-    copies = [pltpu.make_async_copy(*two, sems.at[n]) for n, two in enumerate(far)]
+            out_ref[b, z] = total.astype(bf16)
+
+
+def ladder_kernel(own_ref, pair_ref, got_ref, across_far, across_pair_far, out_ref, *scratch):
+    across_ref, across_pair_ref, sems = scratch
+    own, pair = lax.axis_index("k"), lax.axis_index("b")
+    moves = ((across_far, across_ref), (across_pair_far, across_pair_ref))
+    copies = [pltpu.make_async_copy(*move, sems.at[n]) for n, move in enumerate(moves)]
     for copy in copies:
         copy.start()
-    own, pair = lax.axis_index("k"), lax.axis_index("b")
-    dims = (((1,), (1,)), ((), ()))
+
+    def part(piece, half):
+        dims = (((1,), (1,)), ((), ()))
+        return lax.dot_general(piece[...], got_ref[half], dims, preferred_element_type=f32)
+
+    out_ref[own] = part(own_ref, pair) + part(pair_ref, 1 - pair)
     copies[0].wait()
-    rows = [
-        jnp.concatenate([got_ref[half, z, :, :KD] for z in range(Z)], axis=0)
-        for half in (pair, 1 - pair)
-    ]
-
-    def part(piece, half):
-        return lax.dot_general(piece[...], half, dims, preferred_element_type=f32)
-
-    out_ref[own] = part(own_ref, rows[0]) + part(pair_ref, rows[1])
+    far = part(across_ref, pair)
     copies[1].wait()
-    copies[2].wait()
-    out_ref[1 - own] = part(across_ref, rows[0]) + part(across_pair_ref, rows[1])
+    out_ref[1 - own] = far + part(across_pair_ref, 1 - pair)
 
 
 def plan_kernel(info_ref, place_ref, route_ref):
-    rep, own = lax.axis_index("rep"), lax.axis_index("k")
+    rep, own, here = lax.axis_index("rep"), lax.axis_index("k"), lax.axis_index("z")
 
     def of(r):
+        entries = [here ^ z for z in range(Z)]
         at_core = [
-            jnp.concatenate([info_ref[s, z, r : r + 1, :].astype(f32) for z in range(Z)], axis=0)
+            jnp.concatenate([info_ref[s, e, r : r + 1, :].astype(f32) for e in entries], axis=0)
             for s in range(2)
         ]
         first = jnp.where(own == 0, at_core[0], at_core[1])
@@ -196,10 +193,12 @@
 
     packed = call(pack_kernel, (LAYERS, SEND, KD), bf16, pair_irrep, amplitudes[0], limit=None, flops=2**26)
     got = lax.all_to_all(packed, "rep", 0, 0, tiled=True)
-    shared = call(share_kernel, (2, Z, SHARE, KD + T), bf16, got, flops=2**26)
+    shared, info = call(share_kernel, [(2, Z, SHARE, KD), (1, 8, T)], bf16, got, flops=2**26)
     gathered = lax.all_to_all(
-        shared.reshape(2 * Z, SHARE, KD + T), ("b", "z"), 0, 0, tiled=True
-    ).reshape(2, Z, SHARE, KD + T)
+        shared.reshape(2 * Z, SHARE, KD), ("b", "z"), 0, 0, tiled=True
+    ).reshape(2, Z * SHARE, KD)
+    for step in (1, 2, 4):
+        info = jnp.concatenate([info, lax.ppermute(info, "z", [(z, z ^ step) for z in range(Z)])])
 
     other = lax.ppermute(integrals, "b", swap)
     across = lax.ppermute(integrals, "k", swap)
@@ -214,12 +213,11 @@
         gathered,
         across,
         across_other,
-        far=3,
+        far=2,
         scratch=[
-            pltpu.VMEM((2, Z, SHARE, KD + T), bf16),
             pltpu.VMEM((512, KD), bf16),
             pltpu.VMEM((512, KD), bf16),
-            pltpu.SemaphoreType.DMA((3,)),
+            pltpu.SemaphoreType.DMA((2,)),
         ],
         limit=49,
         flops=2**30,
@@ -229,7 +227,6 @@
     parts = lax.all_to_all(sent, ("k", "g", "b"), 0, 0, tiled=True)
     sums = jnp.sum(parts.reshape(2, 4, 2, 64, Z * SHARE).astype(f32), axis=1)
 
-    info = gathered[0, :, :8, KD:]
     info_across = lax.ppermute(info, "k", swap)
     place, route = call(
         plan_kernel, [(2, 2 * Z, T), (16, T)], i32, jnp.stack([info, info_across]), flops=2**20

time: 111 us -> 108 us (0.973)
  starting transfers between devices: 33.3 us -> 58 us
  waiting for transfers between devices: 43.1 us -> 23.5 us
  blocking collectives: 21.7 us -> 12.8 us
    ppermute x1, waiting for transfers between devices: 28.8 us -> 0.01 us  [step(): other = lax.ppermute(integrals, 'b', swap)]
    all_to_all x1, waiting for transfers between devices: 10.8 us -> 0.01 us  [step(): parts = lax.all_to_all(sent, ('k', 'g', 'b'), 0, 0, tiled=True)]
    all_to_all x1 -> x2, waiting for transfers between devices: 0.01 us -> 10.7 us  [the longest x1 8.05 us: step(): lax.all_to_all(shared.reshape(2 * Z, SHARE, KD), ('b', 'z'), 0, 0, tiled=...]
    all_to_all x1 -> x0, blocking collectives: 10.7 us -> none  [step(): got = lax.all_to_all(packed, 'rep', 0, 0, tiled=True)]
    ppermute x0 -> x3, waiting for transfers between devices: none -> 10.6 us  [step(): lax.ppermute(info, 'z', [(z, z ^ step) for z in range(Z)])]
    ppermute x0 -> x3, starting transfers between devices: none -> 7.83 us  [step(): lax.ppermute(info, 'z', [(z, z ^ step) for z in range(Z)])]
    ppermute x1, starting transfers between devices: 4.9 us -> 11.9 us  [step(): across_other = lax.ppermute(other, 'k', swap)]
    all_to_all x1 -> x2, starting transfers between devices: 11.7 us -> 16.3 us  [the longest x1 11.5 us: step(): lax.all_to_all(shared.reshape(2 * Z, SHARE, KD), ('b', 'z'), 0, 0, tiled=...]
  transfers between devices with their start and end apart: 6 -> 10, of which waited for: 4 -> 7; matrix products, arithmetic and copies ran while one was open for 1% -> 0% of each run, Pallas kernels for 0% -> 1%
where the time goes in v6:
time: 108 us; the launch traced here: 106 us
  starting transfers between devices  58 us (54%)
  waiting for transfers between devices  23.5 us (22%)
  blocking collectives  12.8 us (12%)
  Pallas kernels  9.77 us (9%)
    all_to_all x1, blocking collectives, step(): owned = lax.all_to_all(routed, 'rep', 0, 0, tiled=True)  12.8 us
    ppermute x1, starting transfers between devices, step(): across_other = lax.ppermute(other, 'k', swap)  11.9 us
    all_to_all x1, starting transfers between devices, step(): lax.all_to_all(shared.reshape(2 * Z, SHARE, KD), ('b', 'z'), 0, 0, tiled=...  11.5 us
    ppermute x3, waiting for transfers between devices, step(): lax.ppermute(info, 'z', [(z, z ^ step) for z in range(Z)])  10.6 us
    pallas_call x6, Pallas kernels, call(): pl.pallas_call(kernel, out_shape=[jax.ShapeDtypeStruct(one, dtype) for on...  9.77 us
    all_to_all x1, starting transfers between devices, step(): parts = lax.all_to_all(sent, ('k', 'g', 'b'), 0, 0, tiled=True)  9.62 us
    all_to_all x1, waiting for transfers between devices, step(): lax.all_to_all(shared.reshape(2 * Z, SHARE, KD), ('b', 'z'), 0, 0, tiled=...  8.05 us
    ppermute x3, starting transfers between devices, step(): lax.ppermute(info, 'z', [(z, z ^ step) for z in range(Z)])  7.83 us
  transfers between devices with their start and end apart: 10, of which 7 were waited for; matrix products, arithmetic and copies ran while one was open for 0% of the time, Pallas kernels for 1%

profile of v6, /device:TPU:1, one launch (start us, length us, event | category | flops | bytes accessed | tf_op | source)
XLA Modules:
  0.0 106.3 jit_solution(4199568188901613654)
XLA Ops:
  0.0 2.2 %shard_map.46 = bf16[4,40,1024]{2,1,0:T(8,128)(2,1)} custom-call(s32[1,128]{1,0:T(1,128)} %labels_ref.1, bf16[128,1024]{1,0:T(8,128)(2,1)} %bitcast.17), custom_call_target="tpu_custom_call" | custom-call | flops 67108864 | bytes 2097152 | tf_op jit(solution)/shard_map/pallas_call | solution.py:178
  2.2 4.8 %all-to-all-start = ((bf16[4,40,1024]{2,1,0:T(8,128)(2,1)}), bf16[4,40,1024]{2,1,0:T(8,128)(2,1)S(1)}, u32[]{:S(2)}, u32[]{:S(2)}) async-start(bf16[4,40,1024]{2,1,0:T(8,128)(2,1)} %shard_map.46), calls=%async_computation | async-start | bytes 655360 | tf_op jit(solution)/shard_map/all_to_all | solution.py:195
  7.0 3.2 %collective-permute-start.4 = (bf16[512,1024]{1,0:T(8,128)(2,1)S(1)}, bf16[512,1024]{1,0:T(8,128)(2,1)S(1)}, u32[]{:S(2)}, u32[]{:S(2)}) collective-permute-start(bf16[512,1024]{1,0:T(8,128)(2,1)S(1)} %copy-done), channel_id=1, source_target_pairs={{0,4},{4,0},{1,5},{5,1},{2,6},{6,2},{3,7},{7,3},{8,12},{12,8},{9,1... | collective-permute-start | bytes 3145736 | tf_op jit(solution)/shard_map/ppermute | solution.py:203
  10.2 2.7 %all-to-all-done.got_ref = bf16[4,40,1024]{2,1,0:T(8,128)(2,1)S(1)} async-done(((bf16[4,40,1024]{2,1,0:T(8,128)(2,1)}), bf16[4,40,1024]{2,1,0:T(8,128)(2,1)S(1)}, u32[]{:S(2)}, u32[]{:S(2)}) %all-to-all-start) | async-done | bytes 327712 | tf_op jit(solution)/shard_map/all_to_all | solution.py:195
  12.9 1.3 %shard_map.47 = (bf16[2,8,32,1024]{3,2,1,0:T(8,128)(2,1)}, bf16[1,8,128]{2,1,0:T(8,128)(2,1)S(1)}) custom-call(bf16[4,40,1024]{2,1,0:T(8,128)(2,1)S(1)} %all-to-all-done.got_ref), custom_call_target="tpu_custom_call" | custom-call | flops 67108864 | bytes 2097152 | tf_op jit(solution)/shard_map/pallas_call | solution.py:178
  14.2 11.5 %all-to-all-start.1 = ((bf16[16,32,1024]{2,1,0:T(8,128)(2,1)}), bf16[16,32,1024]{2,1,0:T(8,128)(2,1)S(1)}, u32[]{:S(2)}, u32[]{:S(2)}) async-start(bf16[16,32,1024]{2,1,0:T(8,128)(2,1)} %bitcast.3), calls=%async_computation.1 | async-start | bytes 2097152 | tf_op jit(solution)/shard_map/all_to_all | solution.py:197
  25.7 4.3 %collective-permute-start.5 = (bf16[512,1024]{1,0:T(8,128)(2,1)S(1)}, bf16[512,1024]{1,0:T(8,128)(2,1)S(1)}, u32[]{:S(2)}, u32[]{:S(2)}) collective-permute-start(bf16[512,1024]{1,0:T(8,128)(2,1)S(1)} %copy-done), channel_id=1, source_target_pairs={{0,32},{32,0},{1,33},{33,1},{2,34},{34,2},{3,35},{35,3},{4,36},{36... | collective-permute-start | bytes 3145736 | tf_op jit(solution)/shard_map/ppermute | solution.py:204
  30.0 11.9 %collective-permute-start.6 = (bf16[512,1024]{1,0:T(8,128)(2,1)S(1)}, bf16[512,1024]{1,0:T(8,128)(2,1)}, u32[]{:S(2)}, u32[]{:S(2)}) collective-permute-start(bf16[512,1024]{1,0:T(8,128)(2,1)S(1)} %collective-permute-done.4.pair_ref), channel_id=1, source_target_pairs={{0,32},{32,0},{1,33},{33,1},{2,34},{34,2},{3,35},{35,3},{4,36},{36... | collective-permute-start | bytes 3145736 | tf_op jit(solution)/shard_map/ppermute | solution.py:205
  42.0 1.0 copy-done.2
  42.9 1.4 %collective-permute-done.6.across_pair_far = bf16[512,1024]{1,0:T(8,128)(2,1)} collective-permute-done((bf16[512,1024]{1,0:T(8,128)(2,1)S(1)}, bf16[512,1024]{1,0:T(8,128)(2,1)}, u32[]{:S(2)}, u32[]{:S(2)}) %collective-permute-start.6) | collective-permute-done | bytes 1048608 | tf_op jit(solution)/shard_map/ppermute | solution.py:205
  44.3 8.1 %all-to-all-done.1 = bf16[16,32,1024]{2,1,0:T(8,128)(2,1)S(1)} async-done(((bf16[16,32,1024]{2,1,0:T(8,128)(2,1)}), bf16[16,32,1024]{2,1,0:T(8,128)(2,1)S(1)}, u32[]{:S(2)}, u32[]{:S(2)}) %all-to-all-start.1) | async-done | bytes 1048608 | tf_op jit(solution)/shard_map/all_to_all | solution.py:197
  52.4 3.8 %shard_map.49 = f32[2,512,256]{2,1,0:T(8,128)S(1)} custom-call(bf16[512,1024]{1,0:T(8,128)(2,1)S(1)} %copy-done, bf16[512,1024]{1,0:T(8,128)(2,1)S(1)} %collective-permute-done.4.pair_ref, bf16[2,256,1024]{2,1,0:T(8,128)(2,1)S(1)} %bitcast.14, bf16[512,1024]{1,0:T(8,128)(2,1)} %copy-done.2, bf16[512,1024]{1,0:T(8,128)(2,1)} %collective-permute-done.6.across_pair_far), custom_call_target="tpu_custom_call" | custom-call | flops 1073741824 | bytes 2097152 | tf_op jit(solution)/shard_map/pallas_call | solution.py:178
  56.2 0.9 convert_element_type.9
  57.1 9.6 %all-to-all-start.2 = ((f16[16,64,256]{2,1,0:T(8,128)(2,1)}), f16[16,64,256]{2,1,0:T(8,128)(2,1)S(1)}, u32[]{:S(2)}, u32[]{:S(2)}) async-start(f16[16,64,256]{2,1,0:T(8,128)(2,1)} %bitcast.5), calls=%async_computation.2 | async-start | bytes 1048576 | tf_op jit(solution)/shard_map/all_to_all | solution.py:227
  66.7 2.8 %collective-permute-start = (bf16[1,8,128]{2,1,0:T(8,128)(2,1)S(1)}, bf16[1,8,128]{2,1,0:T(8,128)(2,1)S(1)}, u32[]{:S(2)}, u32[]{:S(2)}) collective-permute-start(bf16[1,8,128]{2,1,0:T(8,128)(2,1)S(1)} %get-tuple-element.9), channel_id=1, source_target_pairs={{0,64},{64,0},{128,192},{192,128},{256,320},{320,256},{384,448},{4... | collective-permute-start | bytes 6152 | tf_op jit(solution)/shard_map/ppermute | solution.py:201
  69.5 1.8 %collective-permute-done = bf16[1,8,128]{2,1,0:T(8,128)(2,1)S(1)} collective-permute-done((bf16[1,8,128]{2,1,0:T(8,128)(2,1)S(1)}, bf16[1,8,128]{2,1,0:T(8,128)(2,1)S(1)}, u32[]{:S(2)}, u32[]{:S(2)}) %collective-permute-start) | collective-permute-done | bytes 2080 | tf_op jit(solution)/shard_map/ppermute | solution.py:201
  71.4 1.9 %collective-permute-start.1 = (bf16[2,8,128]{2,1,0:T(8,128)(2,1)S(1)}, bf16[2,8,128]{2,1,0:T(8,128)(2,1)S(1)}, u32[]{:S(2)}, u32[]{:S(2)}) collective-permute-start(bf16[2,8,128]{2,1,0:T(8,128)(2,1)S(1)} %pad_maximum_fusion.2), channel_id=1, source_target_pairs={{0,128},{64,192},{128,0},{192,64},{256,384},{320,448},{384,256},{4... | collective-permute-start | bytes 12296 | tf_op jit(solution)/shard_map/ppermute | solution.py:201
  73.3 3.6 %collective-permute-done.1 = bf16[2,8,128]{2,1,0:T(8,128)(2,1)S(1)} collective-permute-done((bf16[2,8,128]{2,1,0:T(8,128)(2,1)S(1)}, bf16[2,8,128]{2,1,0:T(8,128)(2,1)S(1)}, u32[]{:S(2)}, u32[]{:S(2)}) %collective-permute-start.1) | collective-permute-done | bytes 4128 | tf_op jit(solution)/shard_map/ppermute | solution.py:201
  76.9 3.1 %collective-permute-start.2 = (bf16[4,8,128]{2,1,0:T(8,128)(2,1)S(1)}, bf16[4,8,128]{2,1,0:T(8,128)(2,1)S(1)}, u32[]{:S(2)}, u32[]{:S(2)}) collective-permute-start(bf16[4,8,128]{2,1,0:T(8,128)(2,1)S(1)} %pad_maximum_fusion.1), channel_id=1, source_target_pairs={{0,256},{64,320},{128,384},{192,448},{256,0},{320,64},{384,128},{4... | collective-permute-start | bytes 24584 | tf_op jit(solution)/shard_map/ppermute | solution.py:201
  80.1 5.1 %collective-permute-done.2 = bf16[4,8,128]{2,1,0:T(8,128)(2,1)S(1)} collective-permute-done((bf16[4,8,128]{2,1,0:T(8,128)(2,1)S(1)}, bf16[4,8,128]{2,1,0:T(8,128)(2,1)S(1)}, u32[]{:S(2)}, u32[]{:S(2)}) %collective-permute-start.2) | collective-permute-done | bytes 8224 | tf_op jit(solution)/shard_map/ppermute | solution.py:201
  85.2 4.9 %collective-permute-start.3 = (bf16[8,8,128]{2,1,0:T(8,128)(2,1)S(1)}, bf16[8,8,128]{2,1,0:T(8,128)(2,1)S(1)}, u32[]{:S(2)}, u32[]{:S(2)}) collective-permute-start(bf16[8,8,128]{2,1,0:T(8,128)(2,1)S(1)} %constant_dynamic-update-slice_fusion), channel_id=1, source_target_pairs={{0,32},{32,0},{1,33},{33,1},{2,34},{34,2},{3,35},{35,3},{4,36},{36... | collective-permute-start | bytes 49160 | tf_op jit(solution)/shard_map/ppermute | solution.py:230
  90.1 0.8 collective-permute-done.3
  91.5 12.8 %all_to_all.20.sums_ref = f32[4,2,2,64,128]{4,3,2,1,0:T(8,128)S(1)} all-to-all(f32[4,2,2,64,128]{4,3,2,1,0:T(8,128)S(1)} %shard_map.50), channel_id=1, replica_groups=mesh['z'=8,'k'=2,'g'=4,'b'=2,'rep'=4] {'rep'}, dimensions={0} | all-to-all | bytes 1048576 | tf_op jit(solution)/shard_map/all_to_all | solution.py:235
  104.3 1.9 %shard_map.51 = bf16[64,2048]{1,0:T(8,128)(2,1)} custom-call(s32[2,16,128]{2,1,0:T(8,128)S(1)} %get-tuple-element.10.place_ref, f32[4,2,2,64,128]{4,3,2,1,0:T(8,128)S(1)} %all_to_all.20.sums_ref, bf16[64,2048]{1,0:T(8,128)(2,1)S(1)} %bitcast.15), custom_call_target="tpu_custom_call" | custom-call | flops 67108864 | bytes 2097152 | tf_op jit(solution)/shard_map/pallas_call | solution.py:178
  (18 shorter events, 0.7 us)
Async XLA Ops:
  0.0 7.0 %copy-start = (bf16[512,1024]{1,0:T(8,128)(2,1)S(1)}, bf16[512,1024]{1,0:T(8,128)(2,1)}, u32[]{:S(2)}) copy-start(bf16[512,1024]{1,0:T(8,128)(2,1)} %own_ref.1) | copy-start | bytes 3145732
  2.2 10.7 %all-to-all-start = ((bf16[4,40,1024]{2,1,0:T(8,128)(2,1)}), bf16[4,40,1024]{2,1,0:T(8,128)(2,1)S(1)}, u32[]{:S(2)}, u32[]{:S(2)}) async-start(bf16[4,40,1024]{2,1,0:T(8,128)(2,1)} %shard_map.46), calls=%async_computation | async-start | bytes 655360 | tf_op jit(solution)/shard_map/all_to_all | solution.py:195
  7.0 23.0 %collective-permute-start.4 = (bf16[512,1024]{1,0:T(8,128)(2,1)S(1)}, bf16[512,1024]{1,0:T(8,128)(2,1)S(1)}, u32[]{:S(2)}, u32[]{:S(2)}) collective-permute-start(bf16[512,1024]{1,0:T(8,128)(2,1)S(1)} %copy-done), channel_id=1, source_target_pairs={{0,4},{4,0},{1,5},{5,1},{2,6},{6,2},{3,7},{7,3},{8,12},{12,8},{9,1... | collective-permute-start | bytes 3145736 | tf_op jit(solution)/shard_map/ppermute | solution.py:203
  14.2 38.2 %all-to-all-start.1 = ((bf16[16,32,1024]{2,1,0:T(8,128)(2,1)}), bf16[16,32,1024]{2,1,0:T(8,128)(2,1)S(1)}, u32[]{:S(2)}, u32[]{:S(2)}) async-start(bf16[16,32,1024]{2,1,0:T(8,128)(2,1)} %bitcast.3), calls=%async_computation.1 | async-start | bytes 2097152 | tf_op jit(solution)/shard_map/all_to_all | solution.py:197
  25.7 16.2 %collective-permute-start.5 = (bf16[512,1024]{1,0:T(8,128)(2,1)S(1)}, bf16[512,1024]{1,0:T(8,128)(2,1)S(1)}, u32[]{:S(2)}, u32[]{:S(2)}) collective-permute-start(bf16[512,1024]{1,0:T(8,128)(2,1)S(1)} %copy-done), channel_id=1, source_target_pairs={{0,32},{32,0},{1,33},{33,1},{2,34},{34,2},{3,35},{35,3},{4,36},{36... | collective-permute-start | bytes 3145736 | tf_op jit(solution)/shard_map/ppermute | solution.py:204
  30.0 14.3 %collective-permute-start.6 = (bf16[512,1024]{1,0:T(8,128)(2,1)S(1)}, bf16[512,1024]{1,0:T(8,128)(2,1)}, u32[]{:S(2)}, u32[]{:S(2)}) collective-permute-start(bf16[512,1024]{1,0:T(8,128)(2,1)S(1)} %collective-permute-done.4.pair_ref), channel_id=1, source_target_pairs={{0,32},{32,0},{1,33},{33,1},{2,34},{34,2},{3,35},{35,3},{4,36},{36... | collective-permute-start | bytes 3145736 | tf_op jit(solution)/shard_map/ppermute | solution.py:205
  41.9 1.0 copy-start.2
  57.1 33.9 %all-to-all-start.2 = ((f16[16,64,256]{2,1,0:T(8,128)(2,1)}), f16[16,64,256]{2,1,0:T(8,128)(2,1)S(1)}, u32[]{:S(2)}, u32[]{:S(2)}) async-start(f16[16,64,256]{2,1,0:T(8,128)(2,1)} %bitcast.5), calls=%async_computation.2 | async-start | bytes 1048576 | tf_op jit(solution)/shard_map/all_to_all | solution.py:227
  66.7 4.6 %collective-permute-start = (bf16[1,8,128]{2,1,0:T(8,128)(2,1)S(1)}, bf16[1,8,128]{2,1,0:T(8,128)(2,1)S(1)}, u32[]{:S(2)}, u32[]{:S(2)}) collective-permute-start(bf16[1,8,128]{2,1,0:T(8,128)(2,1)S(1)} %get-tuple-element.9), channel_id=1, source_target_pairs={{0,64},{64,0},{128,192},{192,128},{256,320},{320,256},{384,448},{4... | collective-permute-start | bytes 6152 | tf_op jit(solution)/shard_map/ppermute | solution.py:201
  71.4 5.5 %collective-permute-start.1 = (bf16[2,8,128]{2,1,0:T(8,128)(2,1)S(1)}, bf16[2,8,128]{2,1,0:T(8,128)(2,1)S(1)}, u32[]{:S(2)}, u32[]{:S(2)}) collective-permute-start(bf16[2,8,128]{2,1,0:T(8,128)(2,1)S(1)} %pad_maximum_fusion.2), channel_id=1, source_target_pairs={{0,128},{64,192},{128,0},{192,64},{256,384},{320,448},{384,256},{4... | collective-permute-start | bytes 12296 | tf_op jit(solution)/shard_map/ppermute | solution.py:201
  76.9 8.3 %collective-permute-start.2 = (bf16[4,8,128]{2,1,0:T(8,128)(2,1)S(1)}, bf16[4,8,128]{2,1,0:T(8,128)(2,1)S(1)}, u32[]{:S(2)}, u32[]{:S(2)}) collective-permute-start(bf16[4,8,128]{2,1,0:T(8,128)(2,1)S(1)} %pad_maximum_fusion.1), channel_id=1, source_target_pairs={{0,256},{64,320},{128,384},{192,448},{256,0},{320,64},{384,128},{4... | collective-permute-start | bytes 24584 | tf_op jit(solution)/shard_map/ppermute | solution.py:201
  85.2 5.7 %collective-permute-start.3 = (bf16[8,8,128]{2,1,0:T(8,128)(2,1)S(1)}, bf16[8,8,128]{2,1,0:T(8,128)(2,1)S(1)}, u32[]{:S(2)}, u32[]{:S(2)}) collective-permute-start(bf16[8,8,128]{2,1,0:T(8,128)(2,1)S(1)} %constant_dynamic-update-slice_fusion), channel_id=1, source_target_pairs={{0,32},{32,0},{1,33},{33,1},{2,34},{34,2},{3,35},{35,3},{4,36},{36... | collective-permute-start | bytes 49160 | tf_op jit(solution)/shard_map/ppermute | solution.py:230
  91.5 12.8 %copy-start.1 = (bf16[1,2048,64]{1,2,0:T(8,128)(2,1)S(1)}, bf16[1,2048,64]{1,2,0:T(8,128)(2,1)}, u32[]{:S(2)}) copy-start(bf16[1,2048,64]{1,2,0:T(8,128)(2,1)} %param.7) | copy-start | bytes 786436

commit v7 on v6

--- a/solution.py
+++ b/solution.py
@@ -27,24 +27,28 @@
     return jnp.dot(active.astype(bf16), before, preferred_element_type=f32).astype(i32)
 
 
-def pack_kernel(labels_ref, rows_ref, out_ref):
+def pack_kernel(labels_ref, rows_far, out_ref, rows_ref, sem):
+    rows_in = pltpu.make_async_copy(rows_far, rows_ref, sem)
+    rows_in.start()
     active = jnp.broadcast_to(labels_ref[...] == 0, (8, T)).astype(i32).astype(f32)
     rank = jnp.where(active[:1] > 0, ranks(active)[:1], -1)
     count = jnp.sum(active, axis=1, keepdims=True).astype(i32)[:1]
     even = (count >> 3) << 3
-    rows = rows_ref[...]
     slot = iota((SEND, T), 0)
     lane = iota((SEND, KD), 1)
     srow = iota((SEND, KD), 0)
     flags = jnp.concatenate([active[:1]] * (KD // T), axis=1)
     info = jnp.where(lane < T, flags, count.astype(f32))
+    hots = []
     for rep in range(LAYERS):
         shared = 8 * (slot & (BASE - 1)) + 2 * rep + (slot >> 4)
         rest = even + slot - REST
         target = jnp.where(slot < REST, shared, rest)
         bound = jnp.where(slot < REST, even, jnp.where(slot < SEND - 1, count, 0))
-        hot = ((rank == target) & (target < bound)).astype(f32).astype(bf16)
-        picked = jnp.dot(hot, rows, preferred_element_type=f32)
+        hots.append(((rank == target) & (target < bound)).astype(f32).astype(bf16))
+    rows_in.wait()
+    for rep, hot in enumerate(hots):
+        picked = jnp.dot(hot, rows_ref[...], preferred_element_type=f32)
         out_ref[rep] = jnp.where(srow == SEND - 1, info, picked).astype(bf16)
 
 
@@ -87,20 +91,26 @@
 def ladder_kernel(own_ref, pair_ref, got_ref, across_far, across_pair_far, out_ref, *scratch):
     across_ref, across_pair_ref, sems = scratch
     own, pair = lax.axis_index("k"), lax.axis_index("b")
-    moves = ((across_far, across_ref), (across_pair_far, across_pair_ref))
+    halves = [pl.ds(at, 256) for at in (0, 256)]
+    moves = [
+        (source.at[rows], target.at[rows])
+        for rows in halves
+        for source, target in ((across_far, across_ref), (across_pair_far, across_pair_ref))
+    ]
     copies = [pltpu.make_async_copy(*move, sems.at[n]) for n, move in enumerate(moves)]
     for copy in copies:
         copy.start()
 
     def part(piece, half):
         dims = (((1,), (1,)), ((), ()))
-        return lax.dot_general(piece[...], got_ref[half], dims, preferred_element_type=f32)
-
-    out_ref[own] = part(own_ref, pair) + part(pair_ref, 1 - pair)
-    copies[0].wait()
-    far = part(across_ref, pair)
-    copies[1].wait()
-    out_ref[1 - own] = far + part(across_pair_ref, 1 - pair)
+        return lax.dot_general(piece, got_ref[half], dims, preferred_element_type=f32)
+
+    out_ref[own] = part(own_ref[...], pair) + part(pair_ref[...], 1 - pair)
+    for n, rows in enumerate(halves):
+        copies[2 * n].wait()
+        copies[2 * n + 1].wait()
+        far = part(across_ref[rows, :], pair) + part(across_pair_ref[rows, :], 1 - pair)
+        out_ref[1 - own, rows, :] = far
 
 
 def plan_kernel(info_ref, place_ref, route_ref):
@@ -191,14 +201,27 @@
 def step(amplitudes, pair_irrep, integrals, residual_in):
     swap = [(0, 1), (1, 0)]
 
-    packed = call(pack_kernel, (LAYERS, SEND, KD), bf16, pair_irrep, amplitudes[0], limit=None, flops=2**26)
+    packed = call(
+        pack_kernel,
+        (LAYERS, SEND, KD),
+        bf16,
+        pair_irrep,
+        amplitudes[0],
+        far=1,
+        scratch=[pltpu.VMEM((T, KD), bf16), pltpu.SemaphoreType.DMA],
+        limit=None,
+        flops=2**26,
+    )
     got = lax.all_to_all(packed, "rep", 0, 0, tiled=True)
     shared, info = call(share_kernel, [(2, Z, SHARE, KD), (1, 8, T)], bf16, got, flops=2**26)
     gathered = lax.all_to_all(
         shared.reshape(2 * Z, SHARE, KD), ("b", "z"), 0, 0, tiled=True
     ).reshape(2, Z * SHARE, KD)
-    for step in (1, 2, 4):
-        info = jnp.concatenate([info, lax.ppermute(info, "z", [(z, z ^ step) for z in range(Z)])])
+    near = [info]
+    for step in (1, 2, 3):
+        near.append(lax.ppermute(info, "z", [(z, z ^ step) for z in range(Z)]))
+    info = jnp.concatenate(near)
+    info = jnp.concatenate([info, lax.ppermute(info, "z", [(z, z ^ 4) for z in range(Z)])])
 
     other = lax.ppermute(integrals, "b", swap)
     across = lax.ppermute(integrals, "k", swap)
@@ -217,7 +240,7 @@
         scratch=[
             pltpu.VMEM((512, KD), bf16),
             pltpu.VMEM((512, KD), bf16),
-            pltpu.SemaphoreType.DMA((2,)),
+            pltpu.SemaphoreType.DMA((4,)),
         ],
         limit=49,
         flops=2**30,

time: 108 us -> 108 us (level)
  starting transfers between devices: 58 us -> 63.3 us
  waiting for transfers between devices: 23.5 us -> 18.3 us
    ppermute x3 -> x4, starting transfers between devices: 7.83 us -> 13.4 us  [the longest x3 9.26 us: step(): near.append(lax.ppermute(info, 'z', [(z, z ^ step) for z in range(Z)]))]
    ppermute x3 -> x4, waiting for transfers between devices: 10.6 us -> 5.39 us  [the longest x1 4.17 us: step(): lax.ppermute(info, 'z', [(z, z ^ 4) for z in range(Z)])]
  transfers between devices with their start and end apart: 10 -> 11, of which waited for: 7 -> 6; matrix products, arithmetic and copies ran while one was open for 0% -> 0% of each run, Pallas kernels for 1% -> 1%
where the time goes in v7:
time: 108 us; the launch traced here: 107 us
  starting transfers between devices  63.3 us (59%)
  waiting for transfers between devices  18.3 us (17%)
  blocking collectives  12.8 us (12%)
  Pallas kernels  10.2 us (9%)
    all_to_all x1, blocking collectives, step(): owned = lax.all_to_all(routed, 'rep', 0, 0, tiled=True)  12.8 us
    ppermute x1, starting transfers between devices, step(): across_other = lax.ppermute(other, 'k', swap)  11.9 us
    all_to_all x1, starting transfers between devices, step(): lax.all_to_all(shared.reshape(2 * Z, SHARE, KD), ('b', 'z'), 0, 0, tiled=...  11.5 us
    pallas_call x6, Pallas kernels, call(): pl.pallas_call(kernel, out_shape=[jax.ShapeDtypeStruct(one, dtype) for on...  10.2 us
    all_to_all x1, starting transfers between devices, step(): parts = lax.all_to_all(sent, ('k', 'g', 'b'), 0, 0, tiled=True)  9.63 us
    ppermute x3, starting transfers between devices, step(): near.append(lax.ppermute(info, 'z', [(z, z ^ step) for z in range(Z)]))  9.26 us
    all_to_all x1, waiting for transfers between devices, step(): lax.all_to_all(shared.reshape(2 * Z, SHARE, KD), ('b', 'z'), 0, 0, tiled=...  8.04 us
    all_to_all x1, starting transfers between devices, step(): got = lax.all_to_all(packed, 'rep', 0, 0, tiled=True)  4.84 us
  transfers between devices with their start and end apart: 11, of which 6 were waited for; matrix products, arithmetic and copies ran while one was open for 0% of the time, Pallas kernels for 1%

profile of v7, /device:TPU:1, one launch (start us, length us, event | category | flops | bytes accessed | tf_op | source)
XLA Modules:
  0.0 106.8 jit_solution(566528695957020460)
XLA Ops:
  0.0 2.7 %shard_map.46 = bf16[4,40,1024]{2,1,0:T(8,128)(2,1)} custom-call(s32[1,128]{1,0:T(1,128)} %labels_ref.1, bf16[128,1024]{1,0:T(8,128)(2,1)} %bitcast.17), custom_call_target="tpu_custom_call" | custom-call | flops 67108864 | bytes 2097152 | tf_op jit(solution)/shard_map/pallas_call | solution.py:188
  2.7 4.8 %all-to-all-start = ((bf16[4,40,1024]{2,1,0:T(8,128)(2,1)}), bf16[4,40,1024]{2,1,0:T(8,128)(2,1)S(1)}, u32[]{:S(2)}, u32[]{:S(2)}) async-start(bf16[4,40,1024]{2,1,0:T(8,128)(2,1)} %shard_map.46), calls=%async_computation | async-start | bytes 655360 | tf_op jit(solution)/shard_map/all_to_all | solution.py:215
  7.6 3.2 %collective-permute-start.5 = (bf16[512,1024]{1,0:T(8,128)(2,1)S(1)}, bf16[512,1024]{1,0:T(8,128)(2,1)S(1)}, u32[]{:S(2)}, u32[]{:S(2)}) collective-permute-start(bf16[512,1024]{1,0:T(8,128)(2,1)S(1)} %copy-done), channel_id=1, source_target_pairs={{0,4},{4,0},{1,5},{5,1},{2,6},{6,2},{3,7},{7,3},{8,12},{12,8},{9,1... | collective-permute-start | bytes 3145736 | tf_op jit(solution)/shard_map/ppermute | solution.py:226
  10.8 2.7 %all-to-all-done.got_ref = bf16[4,40,1024]{2,1,0:T(8,128)(2,1)S(1)} async-done(((bf16[4,40,1024]{2,1,0:T(8,128)(2,1)}), bf16[4,40,1024]{2,1,0:T(8,128)(2,1)S(1)}, u32[]{:S(2)}, u32[]{:S(2)}) %all-to-all-start) | async-done | bytes 327712 | tf_op jit(solution)/shard_map/all_to_all | solution.py:215
  13.5 1.3 %shard_map.47 = (bf16[2,8,32,1024]{3,2,1,0:T(8,128)(2,1)}, bf16[1,8,128]{2,1,0:T(8,128)(2,1)S(1)}) custom-call(bf16[4,40,1024]{2,1,0:T(8,128)(2,1)S(1)} %all-to-all-done.got_ref), custom_call_target="tpu_custom_call" | custom-call | flops 67108864 | bytes 2097152 | tf_op jit(solution)/shard_map/pallas_call | solution.py:188
  14.8 11.5 %all-to-all-start.1 = ((bf16[16,32,1024]{2,1,0:T(8,128)(2,1)}), bf16[16,32,1024]{2,1,0:T(8,128)(2,1)S(1)}, u32[]{:S(2)}, u32[]{:S(2)}) async-start(bf16[16,32,1024]{2,1,0:T(8,128)(2,1)} %bitcast.3), calls=%async_computation.1 | async-start | bytes 2097152 | tf_op jit(solution)/shard_map/all_to_all | solution.py:217
  26.3 4.3 %collective-permute-start.6 = (bf16[512,1024]{1,0:T(8,128)(2,1)S(1)}, bf16[512,1024]{1,0:T(8,128)(2,1)S(1)}, u32[]{:S(2)}, u32[]{:S(2)}) collective-permute-start(bf16[512,1024]{1,0:T(8,128)(2,1)S(1)} %copy-done), channel_id=1, source_target_pairs={{0,32},{32,0},{1,33},{33,1},{2,34},{34,2},{3,35},{35,3},{4,36},{36... | collective-permute-start | bytes 3145736 | tf_op jit(solution)/shard_map/ppermute | solution.py:227
  30.6 11.9 %collective-permute-start.7 = (bf16[512,1024]{1,0:T(8,128)(2,1)S(1)}, bf16[512,1024]{1,0:T(8,128)(2,1)}, u32[]{:S(2)}, u32[]{:S(2)}) collective-permute-start(bf16[512,1024]{1,0:T(8,128)(2,1)S(1)} %collective-permute-done.5.pair_ref), channel_id=1, source_target_pairs={{0,32},{32,0},{1,33},{33,1},{2,34},{34,2},{3,35},{35,3},{4,36},{36... | collective-permute-start | bytes 3145736 | tf_op jit(solution)/shard_map/ppermute | solution.py:228
  42.5 1.0 copy-done.2
  43.5 1.4 %collective-permute-done.7.across_pair_far = bf16[512,1024]{1,0:T(8,128)(2,1)} collective-permute-done((bf16[512,1024]{1,0:T(8,128)(2,1)S(1)}, bf16[512,1024]{1,0:T(8,128)(2,1)}, u32[]{:S(2)}, u32[]{:S(2)}) %collective-permute-start.7) | collective-permute-done | bytes 1048608 | tf_op jit(solution)/shard_map/ppermute | solution.py:228
  44.9 8.0 %all-to-all-done.1 = bf16[16,32,1024]{2,1,0:T(8,128)(2,1)S(1)} async-done(((bf16[16,32,1024]{2,1,0:T(8,128)(2,1)}), bf16[16,32,1024]{2,1,0:T(8,128)(2,1)S(1)}, u32[]{:S(2)}, u32[]{:S(2)}) %all-to-all-start.1) | async-done | bytes 1048608 | tf_op jit(solution)/shard_map/all_to_all | solution.py:217
  52.9 3.7 %shard_map.49 = f32[2,512,256]{2,1,0:T(8,128)S(1)} custom-call(bf16[512,1024]{1,0:T(8,128)(2,1)S(1)} %copy-done, bf16[512,1024]{1,0:T(8,128)(2,1)S(1)} %collective-permute-done.5.pair_ref, bf16[2,256,1024]{2,1,0:T(8,128)(2,1)S(1)} %bitcast.14, bf16[512,1024]{1,0:T(8,128)(2,1)} %copy-done.2, bf16[512,1024]{1,0:T(8,128)(2,1)} %collective-permute-done.7.across_pair_far), custom_call_target="tpu_custom_call" | custom-call | flops 1073741824 | bytes 2097152 | tf_op jit(solution)/shard_map/pallas_call | solution.py:188
  56.7 0.9 convert_element_type.9
  57.5 9.6 %all-to-all-start.2 = ((f16[16,64,256]{2,1,0:T(8,128)(2,1)}), f16[16,64,256]{2,1,0:T(8,128)(2,1)S(1)}, u32[]{:S(2)}, u32[]{:S(2)}) async-start(f16[16,64,256]{2,1,0:T(8,128)(2,1)} %bitcast.5), calls=%async_computation.2 | async-start | bytes 1048576 | tf_op jit(solution)/shard_map/all_to_all | solution.py:250
  67.2 1.9 %collective-permute-start.2 = (bf16[1,8,128]{2,1,0:T(8,128)(2,1)S(1)}, bf16[1,8,128]{2,1,0:T(8,128)(2,1)S(1)}, u32[]{:S(2)}, u32[]{:S(2)}) collective-permute-start(bf16[1,8,128]{2,1,0:T(8,128)(2,1)S(1)} %get-tuple-element.9), channel_id=1, source_target_pairs={{0,192},{64,128},{128,64},{192,0},{256,448},{320,384},{384,320},{4... | collective-permute-start | bytes 6152 | tf_op jit(solution)/shard_map/ppermute | solution.py:222
  69.1 4.0 %collective-permute-start.1 = (bf16[1,8,128]{2,1,0:T(8,128)(2,1)S(1)}, bf16[1,8,128]{2,1,0:T(8,128)(2,1)S(1)}, u32[]{:S(2)}, u32[]{:S(2)}) collective-permute-start(bf16[1,8,128]{2,1,0:T(8,128)(2,1)S(1)} %get-tuple-element.9), channel_id=1, source_target_pairs={{0,128},{64,192},{128,0},{192,64},{256,384},{320,448},{384,256},{4... | collective-permute-start | bytes 6152 | tf_op jit(solution)/shard_map/ppermute | solution.py:222
  73.1 3.4 %collective-permute-start = (bf16[1,8,128]{2,1,0:T(8,128)(2,1)S(1)}, bf16[1,8,128]{2,1,0:T(8,128)(2,1)S(1)}, u32[]{:S(2)}, u32[]{:S(2)}) collective-permute-start(bf16[1,8,128]{2,1,0:T(8,128)(2,1)S(1)} %get-tuple-element.9), channel_id=1, source_target_pairs={{0,64},{64,0},{128,192},{192,128},{256,320},{320,256},{384,448},{4... | collective-permute-start | bytes 6152 | tf_op jit(solution)/shard_map/ppermute | solution.py:222
  76.5 1.2 %collective-permute-done = bf16[1,8,128]{2,1,0:T(8,128)(2,1)S(1)} collective-permute-done((bf16[1,8,128]{2,1,0:T(8,128)(2,1)S(1)}, bf16[1,8,128]{2,1,0:T(8,128)(2,1)S(1)}, u32[]{:S(2)}, u32[]{:S(2)}) %collective-permute-start) | collective-permute-done | bytes 2080 | tf_op jit(solution)/shard_map/ppermute | solution.py:222
  77.7 4.2 %collective-permute-start.3 = (bf16[4,8,128]{2,1,0:T(8,128)(2,1)S(1)}, bf16[4,8,128]{2,1,0:T(8,128)(2,1)S(1)}, u32[]{:S(2)}, u32[]{:S(2)}) collective-permute-start(bf16[4,8,128]{2,1,0:T(8,128)(2,1)S(1)} %pad_maximum_fusion.1), channel_id=1, source_target_pairs={{0,256},{64,320},{128,384},{192,448},{256,0},{320,64},{384,128},{4... | collective-permute-start | bytes 24584 | tf_op jit(solution)/shard_map/ppermute | solution.py:224
  81.9 4.2 %collective-permute-done.3 = bf16[4,8,128]{2,1,0:T(8,128)(2,1)S(1)} collective-permute-done((bf16[4,8,128]{2,1,0:T(8,128)(2,1)S(1)}, bf16[4,8,128]{2,1,0:T(8,128)(2,1)S(1)}, u32[]{:S(2)}, u32[]{:S(2)}) %collective-permute-start.3) | collective-permute-done | bytes 8224 | tf_op jit(solution)/shard_map/ppermute | solution.py:224
  86.1 4.5 %collective-permute-start.4 = (bf16[8,8,128]{2,1,0:T(8,128)(2,1)S(1)}, bf16[8,8,128]{2,1,0:T(8,128)(2,1)S(1)}, u32[]{:S(2)}, u32[]{:S(2)}) collective-permute-start(bf16[8,8,128]{2,1,0:T(8,128)(2,1)S(1)} %constant_dynamic-update-slice_fusion), channel_id=1, source_target_pairs={{0,32},{32,0},{1,33},{33,1},{2,34},{34,2},{3,35},{35,3},{4,36},{36... | collective-permute-start | bytes 49160 | tf_op jit(solution)/shard_map/ppermute | solution.py:253
  90.6 0.8 collective-permute-done.4
  92.0 12.8 %all_to_all.20.sums_ref = f32[4,2,2,64,128]{4,3,2,1,0:T(8,128)S(1)} all-to-all(f32[4,2,2,64,128]{4,3,2,1,0:T(8,128)S(1)} %shard_map.50), channel_id=1, replica_groups=mesh['z'=8,'k'=2,'g'=4,'b'=2,'rep'=4] {'rep'}, dimensions={0} | all-to-all | bytes 1048576 | tf_op jit(solution)/shard_map/all_to_all | solution.py:258
  104.9 1.9 %shard_map.51 = bf16[64,2048]{1,0:T(8,128)(2,1)} custom-call(s32[2,16,128]{2,1,0:T(8,128)S(1)} %get-tuple-element.10.place_ref, f32[4,2,2,64,128]{4,3,2,1,0:T(8,128)S(1)} %all_to_all.20.sums_ref, bf16[64,2048]{1,0:T(8,128)(2,1)S(1)} %bitcast.15), custom_call_target="tpu_custom_call" | custom-call | flops 67108864 | bytes 2097152 | tf_op jit(solution)/shard_map/pallas_call | solution.py:188
  (20 shorter events, 0.7 us)
Async XLA Ops:
  0.0 7.6 %copy-start = (bf16[512,1024]{1,0:T(8,128)(2,1)S(1)}, bf16[512,1024]{1,0:T(8,128)(2,1)}, u32[]{:S(2)}) copy-start(bf16[512,1024]{1,0:T(8,128)(2,1)} %own_ref.1) | copy-start | bytes 3145732
  2.7 10.7 %all-to-all-start = ((bf16[4,40,1024]{2,1,0:T(8,128)(2,1)}), bf16[4,40,1024]{2,1,0:T(8,128)(2,1)S(1)}, u32[]{:S(2)}, u32[]{:S(2)}) async-start(bf16[4,40,1024]{2,1,0:T(8,128)(2,1)} %shard_map.46), calls=%async_computation | async-start | bytes 655360 | tf_op jit(solution)/shard_map/all_to_all | solution.py:215
  7.6 23.0 %collective-permute-start.5 = (bf16[512,1024]{1,0:T(8,128)(2,1)S(1)}, bf16[512,1024]{1,0:T(8,128)(2,1)S(1)}, u32[]{:S(2)}, u32[]{:S(2)}) collective-permute-start(bf16[512,1024]{1,0:T(8,128)(2,1)S(1)} %copy-done), channel_id=1, source_target_pairs={{0,4},{4,0},{1,5},{5,1},{2,6},{6,2},{3,7},{7,3},{8,12},{12,8},{9,1... | collective-permute-start | bytes 3145736 | tf_op jit(solution)/shard_map/ppermute | solution.py:226
  14.8 38.2 %all-to-all-start.1 = ((bf16[16,32,1024]{2,1,0:T(8,128)(2,1)}), bf16[16,32,1024]{2,1,0:T(8,128)(2,1)S(1)}, u32[]{:S(2)}, u32[]{:S(2)}) async-start(bf16[16,32,1024]{2,1,0:T(8,128)(2,1)} %bitcast.3), calls=%async_computation.1 | async-start | bytes 2097152 | tf_op jit(solution)/shard_map/all_to_all | solution.py:217
  26.3 16.2 %collective-permute-start.6 = (bf16[512,1024]{1,0:T(8,128)(2,1)S(1)}, bf16[512,1024]{1,0:T(8,128)(2,1)S(1)}, u32[]{:S(2)}, u32[]{:S(2)}) collective-permute-start(bf16[512,1024]{1,0:T(8,128)(2,1)S(1)} %copy-done), channel_id=1, source_target_pairs={{0,32},{32,0},{1,33},{33,1},{2,34},{34,2},{3,35},{35,3},{4,36},{36... | collective-permute-start | bytes 3145736 | tf_op jit(solution)/shard_map/ppermute | solution.py:227
  30.6 14.3 %collective-permute-start.7 = (bf16[512,1024]{1,0:T(8,128)(2,1)S(1)}, bf16[512,1024]{1,0:T(8,128)(2,1)}, u32[]{:S(2)}, u32[]{:S(2)}) collective-permute-start(bf16[512,1024]{1,0:T(8,128)(2,1)S(1)} %collective-permute-done.5.pair_ref), channel_id=1, source_target_pairs={{0,32},{32,0},{1,33},{33,1},{2,34},{34,2},{3,35},{35,3},{4,36},{36... | collective-permute-start | bytes 3145736 | tf_op jit(solution)/shard_map/ppermute | solution.py:228
  42.5 1.0 copy-start.2
  57.5 34.0 %all-to-all-start.2 = ((f16[16,64,256]{2,1,0:T(8,128)(2,1)}), f16[16,64,256]{2,1,0:T(8,128)(2,1)S(1)}, u32[]{:S(2)}, u32[]{:S(2)}) async-start(f16[16,64,256]{2,1,0:T(8,128)(2,1)} %bitcast.5), calls=%async_computation.2 | async-start | bytes 1048576 | tf_op jit(solution)/shard_map/all_to_all | solution.py:250
  67.2 9.3 %collective-permute-start.2 = (bf16[1,8,128]{2,1,0:T(8,128)(2,1)S(1)}, bf16[1,8,128]{2,1,0:T(8,128)(2,1)S(1)}, u32[]{:S(2)}, u32[]{:S(2)}) collective-permute-start(bf16[1,8,128]{2,1,0:T(8,128)(2,1)S(1)} %get-tuple-element.9), channel_id=1, source_target_pairs={{0,192},{64,128},{128,64},{192,0},{256,448},{320,384},{384,320},{4... | collective-permute-start | bytes 6152 | tf_op jit(solution)/shard_map/ppermute | solution.py:222
  69.1 7.4 %collective-permute-start.1 = (bf16[1,8,128]{2,1,0:T(8,128)(2,1)S(1)}, bf16[1,8,128]{2,1,0:T(8,128)(2,1)S(1)}, u32[]{:S(2)}, u32[]{:S(2)}) collective-permute-start(bf16[1,8,128]{2,1,0:T(8,128)(2,1)S(1)} %get-tuple-element.9), channel_id=1, source_target_pairs={{0,128},{64,192},{128,0},{192,64},{256,384},{320,448},{384,256},{4... | collective-permute-start | bytes 6152 | tf_op jit(solution)/shard_map/ppermute | solution.py:222
  73.1 4.6 %collective-permute-start = (bf16[1,8,128]{2,1,0:T(8,128)(2,1)S(1)}, bf16[1,8,128]{2,1,0:T(8,128)(2,1)S(1)}, u32[]{:S(2)}, u32[]{:S(2)}) collective-permute-start(bf16[1,8,128]{2,1,0:T(8,128)(2,1)S(1)} %get-tuple-element.9), channel_id=1, source_target_pairs={{0,64},{64,0},{128,192},{192,128},{256,320},{320,256},{384,448},{4... | collective-permute-start | bytes 6152 | tf_op jit(solution)/shard_map/ppermute | solution.py:222
  77.7 8.4 %collective-permute-start.3 = (bf16[4,8,128]{2,1,0:T(8,128)(2,1)S(1)}, bf16[4,8,128]{2,1,0:T(8,128)(2,1)S(1)}, u32[]{:S(2)}, u32[]{:S(2)}) collective-permute-start(bf16[4,8,128]{2,1,0:T(8,128)(2,1)S(1)} %pad_maximum_fusion.1), channel_id=1, source_target_pairs={{0,256},{64,320},{128,384},{192,448},{256,0},{320,64},{384,128},{4... | collective-permute-start | bytes 24584 | tf_op jit(solution)/shard_map/ppermute | solution.py:224
  86.1 5.3 %collective-permute-start.4 = (bf16[8,8,128]{2,1,0:T(8,128)(2,1)S(1)}, bf16[8,8,128]{2,1,0:T(8,128)(2,1)S(1)}, u32[]{:S(2)}, u32[]{:S(2)}) collective-permute-start(bf16[8,8,128]{2,1,0:T(8,128)(2,1)S(1)} %constant_dynamic-update-slice_fusion), channel_id=1, source_target_pairs={{0,32},{32,0},{1,33},{33,1},{2,34},{34,2},{3,35},{35,3},{4,36},{36... | collective-permute-start | bytes 49160 | tf_op jit(solution)/shard_map/ppermute | solution.py:253
  92.0 12.9 %copy-start.1 = (bf16[1,2048,64]{1,2,0:T(8,128)(2,1)S(1)}, bf16[1,2048,64]{1,2,0:T(8,128)(2,1)}, u32[]{:S(2)}) copy-start(bf16[1,2048,64]{1,2,0:T(8,128)(2,1)} %param.7) | copy-start | bytes 786436

commit v8 on v6

--- a/solution.py
+++ b/solution.py
@@ -197,8 +197,11 @@
     gathered = lax.all_to_all(
         shared.reshape(2 * Z, SHARE, KD), ("b", "z"), 0, 0, tiled=True
     ).reshape(2, Z * SHARE, KD)
-    for step in (1, 2, 4):
-        info = jnp.concatenate([info, lax.ppermute(info, "z", [(z, z ^ step) for z in range(Z)])])
+    near = [info]
+    for step in (1, 2, 3):
+        near.append(lax.ppermute(info, "z", [(z, z ^ step) for z in range(Z)]))
+    info = jnp.concatenate(near)
+    info = jnp.concatenate([info, lax.ppermute(info, "z", [(z, z ^ 4) for z in range(Z)])])
 
     other = lax.ppermute(integrals, "b", swap)
     across = lax.ppermute(integrals, "k", swap)
@@ -219,7 +222,7 @@
             pltpu.VMEM((512, KD), bf16),
             pltpu.SemaphoreType.DMA((2,)),
         ],
-        limit=49,
+        limit=48,
         flops=2**30,
     )
 

time: 108 us -> 109 us (level)
  starting transfers between devices: 58 us -> 63.2 us
  waiting for transfers between devices: 23.5 us -> 18.4 us
  local copies, waits for them, and re-layouts: 1.02 us -> 2.23 us
    ppermute x3 -> x4, starting transfers between devices: 7.83 us -> 13.4 us  [the longest x3 9.26 us: step(): near.append(lax.ppermute(info, 'z', [(z, z ^ step) for z in range(Z)]))]
    ppermute x3 -> x4, waiting for transfers between devices: 10.6 us -> 5.39 us  [the longest x1 4.16 us: step(): lax.ppermute(info, 'z', [(z, z ^ 4) for z in range(Z)])]
    unnamed x9 -> x12, local copies, waits for them, and re-layouts: 1.02 us -> 2.22 us
  transfers between devices with their start and end apart: 10 -> 11, of which waited for: 7 -> 6; matrix products, arithmetic and copies ran while one was open for 0% -> 0% of each run, Pallas kernels for 1% -> 1%
where the time goes in v8:
time: 109 us; the launch traced here: 107 us
  starting transfers between devices  63.2 us (58%)
  waiting for transfers between devices  18.4 us (17%)
  blocking collectives  12.8 us (12%)
  Pallas kernels  9.54 us (9%)
  local copies, waits for them, and re-layouts  2.23 us (2%)
    all_to_all x1, blocking collectives, step(): owned = lax.all_to_all(routed, 'rep', 0, 0, tiled=True)  12.8 us
    ppermute x1, starting transfers between devices, step(): across_other = lax.ppermute(other, 'k', swap)  11.9 us
    all_to_all x1, starting transfers between devices, step(): lax.all_to_all(shared.reshape(2 * Z, SHARE, KD), ('b', 'z'), 0, 0, tiled=...  11.5 us
    all_to_all x1, starting transfers between devices, step(): parts = lax.all_to_all(sent, ('k', 'g', 'b'), 0, 0, tiled=True)  9.62 us
    pallas_call x6, Pallas kernels, call(): pl.pallas_call(kernel, out_shape=[jax.ShapeDtypeStruct(one, dtype) for on...  9.54 us
    ppermute x3, starting transfers between devices, step(): near.append(lax.ppermute(info, 'z', [(z, z ^ step) for z in range(Z)]))  9.26 us
    all_to_all x1, waiting for transfers between devices, step(): lax.all_to_all(shared.reshape(2 * Z, SHARE, KD), ('b', 'z'), 0, 0, tiled=...  8.07 us
    all_to_all x1, starting transfers between devices, step(): got = lax.all_to_all(packed, 'rep', 0, 0, tiled=True)  4.83 us
  transfers between devices with their start and end apart: 11, of which 6 were waited for; matrix products, arithmetic and copies ran while one was open for 0% of the time, Pallas kernels for 1%

profile of v8, /device:TPU:1, one launch (start us, length us, event | category | flops | bytes accessed | tf_op | source)
XLA Modules:
  0.0 107.3 jit_solution(7662560291436880451)
XLA Ops:
  0.0 2.2 %shard_map.46 = bf16[4,40,1024]{2,1,0:T(8,128)(2,1)} custom-call(s32[1,128]{1,0:T(1,128)} %labels_ref.1, bf16[128,1024]{1,0:T(8,128)(2,1)} %bitcast.17), custom_call_target="tpu_custom_call" | custom-call | flops 67108864 | bytes 2097152 | tf_op jit(solution)/shard_map/pallas_call | solution.py:178
  2.2 4.8 %all-to-all-start = ((bf16[4,40,1024]{2,1,0:T(8,128)(2,1)}), bf16[4,40,1024]{2,1,0:T(8,128)(2,1)S(1)}, u32[]{:S(2)}, u32[]{:S(2)}) async-start(bf16[4,40,1024]{2,1,0:T(8,128)(2,1)} %shard_map.46), calls=%async_computation | async-start | bytes 655360 | tf_op jit(solution)/shard_map/all_to_all | solution.py:195
  7.0 3.2 %collective-permute-start.5 = (bf16[512,1024]{1,0:T(8,128)(2,1)S(1)}, bf16[512,1024]{1,0:T(8,128)(2,1)S(1)}, u32[]{:S(2)}, u32[]{:S(2)}) collective-permute-start(bf16[512,1024]{1,0:T(8,128)(2,1)S(1)} %copy-done), channel_id=1, source_target_pairs={{0,4},{4,0},{1,5},{5,1},{2,6},{6,2},{3,7},{7,3},{8,12},{12,8},{9,1... | collective-permute-start | bytes 3145736 | tf_op jit(solution)/shard_map/ppermute | solution.py:206
  10.2 2.7 %all-to-all-done.got_ref = bf16[4,40,1024]{2,1,0:T(8,128)(2,1)S(1)} async-done(((bf16[4,40,1024]{2,1,0:T(8,128)(2,1)}), bf16[4,40,1024]{2,1,0:T(8,128)(2,1)S(1)}, u32[]{:S(2)}, u32[]{:S(2)}) %all-to-all-start) | async-done | bytes 327712 | tf_op jit(solution)/shard_map/all_to_all | solution.py:195
  12.9 1.3 %shard_map.47 = (bf16[2,8,32,1024]{3,2,1,0:T(8,128)(2,1)}, bf16[1,8,128]{2,1,0:T(8,128)(2,1)S(1)}) custom-call(bf16[4,40,1024]{2,1,0:T(8,128)(2,1)S(1)} %all-to-all-done.got_ref), custom_call_target="tpu_custom_call" | custom-call | flops 67108864 | bytes 2097152 | tf_op jit(solution)/shard_map/pallas_call | solution.py:178
  14.2 11.5 %all-to-all-start.1 = ((bf16[16,32,1024]{2,1,0:T(8,128)(2,1)}), bf16[16,32,1024]{2,1,0:T(8,128)(2,1)S(1)}, u32[]{:S(2)}, u32[]{:S(2)}) async-start(bf16[16,32,1024]{2,1,0:T(8,128)(2,1)} %bitcast.3), calls=%async_computation.1 | async-start | bytes 2097152 | tf_op jit(solution)/shard_map/all_to_all | solution.py:197
  25.7 4.3 %collective-permute-start.6 = (bf16[512,1024]{1,0:T(8,128)(2,1)S(1)}, bf16[512,1024]{1,0:T(8,128)(2,1)S(1)}, u32[]{:S(2)}, u32[]{:S(2)}) collective-permute-start(bf16[512,1024]{1,0:T(8,128)(2,1)S(1)} %copy-done), channel_id=1, source_target_pairs={{0,32},{32,0},{1,33},{33,1},{2,34},{34,2},{3,35},{35,3},{4,36},{36... | collective-permute-start | bytes 3145736 | tf_op jit(solution)/shard_map/ppermute | solution.py:207
  30.0 11.9 %collective-permute-start.7 = (bf16[512,1024]{1,0:T(8,128)(2,1)S(1)}, bf16[512,1024]{1,0:T(8,128)(2,1)}, u32[]{:S(2)}, u32[]{:S(2)}) collective-permute-start(bf16[512,1024]{1,0:T(8,128)(2,1)S(1)} %collective-permute-done.5.pair_ref), channel_id=1, source_target_pairs={{0,32},{32,0},{1,33},{33,1},{2,34},{34,2},{3,35},{35,3},{4,36},{36... | collective-permute-start | bytes 3145736 | tf_op jit(solution)/shard_map/ppermute | solution.py:208
  41.9 1.0 copy-done.1
  42.9 1.4 %collective-permute-done.7.across_pair_far = bf16[512,1024]{1,0:T(8,128)(2,1)} collective-permute-done((bf16[512,1024]{1,0:T(8,128)(2,1)S(1)}, bf16[512,1024]{1,0:T(8,128)(2,1)}, u32[]{:S(2)}, u32[]{:S(2)}) %collective-permute-start.7) | collective-permute-done | bytes 1048608 | tf_op jit(solution)/shard_map/ppermute | solution.py:208
  44.3 8.1 %all-to-all-done.1 = bf16[16,32,1024]{2,1,0:T(8,128)(2,1)S(1)} async-done(((bf16[16,32,1024]{2,1,0:T(8,128)(2,1)}), bf16[16,32,1024]{2,1,0:T(8,128)(2,1)S(1)}, u32[]{:S(2)}, u32[]{:S(2)}) %all-to-all-start.1) | async-done | bytes 1048608 | tf_op jit(solution)/shard_map/all_to_all | solution.py:197
  52.4 1.2 %copy-done.2 = bf16[512,1024]{1,0:T(8,128)(2,1)S(1)} copy-done((bf16[512,1024]{1,0:T(8,128)(2,1)S(1)}, bf16[512,1024]{1,0:T(8,128)(2,1)}, u32[]{:S(2)}) %copy-start.2) | copy-done | bytes 1048600
  53.6 3.6 %shard_map.49 = f32[2,512,256]{2,1,0:T(8,128)S(1)} custom-call(bf16[512,1024]{1,0:T(8,128)(2,1)S(1)} %copy-done, bf16[512,1024]{1,0:T(8,128)(2,1)S(1)} %collective-permute-done.5.pair_ref, bf16[2,256,1024]{2,1,0:T(8,128)(2,1)S(1)} %bitcast.14, bf16[512,1024]{1,0:T(8,128)(2,1)S(1)} %copy-done.2, bf16[512,1024]{1,0:T(8,128)(2,1)} %collective-permute-done.7.across_pair_far), custom_call_target="tpu_custom_call" | custom-call | flops 1073741824 | bytes 2097152 | tf_op jit(solution)/shard_map/pallas_call | solution.py:178
  57.2 0.9 convert_element_type.9
  58.1 9.6 %all-to-all-start.2 = ((f16[16,64,256]{2,1,0:T(8,128)(2,1)}), f16[16,64,256]{2,1,0:T(8,128)(2,1)S(1)}, u32[]{:S(2)}, u32[]{:S(2)}) async-start(f16[16,64,256]{2,1,0:T(8,128)(2,1)} %bitcast.5), calls=%async_computation.2 | async-start | bytes 1048576 | tf_op jit(solution)/shard_map/all_to_all | solution.py:230
  67.7 1.9 %collective-permute-start.2 = (bf16[1,8,128]{2,1,0:T(8,128)(2,1)S(1)}, bf16[1,8,128]{2,1,0:T(8,128)(2,1)S(1)}, u32[]{:S(2)}, u32[]{:S(2)}) collective-permute-start(bf16[1,8,128]{2,1,0:T(8,128)(2,1)S(1)} %get-tuple-element.9), channel_id=1, source_target_pairs={{0,192},{64,128},{128,64},{192,0},{256,448},{320,384},{384,320},{4... | collective-permute-start | bytes 6152 | tf_op jit(solution)/shard_map/ppermute | solution.py:202
  69.6 4.0 %collective-permute-start.1 = (bf16[1,8,128]{2,1,0:T(8,128)(2,1)S(1)}, bf16[1,8,128]{2,1,0:T(8,128)(2,1)S(1)}, u32[]{:S(2)}, u32[]{:S(2)}) collective-permute-start(bf16[1,8,128]{2,1,0:T(8,128)(2,1)S(1)} %get-tuple-element.9), channel_id=1, source_target_pairs={{0,128},{64,192},{128,0},{192,64},{256,384},{320,448},{384,256},{4... | collective-permute-start | bytes 6152 | tf_op jit(solution)/shard_map/ppermute | solution.py:202
  73.6 3.4 %collective-permute-start = (bf16[1,8,128]{2,1,0:T(8,128)(2,1)S(1)}, bf16[1,8,128]{2,1,0:T(8,128)(2,1)S(1)}, u32[]{:S(2)}, u32[]{:S(2)}) collective-permute-start(bf16[1,8,128]{2,1,0:T(8,128)(2,1)S(1)} %get-tuple-element.9), channel_id=1, source_target_pairs={{0,64},{64,0},{128,192},{192,128},{256,320},{320,256},{384,448},{4... | collective-permute-start | bytes 6152 | tf_op jit(solution)/shard_map/ppermute | solution.py:202
  77.0 1.2 %collective-permute-done = bf16[1,8,128]{2,1,0:T(8,128)(2,1)S(1)} collective-permute-done((bf16[1,8,128]{2,1,0:T(8,128)(2,1)S(1)}, bf16[1,8,128]{2,1,0:T(8,128)(2,1)S(1)}, u32[]{:S(2)}, u32[]{:S(2)}) %collective-permute-start) | collective-permute-done | bytes 2080 | tf_op jit(solution)/shard_map/ppermute | solution.py:202
  78.3 4.2 %collective-permute-start.3 = (bf16[4,8,128]{2,1,0:T(8,128)(2,1)S(1)}, bf16[4,8,128]{2,1,0:T(8,128)(2,1)S(1)}, u32[]{:S(2)}, u32[]{:S(2)}) collective-permute-start(bf16[4,8,128]{2,1,0:T(8,128)(2,1)S(1)} %pad_maximum_fusion.1), channel_id=1, source_target_pairs={{0,256},{64,320},{128,384},{192,448},{256,0},{320,64},{384,128},{4... | collective-permute-start | bytes 24584 | tf_op jit(solution)/shard_map/ppermute | solution.py:204
  82.5 4.2 %collective-permute-done.3 = bf16[4,8,128]{2,1,0:T(8,128)(2,1)S(1)} collective-permute-done((bf16[4,8,128]{2,1,0:T(8,128)(2,1)S(1)}, bf16[4,8,128]{2,1,0:T(8,128)(2,1)S(1)}, u32[]{:S(2)}, u32[]{:S(2)}) %collective-permute-start.3) | collective-permute-done | bytes 8224 | tf_op jit(solution)/shard_map/ppermute | solution.py:204
  86.7 4.5 %collective-permute-start.4 = (bf16[8,8,128]{2,1,0:T(8,128)(2,1)S(1)}, bf16[8,8,128]{2,1,0:T(8,128)(2,1)S(1)}, u32[]{:S(2)}, u32[]{:S(2)}) collective-permute-start(bf16[8,8,128]{2,1,0:T(8,128)(2,1)S(1)} %constant_dynamic-update-slice_fusion), channel_id=1, source_target_pairs={{0,32},{32,0},{1,33},{33,1},{2,34},{34,2},{3,35},{35,3},{4,36},{36... | collective-permute-start | bytes 49160 | tf_op jit(solution)/shard_map/ppermute | solution.py:233
  92.6 12.8 %all_to_all.20.sums_ref = f32[4,2,2,64,128]{4,3,2,1,0:T(8,128)S(1)} all-to-all(f32[4,2,2,64,128]{4,3,2,1,0:T(8,128)S(1)} %shard_map.50), channel_id=1, replica_groups=mesh['z'=8,'k'=2,'g'=4,'b'=2,'rep'=4] {'rep'}, dimensions={0} | all-to-all | bytes 1048576 | tf_op jit(solution)/shard_map/all_to_all | solution.py:238
  105.4 1.9 %shard_map.51 = bf16[64,2048]{1,0:T(8,128)(2,1)} custom-call(s32[2,16,128]{2,1,0:T(8,128)S(1)} %get-tuple-element.10.place_ref, f32[4,2,2,64,128]{4,3,2,1,0:T(8,128)S(1)} %all_to_all.20.sums_ref, bf16[64,2048]{1,0:T(8,128)(2,1)S(1)} %bitcast.15), custom_call_target="tpu_custom_call" | custom-call | flops 67108864 | bytes 2097152 | tf_op jit(solution)/shard_map/pallas_call | solution.py:178
  (22 shorter events, 1.5 us)
Async XLA Ops:
  0.0 7.0 %copy-start = (bf16[512,1024]{1,0:T(8,128)(2,1)S(1)}, bf16[512,1024]{1,0:T(8,128)(2,1)}, u32[]{:S(2)}) copy-start(bf16[512,1024]{1,0:T(8,128)(2,1)} %own_ref.1) | copy-start | bytes 3145732
  2.2 10.7 %all-to-all-start = ((bf16[4,40,1024]{2,1,0:T(8,128)(2,1)}), bf16[4,40,1024]{2,1,0:T(8,128)(2,1)S(1)}, u32[]{:S(2)}, u32[]{:S(2)}) async-start(bf16[4,40,1024]{2,1,0:T(8,128)(2,1)} %shard_map.46), calls=%async_computation | async-start | bytes 655360 | tf_op jit(solution)/shard_map/all_to_all | solution.py:195
  7.0 23.0 %collective-permute-start.5 = (bf16[512,1024]{1,0:T(8,128)(2,1)S(1)}, bf16[512,1024]{1,0:T(8,128)(2,1)S(1)}, u32[]{:S(2)}, u32[]{:S(2)}) collective-permute-start(bf16[512,1024]{1,0:T(8,128)(2,1)S(1)} %copy-done), channel_id=1, source_target_pairs={{0,4},{4,0},{1,5},{5,1},{2,6},{6,2},{3,7},{7,3},{8,12},{12,8},{9,1... | collective-permute-start | bytes 3145736 | tf_op jit(solution)/shard_map/ppermute | solution.py:206
  14.2 38.2 %all-to-all-start.1 = ((bf16[16,32,1024]{2,1,0:T(8,128)(2,1)}), bf16[16,32,1024]{2,1,0:T(8,128)(2,1)S(1)}, u32[]{:S(2)}, u32[]{:S(2)}) async-start(bf16[16,32,1024]{2,1,0:T(8,128)(2,1)} %bitcast.3), calls=%async_computation.1 | async-start | bytes 2097152 | tf_op jit(solution)/shard_map/all_to_all | solution.py:197
  25.7 16.2 %collective-permute-start.6 = (bf16[512,1024]{1,0:T(8,128)(2,1)S(1)}, bf16[512,1024]{1,0:T(8,128)(2,1)S(1)}, u32[]{:S(2)}, u32[]{:S(2)}) collective-permute-start(bf16[512,1024]{1,0:T(8,128)(2,1)S(1)} %copy-done), channel_id=1, source_target_pairs={{0,32},{32,0},{1,33},{33,1},{2,34},{34,2},{3,35},{35,3},{4,36},{36... | collective-permute-start | bytes 3145736 | tf_op jit(solution)/shard_map/ppermute | solution.py:207
  30.0 14.3 %collective-permute-start.7 = (bf16[512,1024]{1,0:T(8,128)(2,1)S(1)}, bf16[512,1024]{1,0:T(8,128)(2,1)}, u32[]{:S(2)}, u32[]{:S(2)}) collective-permute-start(bf16[512,1024]{1,0:T(8,128)(2,1)S(1)} %collective-permute-done.5.pair_ref), channel_id=1, source_target_pairs={{0,32},{32,0},{1,33},{33,1},{2,34},{34,2},{3,35},{35,3},{4,36},{36... | collective-permute-start | bytes 3145736 | tf_op jit(solution)/shard_map/ppermute | solution.py:208
  41.9 1.0 copy-start.1
  52.4 1.2 %copy-start.2 = (bf16[512,1024]{1,0:T(8,128)(2,1)S(1)}, bf16[512,1024]{1,0:T(8,128)(2,1)}, u32[]{:S(2)}) copy-start(bf16[512,1024]{1,0:T(8,128)(2,1)} %copy-done.1) | copy-start | bytes 3145732
  58.1 34.0 %all-to-all-start.2 = ((f16[16,64,256]{2,1,0:T(8,128)(2,1)}), f16[16,64,256]{2,1,0:T(8,128)(2,1)S(1)}, u32[]{:S(2)}, u32[]{:S(2)}) async-start(f16[16,64,256]{2,1,0:T(8,128)(2,1)} %bitcast.5), calls=%async_computation.2 | async-start | bytes 1048576 | tf_op jit(solution)/shard_map/all_to_all | solution.py:230
  67.7 9.3 %collective-permute-start.2 = (bf16[1,8,128]{2,1,0:T(8,128)(2,1)S(1)}, bf16[1,8,128]{2,1,0:T(8,128)(2,1)S(1)}, u32[]{:S(2)}, u32[]{:S(2)}) collective-permute-start(bf16[1,8,128]{2,1,0:T(8,128)(2,1)S(1)} %get-tuple-element.9), channel_id=1, source_target_pairs={{0,192},{64,128},{128,64},{192,0},{256,448},{320,384},{384,320},{4... | collective-permute-start | bytes 6152 | tf_op jit(solution)/shard_map/ppermute | solution.py:202
  69.6 7.4 %collective-permute-start.1 = (bf16[1,8,128]{2,1,0:T(8,128)(2,1)S(1)}, bf16[1,8,128]{2,1,0:T(8,128)(2,1)S(1)}, u32[]{:S(2)}, u32[]{:S(2)}) collective-permute-start(bf16[1,8,128]{2,1,0:T(8,128)(2,1)S(1)} %get-tuple-element.9), channel_id=1, source_target_pairs={{0,128},{64,192},{128,0},{192,64},{256,384},{320,448},{384,256},{4... | collective-permute-start | bytes 6152 | tf_op jit(solution)/shard_map/ppermute | solution.py:202
  73.6 4.6 %collective-permute-start = (bf16[1,8,128]{2,1,0:T(8,128)(2,1)S(1)}, bf16[1,8,128]{2,1,0:T(8,128)(2,1)S(1)}, u32[]{:S(2)}, u32[]{:S(2)}) collective-permute-start(bf16[1,8,128]{2,1,0:T(8,128)(2,1)S(1)} %get-tuple-element.9), channel_id=1, source_target_pairs={{0,64},{64,0},{128,192},{192,128},{256,320},{320,256},{384,448},{4... | collective-permute-start | bytes 6152 | tf_op jit(solution)/shard_map/ppermute | solution.py:202
  78.3 8.4 %collective-permute-start.3 = (bf16[4,8,128]{2,1,0:T(8,128)(2,1)S(1)}, bf16[4,8,128]{2,1,0:T(8,128)(2,1)S(1)}, u32[]{:S(2)}, u32[]{:S(2)}) collective-permute-start(bf16[4,8,128]{2,1,0:T(8,128)(2,1)S(1)} %pad_maximum_fusion.1), channel_id=1, source_target_pairs={{0,256},{64,320},{128,384},{192,448},{256,0},{320,64},{384,128},{4... | collective-permute-start | bytes 24584 | tf_op jit(solution)/shard_map/ppermute | solution.py:204
  86.7 5.3 %collective-permute-start.4 = (bf16[8,8,128]{2,1,0:T(8,128)(2,1)S(1)}, bf16[8,8,128]{2,1,0:T(8,128)(2,1)S(1)}, u32[]{:S(2)}, u32[]{:S(2)}) collective-permute-start(bf16[8,8,128]{2,1,0:T(8,128)(2,1)S(1)} %constant_dynamic-update-slice_fusion), channel_id=1, source_target_pairs={{0,32},{32,0},{1,33},{33,1},{2,34},{34,2},{3,35},{35,3},{4,36},{36... | collective-permute-start | bytes 49160 | tf_op jit(solution)/shard_map/ppermute | solution.py:233
  92.6 12.9 %copy-start.3 = (bf16[1,2048,64]{1,2,0:T(8,128)(2,1)S(1)}, bf16[1,2048,64]{1,2,0:T(8,128)(2,1)}, u32[]{:S(2)}) copy-start(bf16[1,2048,64]{1,2,0:T(8,128)(2,1)} %param.7) | copy-start | bytes 786436

commit v9 on v8

--- a/solution.py
+++ b/solution.py
@@ -103,31 +103,36 @@
     out_ref[1 - own] = far + part(across_pair_ref, 1 - pair)
 
 
-def plan_kernel(info_ref, place_ref, route_ref):
-    rep, own, here = lax.axis_index("rep"), lax.axis_index("k"), lax.axis_index("z")
-
-    def of(r):
-        entries = [here ^ z for z in range(Z)]
-        at_core = [
-            jnp.concatenate([info_ref[s, e, r : r + 1, :].astype(f32) for e in entries], axis=0)
-            for s in range(2)
-        ]
-        first = jnp.where(own == 0, at_core[0], at_core[1])
-        second = jnp.where(own == 0, at_core[1], at_core[0])
-        return jnp.concatenate([first, second], axis=0)
-
-    active = of(0)
+def by_index(info_ref, r):
+    own, here = lax.axis_index("k"), lax.axis_index("z")
+    entries = [here ^ z for z in range(Z)]
+    at_core = [
+        jnp.concatenate([info_ref[s, e, r : r + 1, :].astype(f32) for e in entries], axis=0)
+        for s in range(2)
+    ]
+    first = jnp.where(own == 0, at_core[0], at_core[1])
+    second = jnp.where(own == 0, at_core[1], at_core[0])
+    return jnp.concatenate([first, second], axis=0)
+
+
+def place_kernel(info_ref, place_ref):
+    rep = lax.axis_index("rep")
+    active = by_index(info_ref, 0)
     rank = ranks(active)
     offset = jnp.zeros((2 * Z, T), i32)
     even = jnp.zeros((2 * Z, T), i32)
-    counts = [of(1 + l).astype(i32) for l in range(LAYERS)]
-    for l, n in enumerate(counts):
+    for l in range(LAYERS):
+        n = by_index(info_ref, 1 + l).astype(i32)
         offset += jnp.where(l < rep, n & 7, 0)
         even = jnp.where(l == rep, (n >> 3) << 3, even)
     cls = jnp.where(rank < even, rank, offset + rank - even) & 7
     place_ref[0] = jnp.where(active > 0, cls, -1)
     place_ref[1] = jnp.minimum(rank >> 3, BASE - 1)
 
+
+def plan_kernel(info_ref, route_ref):
+    rep = lax.axis_index("rep")
+    counts = [by_index(info_ref, 1 + l).astype(i32) for l in range(LAYERS)]
     lane = iota((1, T), 1)
     for k in range(2):
         spread = []
@@ -222,7 +227,7 @@
             pltpu.VMEM((512, KD), bf16),
             pltpu.SemaphoreType.DMA((2,)),
         ],
-        limit=48,
+        limit=49,
         flops=2**30,
     )
 
@@ -231,9 +236,9 @@
     sums = jnp.sum(parts.reshape(2, 4, 2, 64, Z * SHARE).astype(f32), axis=1)
 
     info_across = lax.ppermute(info, "k", swap)
-    place, route = call(
-        plan_kernel, [(2, 2 * Z, T), (16, T)], i32, jnp.stack([info, info_across]), flops=2**20
-    )
+    infos = jnp.stack([info, info_across])
+    route = call(plan_kernel, (16, T), i32, infos, flops=2**20)
+    place = call(place_kernel, (2, 2 * Z, T), i32, infos, flops=2**20)
     routed = call(route_kernel, (LAYERS, 2, 2, 64, T), f32, route, sums, flops=2**24)
     owned = lax.all_to_all(routed, "rep", 0, 0, tiled=True)
     out = call(final_kernel, (64, 2048), bf16, place, owned, residual_in[0].T, flops=2**26)

time: 109 us -> 109 us (level)
  blocking collectives: 12.8 us -> 0 us
  waiting for transfers between devices: 18.4 us -> 27.1 us
  starting transfers between devices: 63.2 us -> 67.6 us
  local copies, waits for them, and re-layouts: 2.23 us -> 1.04 us
    all_to_all x1 -> x0, blocking collectives: 12.8 us -> none  [step(): owned = lax.all_to_all(routed, 'rep', 0, 0, tiled=True)]
    all_to_all x0 -> x1, waiting for transfers between devices: none -> 8.81 us  [step(): owned = lax.all_to_all(routed, 'rep', 0, 0, tiled=True)]
    all_to_all x0 -> x1, starting transfers between devices: none -> 4.38 us  [step(): owned = lax.all_to_all(routed, 'rep', 0, 0, tiled=True)]
    unnamed x12 -> x10, local copies, waits for them, and re-layouts: 2.22 us -> 1.03 us
    pallas_call x6 -> x7, Pallas kernels: 9.54 us -> 10.6 us  [call(): pl.pallas_call(kernel, out_shape=[jax.ShapeDtypeStruct(one, dtype) for on...]
  transfers between devices with their start and end apart: 11 -> 12, of which waited for: 6 -> 7; matrix products, arithmetic and copies ran while one was open for 0% -> 0% of each run, Pallas kernels for 1% -> 1%
where the time goes in v9:
time: 109 us; the launch traced here: 108 us
  starting transfers between devices  67.6 us (62%)
  waiting for transfers between devices  27.1 us (25%)
  Pallas kernels  10.6 us (10%)
    ppermute x1, starting transfers between devices, step(): across_other = lax.ppermute(other, 'k', swap)  11.9 us
    all_to_all x1, starting transfers between devices, step(): lax.all_to_all(shared.reshape(2 * Z, SHARE, KD), ('b', 'z'), 0, 0, tiled=...  11.5 us
    pallas_call x7, Pallas kernels, call(): pl.pallas_call(kernel, out_shape=[jax.ShapeDtypeStruct(one, dtype) for on...  10.6 us
    all_to_all x1, starting transfers between devices, step(): parts = lax.all_to_all(sent, ('k', 'g', 'b'), 0, 0, tiled=True)  9.62 us
    ppermute x3, starting transfers between devices, step(): near.append(lax.ppermute(info, 'z', [(z, z ^ step) for z in range(Z)]))  9.26 us
    all_to_all x1, waiting for transfers between devices, step(): owned = lax.all_to_all(routed, 'rep', 0, 0, tiled=True)  8.81 us
    all_to_all x1, waiting for transfers between devices, step(): lax.all_to_all(shared.reshape(2 * Z, SHARE, KD), ('b', 'z'), 0, 0, tiled=...  8.06 us
    all_to_all x1, starting transfers between devices, step(): got = lax.all_to_all(packed, 'rep', 0, 0, tiled=True)  4.83 us
  transfers between devices with their start and end apart: 12, of which 7 were waited for; matrix products, arithmetic and copies ran while one was open for 0% of the time, Pallas kernels for 1%

profile of v9, /device:TPU:1, one launch (start us, length us, event | category | flops | bytes accessed | tf_op | source)
XLA Modules:
  0.0 107.6 jit_solution(17144015796641591823)
XLA Ops:
  0.0 2.2 %shard_map.46 = bf16[4,40,1024]{2,1,0:T(8,128)(2,1)} custom-call(s32[1,128]{1,0:T(1,128)} %labels_ref.1, bf16[128,1024]{1,0:T(8,128)(2,1)} %bitcast.17), custom_call_target="tpu_custom_call" | custom-call | flops 67108864 | bytes 2097152 | tf_op jit(solution)/shard_map/pallas_call | solution.py:183
  2.2 4.8 %all-to-all-start = ((bf16[4,40,1024]{2,1,0:T(8,128)(2,1)}), bf16[4,40,1024]{2,1,0:T(8,128)(2,1)S(1)}, u32[]{:S(2)}, u32[]{:S(2)}) async-start(bf16[4,40,1024]{2,1,0:T(8,128)(2,1)} %shard_map.46), calls=%async_computation | async-start | bytes 655360 | tf_op jit(solution)/shard_map/all_to_all | solution.py:200
  7.0 3.2 %collective-permute-start.5 = (bf16[512,1024]{1,0:T(8,128)(2,1)S(1)}, bf16[512,1024]{1,0:T(8,128)(2,1)S(1)}, u32[]{:S(2)}, u32[]{:S(2)}) collective-permute-start(bf16[512,1024]{1,0:T(8,128)(2,1)S(1)} %copy-done), channel_id=1, source_target_pairs={{0,4},{4,0},{1,5},{5,1},{2,6},{6,2},{3,7},{7,3},{8,12},{12,8},{9,1... | collective-permute-start | bytes 3145736 | tf_op jit(solution)/shard_map/ppermute | solution.py:211
  10.2 2.7 %all-to-all-done.got_ref = bf16[4,40,1024]{2,1,0:T(8,128)(2,1)S(1)} async-done(((bf16[4,40,1024]{2,1,0:T(8,128)(2,1)}), bf16[4,40,1024]{2,1,0:T(8,128)(2,1)S(1)}, u32[]{:S(2)}, u32[]{:S(2)}) %all-to-all-start) | async-done | bytes 327712 | tf_op jit(solution)/shard_map/all_to_all | solution.py:200
  12.9 1.3 %shard_map.47 = (bf16[2,8,32,1024]{3,2,1,0:T(8,128)(2,1)}, bf16[1,8,128]{2,1,0:T(8,128)(2,1)S(1)}) custom-call(bf16[4,40,1024]{2,1,0:T(8,128)(2,1)S(1)} %all-to-all-done.got_ref), custom_call_target="tpu_custom_call" | custom-call | flops 67108864 | bytes 2097152 | tf_op jit(solution)/shard_map/pallas_call | solution.py:183
  14.2 11.5 %all-to-all-start.1 = ((bf16[16,32,1024]{2,1,0:T(8,128)(2,1)}), bf16[16,32,1024]{2,1,0:T(8,128)(2,1)S(1)}, u32[]{:S(2)}, u32[]{:S(2)}) async-start(bf16[16,32,1024]{2,1,0:T(8,128)(2,1)} %bitcast.3), calls=%async_computation.1 | async-start | bytes 2097152 | tf_op jit(solution)/shard_map/all_to_all | solution.py:202
  25.7 4.3 %collective-permute-start.6 = (bf16[512,1024]{1,0:T(8,128)(2,1)S(1)}, bf16[512,1024]{1,0:T(8,128)(2,1)S(1)}, u32[]{:S(2)}, u32[]{:S(2)}) collective-permute-start(bf16[512,1024]{1,0:T(8,128)(2,1)S(1)} %copy-done), channel_id=1, source_target_pairs={{0,32},{32,0},{1,33},{33,1},{2,34},{34,2},{3,35},{35,3},{4,36},{36... | collective-permute-start | bytes 3145736 | tf_op jit(solution)/shard_map/ppermute | solution.py:212
  30.0 11.9 %collective-permute-start.7 = (bf16[512,1024]{1,0:T(8,128)(2,1)S(1)}, bf16[512,1024]{1,0:T(8,128)(2,1)}, u32[]{:S(2)}, u32[]{:S(2)}) collective-permute-start(bf16[512,1024]{1,0:T(8,128)(2,1)S(1)} %collective-permute-done.5.pair_ref), channel_id=1, source_target_pairs={{0,32},{32,0},{1,33},{33,1},{2,34},{34,2},{3,35},{35,3},{4,36},{36... | collective-permute-start | bytes 3145736 | tf_op jit(solution)/shard_map/ppermute | solution.py:213
  42.0 1.0 copy-done.2
  42.9 1.4 %collective-permute-done.7.across_pair_far = bf16[512,1024]{1,0:T(8,128)(2,1)} collective-permute-done((bf16[512,1024]{1,0:T(8,128)(2,1)S(1)}, bf16[512,1024]{1,0:T(8,128)(2,1)}, u32[]{:S(2)}, u32[]{:S(2)}) %collective-permute-start.7) | collective-permute-done | bytes 1048608 | tf_op jit(solution)/shard_map/ppermute | solution.py:213
  44.3 8.1 %all-to-all-done.1 = bf16[16,32,1024]{2,1,0:T(8,128)(2,1)S(1)} async-done(((bf16[16,32,1024]{2,1,0:T(8,128)(2,1)}), bf16[16,32,1024]{2,1,0:T(8,128)(2,1)S(1)}, u32[]{:S(2)}, u32[]{:S(2)}) %all-to-all-start.1) | async-done | bytes 1048608 | tf_op jit(solution)/shard_map/all_to_all | solution.py:202
  52.4 3.8 %shard_map.50 = f32[2,512,256]{2,1,0:T(8,128)S(1)} custom-call(bf16[512,1024]{1,0:T(8,128)(2,1)S(1)} %copy-done, bf16[512,1024]{1,0:T(8,128)(2,1)S(1)} %collective-permute-done.5.pair_ref, bf16[2,256,1024]{2,1,0:T(8,128)(2,1)S(1)} %bitcast.14, bf16[512,1024]{1,0:T(8,128)(2,1)} %copy-done.2, bf16[512,1024]{1,0:T(8,128)(2,1)} %collective-permute-done.7.across_pair_far), custom_call_target="tpu_custom_call" | custom-call | flops 1073741824 | bytes 2097152 | tf_op jit(solution)/shard_map/pallas_call | solution.py:183
  57.1 9.6 %all-to-all-start.2 = ((f16[16,64,256]{2,1,0:T(8,128)(2,1)}), f16[16,64,256]{2,1,0:T(8,128)(2,1)S(1)}, u32[]{:S(2)}, u32[]{:S(2)}) async-start(f16[16,64,256]{2,1,0:T(8,128)(2,1)} %bitcast.5), calls=%async_computation.2 | async-start | bytes 1048576 | tf_op jit(solution)/shard_map/all_to_all | solution.py:235
  66.7 1.9 %collective-permute-start.2 = (bf16[1,8,128]{2,1,0:T(8,128)(2,1)S(1)}, bf16[1,8,128]{2,1,0:T(8,128)(2,1)S(1)}, u32[]{:S(2)}, u32[]{:S(2)}) collective-permute-start(bf16[1,8,128]{2,1,0:T(8,128)(2,1)S(1)} %get-tuple-element.7), channel_id=1, source_target_pairs={{0,192},{64,128},{128,64},{192,0},{256,448},{320,384},{384,320},{4... | collective-permute-start | bytes 6152 | tf_op jit(solution)/shard_map/ppermute | solution.py:207
  68.7 4.0 %collective-permute-start.1 = (bf16[1,8,128]{2,1,0:T(8,128)(2,1)S(1)}, bf16[1,8,128]{2,1,0:T(8,128)(2,1)S(1)}, u32[]{:S(2)}, u32[]{:S(2)}) collective-permute-start(bf16[1,8,128]{2,1,0:T(8,128)(2,1)S(1)} %get-tuple-element.7), channel_id=1, source_target_pairs={{0,128},{64,192},{128,0},{192,64},{256,384},{320,448},{384,256},{4... | collective-permute-start | bytes 6152 | tf_op jit(solution)/shard_map/ppermute | solution.py:207
  72.6 3.4 %collective-permute-start = (bf16[1,8,128]{2,1,0:T(8,128)(2,1)S(1)}, bf16[1,8,128]{2,1,0:T(8,128)(2,1)S(1)}, u32[]{:S(2)}, u32[]{:S(2)}) collective-permute-start(bf16[1,8,128]{2,1,0:T(8,128)(2,1)S(1)} %get-tuple-element.7), channel_id=1, source_target_pairs={{0,64},{64,0},{128,192},{192,128},{256,320},{320,256},{384,448},{4... | collective-permute-start | bytes 6152 | tf_op jit(solution)/shard_map/ppermute | solution.py:207
  76.1 1.2 %collective-permute-done = bf16[1,8,128]{2,1,0:T(8,128)(2,1)S(1)} collective-permute-done((bf16[1,8,128]{2,1,0:T(8,128)(2,1)S(1)}, bf16[1,8,128]{2,1,0:T(8,128)(2,1)S(1)}, u32[]{:S(2)}, u32[]{:S(2)}) %collective-permute-start) | collective-permute-done | bytes 2080 | tf_op jit(solution)/shard_map/ppermute | solution.py:207
  77.3 4.2 %collective-permute-start.3 = (bf16[4,8,128]{2,1,0:T(8,128)(2,1)S(1)}, bf16[4,8,128]{2,1,0:T(8,128)(2,1)S(1)}, u32[]{:S(2)}, u32[]{:S(2)}) collective-permute-start(bf16[4,8,128]{2,1,0:T(8,128)(2,1)S(1)} %pad_maximum_fusion.1), channel_id=1, source_target_pairs={{0,256},{64,320},{128,384},{192,448},{256,0},{320,64},{384,128},{4... | collective-permute-start | bytes 24584 | tf_op jit(solution)/shard_map/ppermute | solution.py:209
  81.5 4.2 %collective-permute-done.3 = bf16[4,8,128]{2,1,0:T(8,128)(2,1)S(1)} collective-permute-done((bf16[4,8,128]{2,1,0:T(8,128)(2,1)S(1)}, bf16[4,8,128]{2,1,0:T(8,128)(2,1)S(1)}, u32[]{:S(2)}, u32[]{:S(2)}) %collective-permute-start.3) | collective-permute-done | bytes 8224 | tf_op jit(solution)/shard_map/ppermute | solution.py:209
  85.7 4.5 %collective-permute-start.4 = (bf16[8,8,128]{2,1,0:T(8,128)(2,1)S(1)}, bf16[8,8,128]{2,1,0:T(8,128)(2,1)S(1)}, u32[]{:S(2)}, u32[]{:S(2)}) collective-permute-start(bf16[8,8,128]{2,1,0:T(8,128)(2,1)S(1)} %constant_dynamic-update-slice_fusion), channel_id=1, source_target_pairs={{0,32},{32,0},{1,33},{33,1},{2,34},{34,2},{3,35},{35,3},{4,36},{36... | collective-permute-start | bytes 49160 | tf_op jit(solution)/shard_map/ppermute | solution.py:238
  91.1 1.2 %shard_map.51 = f32[4,2,2,64,128]{4,3,2,1,0:T(8,128)} custom-call(s32[16,128]{1,0:T(8,128)S(1)} %shard_map.49.route_ref, f32[2,2,64,256]{3,2,1,0:T(8,128)S(1)} %convert_reduce_fusion.sums_ref), custom_call_target="tpu_custom_call" | custom-call | flops 16777216 | bytes 2097152 | tf_op jit(solution)/shard_map/pallas_call | solution.py:183
  92.3 4.4 %all-to-all-start.3 = ((f32[4,2,2,64,128]{4,3,2,1,0:T(8,128)}), f32[4,2,2,64,128]{4,3,2,1,0:T(8,128)S(1)}, u32[]{:S(2)}, u32[]{:S(2)}) async-start(f32[4,2,2,64,128]{4,3,2,1,0:T(8,128)} %shard_map.51), calls=%async_computation.3 | async-start | bytes 1048576 | tf_op jit(solution)/shard_map/all_to_all | solution.py:243
  96.8 8.8 %all-to-all-done.3.sums_ref = f32[4,2,2,64,128]{4,3,2,1,0:T(8,128)S(1)} async-done(((f32[4,2,2,64,128]{4,3,2,1,0:T(8,128)}), f32[4,2,2,64,128]{4,3,2,1,0:T(8,128)S(1)}, u32[]{:S(2)}, u32[]{:S(2)}) %all-to-all-start.3) | async-done | bytes 524320 | tf_op jit(solution)/shard_map/all_to_all | solution.py:243
  105.6 1.9 %shard_map.52 = bf16[64,2048]{1,0:T(8,128)(2,1)} custom-call(s32[2,16,128]{2,1,0:T(8,128)S(1)} %shard_map.48.place_ref, f32[4,2,2,64,128]{4,3,2,1,0:T(8,128)S(1)} %all-to-all-done.3.sums_ref, bf16[64,2048]{1,0:T(8,128)(2,1)S(1)} %bitcast.15), custom_call_target="tpu_custom_call" | custom-call | flops 67108864 | bytes 2097152 | tf_op jit(solution)/shard_map/pallas_call | solution.py:183
  (22 shorter events, 2.0 us)
Async XLA Ops:
  0.0 7.0 %copy-start = (bf16[512,1024]{1,0:T(8,128)(2,1)S(1)}, bf16[512,1024]{1,0:T(8,128)(2,1)}, u32[]{:S(2)}) copy-start(bf16[512,1024]{1,0:T(8,128)(2,1)} %own_ref.1) | copy-start | bytes 3145732
  2.2 10.7 %all-to-all-start = ((bf16[4,40,1024]{2,1,0:T(8,128)(2,1)}), bf16[4,40,1024]{2,1,0:T(8,128)(2,1)S(1)}, u32[]{:S(2)}, u32[]{:S(2)}) async-start(bf16[4,40,1024]{2,1,0:T(8,128)(2,1)} %shard_map.46), calls=%async_computation | async-start | bytes 655360 | tf_op jit(solution)/shard_map/all_to_all | solution.py:200
  7.0 23.0 %collective-permute-start.5 = (bf16[512,1024]{1,0:T(8,128)(2,1)S(1)}, bf16[512,1024]{1,0:T(8,128)(2,1)S(1)}, u32[]{:S(2)}, u32[]{:S(2)}) collective-permute-start(bf16[512,1024]{1,0:T(8,128)(2,1)S(1)} %copy-done), channel_id=1, source_target_pairs={{0,4},{4,0},{1,5},{5,1},{2,6},{6,2},{3,7},{7,3},{8,12},{12,8},{9,1... | collective-permute-start | bytes 3145736 | tf_op jit(solution)/shard_map/ppermute | solution.py:211
  14.2 38.2 %all-to-all-start.1 = ((bf16[16,32,1024]{2,1,0:T(8,128)(2,1)}), bf16[16,32,1024]{2,1,0:T(8,128)(2,1)S(1)}, u32[]{:S(2)}, u32[]{:S(2)}) async-start(bf16[16,32,1024]{2,1,0:T(8,128)(2,1)} %bitcast.3), calls=%async_computation.1 | async-start | bytes 2097152 | tf_op jit(solution)/shard_map/all_to_all | solution.py:202
  25.7 16.2 %collective-permute-start.6 = (bf16[512,1024]{1,0:T(8,128)(2,1)S(1)}, bf16[512,1024]{1,0:T(8,128)(2,1)S(1)}, u32[]{:S(2)}, u32[]{:S(2)}) collective-permute-start(bf16[512,1024]{1,0:T(8,128)(2,1)S(1)} %copy-done), channel_id=1, source_target_pairs={{0,32},{32,0},{1,33},{33,1},{2,34},{34,2},{3,35},{35,3},{4,36},{36... | collective-permute-start | bytes 3145736 | tf_op jit(solution)/shard_map/ppermute | solution.py:212
  30.0 14.3 %collective-permute-start.7 = (bf16[512,1024]{1,0:T(8,128)(2,1)S(1)}, bf16[512,1024]{1,0:T(8,128)(2,1)}, u32[]{:S(2)}, u32[]{:S(2)}) collective-permute-start(bf16[512,1024]{1,0:T(8,128)(2,1)S(1)} %collective-permute-done.5.pair_ref), channel_id=1, source_target_pairs={{0,32},{32,0},{1,33},{33,1},{2,34},{34,2},{3,35},{35,3},{4,36},{36... | collective-permute-start | bytes 3145736 | tf_op jit(solution)/shard_map/ppermute | solution.py:213
  41.9 1.0 copy-start.2
  57.1 33.9 %all-to-all-start.2 = ((f16[16,64,256]{2,1,0:T(8,128)(2,1)}), f16[16,64,256]{2,1,0:T(8,128)(2,1)S(1)}, u32[]{:S(2)}, u32[]{:S(2)}) async-start(f16[16,64,256]{2,1,0:T(8,128)(2,1)} %bitcast.5), calls=%async_computation.2 | async-start | bytes 1048576 | tf_op jit(solution)/shard_map/all_to_all | solution.py:235
  66.7 9.3 %collective-permute-start.2 = (bf16[1,8,128]{2,1,0:T(8,128)(2,1)S(1)}, bf16[1,8,128]{2,1,0:T(8,128)(2,1)S(1)}, u32[]{:S(2)}, u32[]{:S(2)}) collective-permute-start(bf16[1,8,128]{2,1,0:T(8,128)(2,1)S(1)} %get-tuple-element.7), channel_id=1, source_target_pairs={{0,192},{64,128},{128,64},{192,0},{256,448},{320,384},{384,320},{4... | collective-permute-start | bytes 6152 | tf_op jit(solution)/shard_map/ppermute | solution.py:207
  68.7 7.4 %collective-permute-start.1 = (bf16[1,8,128]{2,1,0:T(8,128)(2,1)S(1)}, bf16[1,8,128]{2,1,0:T(8,128)(2,1)S(1)}, u32[]{:S(2)}, u32[]{:S(2)}) collective-permute-start(bf16[1,8,128]{2,1,0:T(8,128)(2,1)S(1)} %get-tuple-element.7), channel_id=1, source_target_pairs={{0,128},{64,192},{128,0},{192,64},{256,384},{320,448},{384,256},{4... | collective-permute-start | bytes 6152 | tf_op jit(solution)/shard_map/ppermute | solution.py:207
  72.6 4.7 %collective-permute-start = (bf16[1,8,128]{2,1,0:T(8,128)(2,1)S(1)}, bf16[1,8,128]{2,1,0:T(8,128)(2,1)S(1)}, u32[]{:S(2)}, u32[]{:S(2)}) collective-permute-start(bf16[1,8,128]{2,1,0:T(8,128)(2,1)S(1)} %get-tuple-element.7), channel_id=1, source_target_pairs={{0,64},{64,0},{128,192},{192,128},{256,320},{320,256},{384,448},{4... | collective-permute-start | bytes 6152 | tf_op jit(solution)/shard_map/ppermute | solution.py:207
  77.3 8.4 %collective-permute-start.3 = (bf16[4,8,128]{2,1,0:T(8,128)(2,1)S(1)}, bf16[4,8,128]{2,1,0:T(8,128)(2,1)S(1)}, u32[]{:S(2)}, u32[]{:S(2)}) collective-permute-start(bf16[4,8,128]{2,1,0:T(8,128)(2,1)S(1)} %pad_maximum_fusion.1), channel_id=1, source_target_pairs={{0,256},{64,320},{128,384},{192,448},{256,0},{320,64},{384,128},{4... | collective-permute-start | bytes 24584 | tf_op jit(solution)/shard_map/ppermute | solution.py:209
  85.7 5.3 %collective-permute-start.4 = (bf16[8,8,128]{2,1,0:T(8,128)(2,1)S(1)}, bf16[8,8,128]{2,1,0:T(8,128)(2,1)S(1)}, u32[]{:S(2)}, u32[]{:S(2)}) collective-permute-start(bf16[8,8,128]{2,1,0:T(8,128)(2,1)S(1)} %constant_dynamic-update-slice_fusion), channel_id=1, source_target_pairs={{0,32},{32,0},{1,33},{33,1},{2,34},{34,2},{3,35},{35,3},{4,36},{36... | collective-permute-start | bytes 49160 | tf_op jit(solution)/shard_map/ppermute | solution.py:238
  92.3 13.3 %copy-start.1 = (bf16[1,2048,64]{1,2,0:T(8,128)(2,1)S(1)}, bf16[1,2048,64]{1,2,0:T(8,128)(2,1)}, u32[]{:S(2)}) copy-start(bf16[1,2048,64]{1,2,0:T(8,128)(2,1)} %param.7) | copy-start | bytes 786436
  92.3 13.3 %all-to-all-start.3 = ((f32[4,2,2,64,128]{4,3,2,1,0:T(8,128)}), f32[4,2,2,64,128]{4,3,2,1,0:T(8,128)S(1)}, u32[]{:S(2)}, u32[]{:S(2)}) async-start(f32[4,2,2,64,128]{4,3,2,1,0:T(8,128)} %shard_map.51), calls=%async_computation.3 | async-start | bytes 1048576 | tf_op jit(solution)/shard_map/all_to_all | solution.py:243
